TPU v7x, 32 devices: a whole 2x2x4 slice. The times are simulated.
32 devices in a mesh: wide: 16 (over z, x, core), narrow: 2 (over y).
Axes of the slice: x: 2, y: 2, z: 4, core: 2. Of those that a mesh axis runs over, the one named last changes fastest.
Arguments:
- tokens: bfloat16 [32, 256, 1152], P('wide', 'narrow'), may hold values from -6 to 6
- cond: bfloat16 [32, 1152], P('wide'), may hold values from -6 to 6
- timesteps: int32 [32], P('wide'), may hold values from 0 to 999
- counts: int32 [16], P('wide'), may hold values from 1 to 2, as said below
- w_ada: bfloat16 [1152, 6912], P('wide'), may hold values from -0.1875 to 0.1875
- b_ada: bfloat16 [6912], P('wide'), may hold values from -2 to 2
- w_qkv: bfloat16 [1152, 3456], P('wide'), may hold values from -0.1875 to 0.1875
- b_qv: bfloat16 [2304], P('wide'), may hold values from -2 to 2
- w_proj: bfloat16 [1152, 1152], P('wide'), may hold values from -1.5 to 1.5
- b_proj: bfloat16 [1152], P('wide'), may hold values from -2 to 2
- w_fc1: bfloat16 [1152, 4608], P('wide'), may hold values from -0.1875 to 0.1875
- b_fc1: bfloat16 [4608], P('wide'), may hold values from -2 to 2
- w_fc2: bfloat16 [4608, 1152], P('wide'), may hold values from -0.09375 to 0.09375
- b_fc2: bfloat16 [1152], P('wide'), may hold values from -2 to 2
- cotangent: bfloat16 [32, 256, 1152], P('wide', 'narrow'), may hold values from -6 to 6
Outputs:
- out: bfloat16 [32, 256, 1152], P('wide', 'narrow')
- grad_tokens: float32 [32, 256, 1152], P('wide', 'narrow')
- grad_cond: float32 [32, 1152], P('wide')
- grad_w_ada: float32 [1152, 6912], P('wide')
- grad_b_ada: float32 [6912], P('wide')
- grad_w_qkv: float32 [1152, 3456], P('wide')
- grad_b_qv: float32 [2304], P('wide')
- grad_w_proj: float32 [1152, 1152], P('wide')
- grad_b_proj: float32 [1152], P('wide')
- grad_w_fc1: float32 [1152, 4608], P('wide')
- grad_b_fc1: float32 [4608], P('wide')
- grad_w_fc2: float32 [4608, 1152], P('wide')
- grad_b_fc2: float32 [1152], P('wide')
Inputs may be any that keep to these rules, and one draw needn't show every extreme that they name: Image slot s of index w of wide is occupied when s < counts[w]; empty slots have zero output and add nothing to any gradient. In every draw some index of wide has all 2 slots occupied and some index has only one.
All inputs are finite; a program needn't handle non-finite values.
Results may differ from a plain program's by a relative error of at most 0.018.
The roundings to bfloat16 on the way count: a program that leaves them out, or rounds other values in their place, can miss the bound.
Values may be sent and summed in bfloat16 or wider, within the bound.
A program may use at most 256 MiB of HBM per device.

v0:
```python
import math

import jax
import jax.numpy as jnp
from jax import lax
from jax.sharding import PartitionSpec as P

HEADS = 16
HEAD_DIM = 72


eps_norm = 1e-06


def norm_rows(value):
    center = value - jnp.mean(value, axis=-1, keepdims=True)
    inv_std = lax.rsqrt(jnp.mean(center * center, axis=-1, keepdims=True) + eps_norm)
    return (center * inv_std, inv_std)


def norm_back(grad, normed, inv_std):
    return inv_std * (
        grad
        - jnp.mean(grad, axis=-1, keepdims=True)
        - normed * jnp.mean(grad * normed, axis=-1, keepdims=True)
    )


def gelu_tanh(value):
    return (
        0.5
        * value
        * (1.0 + jnp.tanh(0.7978845608028654 * (value + 0.044715 * value * value * value)))
    )


def time_features(steps, width):
    half_width = width // 2
    freqs = jnp.exp(-math.log(10000.0) * jnp.arange(half_width).astype(jnp.float32) / half_width)
    angles = steps.astype(jnp.float32)[:, None] * freqs[None, :]
    return jnp.concatenate([jnp.cos(angles), jnp.sin(angles)], axis=-1)


def apply_right(left, weight):
    return jnp.einsum("csk,kn->csn", left, weight, preferred_element_type=jnp.float32)


def apply_back(grad, weight):
    return jnp.einsum("csn,kn->csk", grad, weight, preferred_element_type=jnp.float32)


def outer_sum(left, right):
    return jnp.einsum("csk,csn->kn", left, right, preferred_element_type=jnp.float32)


def token_sum(value):
    return jnp.sum(value.astype(jnp.float32), axis=(0, 1))


def on_device(
    tokens,
    cond,
    timesteps,
    counts,
    w_ada,
    b_ada,
    w_qkv,
    b_qv,
    w_proj,
    b_proj,
    w_fc1,
    b_fc1,
    w_fc2,
    b_fc2,
    cotangent,
):
    slots, half_len, width = tokens.shape
    head_scale = 1.0 / math.sqrt(HEAD_DIM)
    gathered = (
        lax.all_gather(w_ada, "wide", axis=0, tiled=True),
        lax.all_gather(b_ada, "wide", axis=0, tiled=True),
        lax.all_gather(w_qkv, "wide", axis=0, tiled=True),
        lax.all_gather(b_qv, "wide", axis=0, tiled=True),
        lax.all_gather(w_proj, "wide", axis=0, tiled=True),
        lax.all_gather(b_proj, "wide", axis=0, tiled=True),
        lax.all_gather(w_fc1, "wide", axis=0, tiled=True),
        lax.all_gather(b_fc1, "wide", axis=0, tiled=True),
        lax.all_gather(w_fc2, "wide", axis=0, tiled=True),
        lax.all_gather(b_fc2, "wide", axis=0, tiled=True),
    )
    (
        ada_full,
        ada_bias,
        qkv_full,
        qv_bias,
        proj_full,
        proj_bias,
        fc1_full,
        fc1_bias,
        fc2_full,
        fc2_bias,
    ) = gathered
    live_slot = (jnp.arange(slots, dtype=jnp.int32) < counts[0]).astype(jnp.float32)[:, None, None]
    tok_float = tokens.astype(jnp.float32)
    cond_vec = cond.astype(jnp.float32) + time_features(timesteps, width)
    cond_sig = jax.nn.sigmoid(cond_vec)
    silu_low = (cond_vec * cond_sig).astype(jnp.bfloat16)
    modulate = jnp.dot(silu_low, ada_full, preferred_element_type=jnp.float32) + ada_bias.astype(
        jnp.float32
    )
    shift_one, scale_one, gate_one, shift_two, scale_two, gate_two = [
        modulate[:, None, i * width : (i + 1) * width] for i in range(6)
    ]
    normed_one, inv_one = norm_rows(tok_float)
    a_in = (normed_one * (1.0 + scale_one) + shift_one).astype(jnp.bfloat16)
    qkv = apply_right(a_in, qkv_full)
    bias_qv = qv_bias.astype(jnp.float32)
    query = (qkv[..., :width] + bias_qv[:width]).astype(jnp.bfloat16)
    keys = qkv[..., width : 2 * width].astype(jnp.bfloat16)
    values = (qkv[..., 2 * width :] + bias_qv[width:]).astype(jnp.bfloat16)
    keys_all, values_all = (
        lax.all_gather(keys, "narrow", axis=1, tiled=True),
        lax.all_gather(values, "narrow", axis=1, tiled=True),
    )
    query_heads = query.reshape(slots, half_len, HEADS, HEAD_DIM)
    key_heads = keys_all.reshape(slots, -1, HEADS, HEAD_DIM)
    value_heads = values_all.reshape(slots, -1, HEADS, HEAD_DIM)
    scores = (
        jnp.einsum("cqhe,ckhe->chqk", query_heads, key_heads, preferred_element_type=jnp.float32)
        * head_scale
    )
    log_total = jax.nn.logsumexp(scores, axis=-1, keepdims=True)
    probs = jnp.exp(scores - log_total)
    probs_low = probs.astype(jnp.bfloat16)
    attended = jnp.einsum(
        "chqk,ckhe->cqhe", probs_low, value_heads, preferred_element_type=jnp.float32
    )
    attended = attended.reshape(slots, half_len, width).astype(jnp.bfloat16)
    attn_out = apply_right(attended, proj_full) + proj_bias.astype(jnp.float32)
    mid = tok_float + gate_one * attn_out
    normed_two, inv_two = norm_rows(mid)
    m_in = (normed_two * (1.0 + scale_two) + shift_two).astype(jnp.bfloat16)
    hidden = apply_right(m_in, fc1_full) + fc1_bias.astype(jnp.float32)
    act_low = gelu_tanh(hidden).astype(jnp.bfloat16)
    mlp_out = apply_right(act_low, fc2_full) + fc2_bias.astype(jnp.float32)
    out = (live_slot * (mid + gate_two * mlp_out)).astype(jnp.bfloat16)
    weights_back = (
        lax.all_gather(w_ada, "wide", axis=0, tiled=True),
        lax.all_gather(b_ada, "wide", axis=0, tiled=True),
        lax.all_gather(w_qkv, "wide", axis=0, tiled=True),
        lax.all_gather(b_qv, "wide", axis=0, tiled=True),
        lax.all_gather(w_proj, "wide", axis=0, tiled=True),
        lax.all_gather(b_proj, "wide", axis=0, tiled=True),
        lax.all_gather(w_fc1, "wide", axis=0, tiled=True),
        lax.all_gather(b_fc1, "wide", axis=0, tiled=True),
        lax.all_gather(w_fc2, "wide", axis=0, tiled=True),
        lax.all_gather(b_fc2, "wide", axis=0, tiled=True),
    )
    ada_back = weights_back[0]
    qkv_back = weights_back[2]
    proj_back = weights_back[4]
    fc1_back = weights_back[6]
    fc2_back = weights_back[8]
    grad_out = live_slot * cotangent.astype(jnp.float32)
    d_mlp = (gate_two * grad_out).astype(jnp.bfloat16)
    d_gate_two = jnp.sum(grad_out * mlp_out, axis=1)
    fc2_bias_sum = token_sum(d_mlp)
    d_act = apply_back(d_mlp, fc2_back)
    unused, gelu_pull = jax.vjp(gelu_tanh, hidden)
    d_hidden = gelu_pull(d_act)[0].astype(jnp.bfloat16)
    fc1_bias_sum = token_sum(d_hidden)
    d_m_in = apply_back(d_hidden, fc1_back)
    d_scale_two = jnp.sum(d_m_in * normed_two, axis=1)
    d_shift_two = jnp.sum(d_m_in, axis=1)
    d_mid = grad_out + norm_back(d_m_in * (1.0 + scale_two), normed_two, inv_two)
    d_attn = (gate_one * d_mid).astype(jnp.bfloat16)
    d_gate_one = jnp.sum(d_mid * attn_out, axis=1)
    proj_bias_sum = token_sum(d_attn)
    d_att = (
        apply_back(d_attn, proj_back).astype(jnp.bfloat16).reshape(slots, half_len, HEADS, HEAD_DIM)
    )
    d_probs = jnp.einsum("cqhe,ckhe->chqk", d_att, value_heads, preferred_element_type=jnp.float32)
    d_scores = (probs * (d_probs - jnp.sum(probs * d_probs, axis=-1, keepdims=True))).astype(
        jnp.bfloat16
    )
    d_query = (
        jnp.einsum("chqk,ckhe->cqhe", d_scores, key_heads, preferred_element_type=jnp.float32)
        * head_scale
    )
    d_query = d_query.reshape(slots, half_len, width).astype(jnp.bfloat16)
    d_keys_all = (
        jnp.einsum("chqk,cqhe->ckhe", d_scores, query_heads, preferred_element_type=jnp.float32)
        * head_scale
    )
    d_values_all = jnp.einsum(
        "chqk,cqhe->ckhe", probs_low, d_att, preferred_element_type=jnp.float32
    )
    d_keys_all = d_keys_all.reshape(slots, -1, width)
    d_values_all = d_values_all.reshape(slots, -1, width)
    d_keys, d_values = (
        lax.psum_scatter(
            d_keys_all.astype(jnp.bfloat16), "narrow", scatter_dimension=1, tiled=True
        ).astype(jnp.float32),
        lax.psum_scatter(
            d_values_all.astype(jnp.bfloat16), "narrow", scatter_dimension=1, tiled=True
        ).astype(jnp.float32),
    )
    d_values_low = d_values.astype(jnp.bfloat16)
    d_qkv = jnp.concatenate([d_query, d_keys.astype(jnp.bfloat16), d_values_low], axis=-1)
    qv_bias_sum = jnp.concatenate([token_sum(d_query), token_sum(d_values_low)], axis=0)
    d_a_in = apply_back(d_qkv, qkv_back)
    d_scale_one = jnp.sum(d_a_in * normed_one, axis=1)
    d_shift_one = jnp.sum(d_a_in, axis=1)
    grad_tokens = d_mid + norm_back(d_a_in * (1.0 + scale_one), normed_one, inv_one)
    d_modulate = jnp.concatenate(
        [d_shift_one, d_scale_one, d_gate_one, d_shift_two, d_scale_two, d_gate_two], axis=-1
    )
    summed = (
        lax.psum(d_modulate.astype(jnp.bfloat16), "narrow").astype(jnp.float32),
        lax.psum(qv_bias_sum.astype(jnp.bfloat16), "narrow").astype(jnp.float32),
        lax.psum(proj_bias_sum.astype(jnp.bfloat16), "narrow").astype(jnp.float32),
        lax.psum(fc1_bias_sum.astype(jnp.bfloat16), "narrow").astype(jnp.float32),
        lax.psum(fc2_bias_sum.astype(jnp.bfloat16), "narrow").astype(jnp.float32),
    )
    d_mod_low = summed[0].astype(jnp.bfloat16)
    grad_ada_bias = jnp.sum(d_mod_low.astype(jnp.float32), axis=0)
    d_silu = jnp.einsum("cn,kn->ck", d_mod_low, ada_back, preferred_element_type=jnp.float32)
    grad_cond = d_silu * (cond_sig + cond_vec * cond_sig * (1.0 - cond_sig))
    pair_count = lax.axis_size("narrow")
    ada_cols = d_mod_low.shape[1] // pair_count
    mod_piece = lax.dynamic_slice_in_dim(
        d_mod_low, lax.axis_index("narrow") * ada_cols, ada_cols, 1
    )
    grad_ada_part = jnp.einsum("ck,cn->kn", silu_low, mod_piece, preferred_element_type=jnp.float32)
    lefts = (
        lax.all_gather(a_in, "narrow", axis=1, tiled=True),
        lax.all_gather(attended, "narrow", axis=1, tiled=True),
        lax.all_gather(m_in, "narrow", axis=1, tiled=True),
        lax.all_gather(act_low, "narrow", axis=1, tiled=True),
    )
    rights = (
        lax.all_to_all(d_qkv, "narrow", split_axis=2, concat_axis=1, tiled=True),
        lax.all_to_all(d_attn, "narrow", split_axis=2, concat_axis=1, tiled=True),
        lax.all_to_all(d_hidden, "narrow", split_axis=2, concat_axis=1, tiled=True),
        lax.all_to_all(d_mlp, "narrow", split_axis=2, concat_axis=1, tiled=True),
    )
    grad_qkv_part = outer_sum(lefts[0], rights[0])
    grad_proj_part = outer_sum(lefts[1], rights[1])
    grad_fc1_part = outer_sum(lefts[2], rights[2])
    grad_fc2_part = outer_sum(lefts[3], rights[3])
    shards = (
        lax.psum_scatter(grad_ada_part, "wide", scatter_dimension=0, tiled=True),
        lax.psum_scatter(grad_ada_bias, "wide", scatter_dimension=0, tiled=True),
        lax.psum_scatter(grad_qkv_part, "wide", scatter_dimension=0, tiled=True),
        lax.psum_scatter(summed[1], "wide", scatter_dimension=0, tiled=True),
        lax.psum_scatter(grad_proj_part, "wide", scatter_dimension=0, tiled=True),
        lax.psum_scatter(summed[2], "wide", scatter_dimension=0, tiled=True),
        lax.psum_scatter(grad_fc1_part, "wide", scatter_dimension=0, tiled=True),
        lax.psum_scatter(summed[3], "wide", scatter_dimension=0, tiled=True),
        lax.psum_scatter(grad_fc2_part, "wide", scatter_dimension=0, tiled=True),
        lax.psum_scatter(summed[4], "wide", scatter_dimension=0, tiled=True),
    )
    joined = (
        lax.all_gather(shards[0].astype(jnp.bfloat16), "narrow", axis=1, tiled=True).astype(
            jnp.float32
        ),
        lax.all_gather(shards[2].astype(jnp.bfloat16), "narrow", axis=1, tiled=True).astype(
            jnp.float32
        ),
        lax.all_gather(shards[4].astype(jnp.bfloat16), "narrow", axis=1, tiled=True).astype(
            jnp.float32
        ),
        lax.all_gather(shards[6].astype(jnp.bfloat16), "narrow", axis=1, tiled=True).astype(
            jnp.float32
        ),
        lax.all_gather(shards[8].astype(jnp.bfloat16), "narrow", axis=1, tiled=True).astype(
            jnp.float32
        ),
    )
    return (
        out,
        grad_tokens,
        grad_cond,
        joined[0],
        shards[1],
        joined[1],
        shards[3],
        joined[2],
        shards[5],
        joined[3],
        shards[7],
        joined[4],
        shards[9],
    )


def solution(mesh):
    in_specs = (
        P("wide", "narrow", None),
        P("wide", None),
        P("wide"),
        P("wide"),
        P("wide", None),
        P("wide"),
        P("wide", None),
        P("wide"),
        P("wide", None),
        P("wide"),
        P("wide", None),
        P("wide"),
        P("wide", None),
        P("wide"),
        P("wide", "narrow", None),
    )
    out_specs = (
        P("wide", "narrow", None),
        P("wide", "narrow", None),
        P("wide", None),
        P("wide", None),
        P("wide"),
        P("wide", None),
        P("wide"),
        P("wide", None),
        P("wide"),
        P("wide", None),
        P("wide"),
        P("wide", None),
        P("wide"),
    )
    return jax.shard_map(
        on_device, mesh=mesh, in_specs=in_specs, out_specs=out_specs, check_vma=False
    )
```

profile of v0, /device:TPU:0, one launch (start us, length us, event | category | flops | bytes accessed | tf_op | source)
XLA Modules:
  0.0 1349.9 jit_solution(15534898792074992465)
XLA Ops:
  8.7 1.3 fusion.68
  17.0 65.5 %all-reduce.13 = (bf16[6912]{0:T(1024)(128)(2,1)S(1)}, bf16[2304]{0:T(1024)(128)(2,1)S(1)}, bf16[1152]{0:T(1024)(128)(2,1)S(1)}, bf16[4608]{0:T(1024)(128)(2,1)S(1)}, bf16[1152]{0:T(1024)(128)(2,1)S(1)}) all-reduce(bf16[6912]{0:T(1024)(128)(2,1)S(1)} %dynamic-update-slice, ...), channel_id=1, replica_groups=mesh['wide'=16,'narrow'=2] {'wide'}, use_global_device_ids=true, to_apply=%add | all-reduce | flops 16128 | bytes 64512
  83.8 51.2 %all-gather.15.cloned.1.call-done = bf16[1152,6912]{1,0:T(8,128)(2,1)} async-done(((bf16[72,6912]{1,0:T(8,128)(2,1)}), bf16[1152,6912]{1,0:T(8,128)(2,1)}) %all-gather.15.cloned.1.call-update) | async-done | bytes 15925264 | tf_op jit(solution)/shard_map/all_gather | solution.py:80
  135.0 7.7 convolution_add_fusion
  144.3 63.4 %all-gather.17.cloned.1.call-done = bf16[1152,3456]{1,0:T(8,128)(2,1)} async-done(((bf16[72,3456]{1,0:T(8,128)(2,1)}), bf16[1152,3456]{1,0:T(8,128)(2,1)}) %all-gather.17.cloned.1.call-update) | async-done | bytes 7962640 | tf_op jit(solution)/shard_map/all_gather | solution.py:82
  207.7 5.8 fusion.10
  213.5 1.8 copy-done.3
  216.3 2.6 fusion.50
  223.7 1.6 fusion.63
  225.3 12.2 all-gather.21.cloned.1.call-done
  237.5 1.6 copy.95
  239.0 23.2 %all-gather.19.cloned.1.call-done = bf16[2,256,1152]{2,1,0:T(8,128)(2,1)} async-done(((bf16[2,128,1152]{2,1,0:T(8,128)(2,1)}), bf16[2,256,1152]{2,1,0:T(8,128)(2,1)}) %all-gather.19.cloned.1.call-update) | async-done | bytes 1179664 | tf_op jit(solution)/shard_map/all_gather | solution.py:123
  262.3 1.6 copy.93
  264.8 1.4 exponential_reduce_fusion
  268.1 39.5 %all-gather.23.cloned.1.call-done = bf16[1152,1152]{1,0:T(8,128)(2,1)} async-done(((bf16[72,1152]{1,0:T(8,128)(2,1)}), bf16[1152,1152]{1,0:T(8,128)(2,1)}) %all-gather.23.cloned.1.call-update) | async-done | bytes 2654224 | tf_op jit(solution)/shard_map/all_gather | solution.py:84
  307.6 3.9 fusion.65
  313.9 83.2 %all-gather.25.cloned.1.call-done = bf16[1152,4608]{1,0:T(8,128)(2,1)} async-done(((bf16[72,4608]{1,0:T(8,128)(2,1)}), bf16[1152,4608]{1,0:T(8,128)(2,1)}) %all-gather.25.cloned.1.call-update) | async-done | bytes 10616848 | tf_op jit(solution)/shard_map/all_gather | solution.py:86
  397.1 10.2 multiply_convert_fusion
  407.3 79.0 %all-gather.27.cloned.1.call-done = bf16[4608,1152]{1,0:T(8,128)(2,1)} async-done(((bf16[288,1152]{1,0:T(8,128)(2,1)}), bf16[4608,1152]{1,0:T(8,128)(2,1)}) %all-gather.27.cloned.1.call-update) | async-done | bytes 10616848 | tf_op jit(solution)/shard_map/all_gather | solution.py:88
  486.3 10.0 fusion.70
  496.4 4.2 fusion.4
  500.7 10.0 multiply_reduce_fusion.2
  510.8 2.2 fusion.64
  515.2 3.8 multiply_reduce_fusion
  519.0 1.5 multiply_convert_fusion.1
  520.5 1.5 multiply_convert_fusion.2
  522.0 2.4 copy.98
  524.5 4.2 convolution_convert_fusion
  528.7 2.4 copy.99
  533.2 1.8 copy.106
  535.0 14.7 %all_to_all.72 = bf16[2,128,1152]{1,0,2:T(2,128)(2,1)S(1)} all-to-all(bf16[2,128,1152]{1,0,2:T(2,128)(2,1)} %copy.106), channel_id=1, replica_groups=mesh['wide'=16,'narrow'=2] {'narrow'}, dimensions={2} | all-to-all | bytes 1179648 | tf_op jit(solution)/shard_map/all_to_all | solution.py:243
  549.8 4.0 convolution_bitcast_fusion.3
  553.8 3.5 fusion.69
  557.4 1.5 copy.100
  558.9 15.0 %reduce-scatter.14.cloned.1.call-done = bf16[2,128,1152]{2,1,0:T(8,128)(2,1)} async-done(((bf16[2,256,1152]{2,1,0:T(8,128)(2,1)}), bf16[2,128,1152]{2,1,0:T(8,128)(2,1)}) %reduce-scatter.14.cloned.1.call-update) | async-done | bytes 589840 | tf_op jit(solution)/shard_map/reduce_scatter | solution.py:204
  573.9 2.6 pad_maximum_fusion
  576.5 4.9 copy.101
  581.3 35.6 %all_to_all.73 = bf16[2,128,3456]{1,0,2:T(2,128)(2,1)S(1)} all-to-all(bf16[2,128,3456]{1,0,2:T(2,128)(2,1)S(1)} %copy.101), channel_id=1, replica_groups=mesh['wide'=16,'narrow'=2] {'narrow'}, dimensions={2} | all-to-all | bytes 3538944 | tf_op jit(solution)/shard_map/all_to_all | solution.py:242
  617.2 6.9 convolution_bitcast_fusion.2
  624.2 5.6 copy.110
  629.9 45.5 %all_to_all.74 = bf16[2,128,4608]{1,0,2:T(2,128)(2,1)} all-to-all(bf16[2,128,4608]{1,0,2:T(2,128)(2,1)S(1)} %copy.110), channel_id=1, replica_groups=mesh['wide'=16,'narrow'=2] {'narrow'}, dimensions={2} | all-to-all | bytes 4718592 | tf_op jit(solution)/shard_map/all_to_all | solution.py:244
  675.3 5.7 copy.111
  681.0 7.2 convolution_bitcast_fusion
  689.9 17.3 %all_to_all.75 = bf16[2,128,1152]{1,0,2:T(2,128)(2,1)S(1)} all-to-all(bf16[2,128,1152]{1,0,2:T(2,128)(2,1)S(1)} %copy.113), channel_id=1, replica_groups=mesh['wide'=16,'narrow'=2] {'narrow'}, dimensions={2} | all-to-all | bytes 1179648 | tf_op jit(solution)/shard_map/all_to_all | solution.py:245
  707.3 10.7 all-gather.35.cloned.1.call-done
  718.1 10.6 convolution_bitcast_fusion.1
  730.5 6.4 fusion.48
  737.1 1.6 multiply_reduce_fusion.4
  738.9 7.5 all-reduce.14
  746.4 8.1 fusion.58
  757.2 61.2 %all-reduce.12 = (f32[6912]{0:T(1024)S(1)}, f32[2304]{0:T(1024)S(1)}, f32[1152]{0:T(1024)S(1)}, f32[4608]{0:T(1024)S(1)}, f32[1152]{0:T(1024)S(1)}) all-reduce(f32[6912]{0:T(1024)S(1)} %convert_reduce_fusion.1, bf16[2304]{0:T(1024)(128)(2,1)S(1)} %get-tuple-element.32, ...), channel_id=5, replica_groups=mesh['wide'=16,'narrow'=2] {'wide'}, use_global_device_ids=true, to_apply=%region_22.0.clone | all-reduce | flops 16128 | bytes 110592
  821.5 10.7 convolution_multiply_fusion
  833.1 5.2 all-gather.1
  839.5 54.7 %reduce-scatter.16.cloned.1.call-done = f32[72,1728]{1,0:T(8,128)} async-done(((f32[1152,1728]{1,0:T(8,128)}), f32[72,1728]{1,0:T(8,128)}) %reduce-scatter.16.cloned.1.call-update) | async-done | bytes 497680 | tf_op jit(solution)/shard_map/reduce_scatter | solution.py:254
  895.3 8.7 all-gather
  904.3 1.8 reshape.166
  906.1 112.0 %reduce-scatter.18.cloned.1.call-done = f32[72,2304]{1,0:T(8,128)} async-done(((f32[1152,2304]{1,0:T(8,128)}), f32[72,2304]{1,0:T(8,128)}) %reduce-scatter.18.cloned.1.call-update) | async-done | bytes 663568 | tf_op jit(solution)/shard_map/reduce_scatter | solution.py:258
  1019.2 10.1 all_gather.86
  1030.5 119.4 %reduce-scatter.20.cloned.1.call-done = f32[288,576]{1,0:T(8,128)} async-done(((f32[4608,576]{1,0:T(8,128)}), f32[288,576]{1,0:T(8,128)}) %reduce-scatter.20.cloned.1.call-update) | async-done | bytes 663568 | tf_op jit(solution)/shard_map/reduce_scatter | solution.py:260
  1151.1 10.9 all-gather.2
  1162.6 2.0 reshape.168
  1164.6 161.5 %reduce-scatter.22.cloned.1.call-done = f32[72,3456]{1,0:T(8,128)} async-done(((f32[1152,3456]{1,0:T(8,128)}), f32[72,3456]{1,0:T(8,128)}) %reduce-scatter.22.cloned.1.call-update) | async-done | bytes 995344
  1327.3 13.8 %all_gather.80 = bf16[72,6912]{1,0:T(8,128)(2,1)S(1)} all-gather(bf16[72,3456]{1,0:T(8,128)(2,1)S(1)} %convert_element_type.222), channel_id=1, replica_groups=mesh['wide'=16,'narrow'=2] {'narrow'}, dimensions={1}, use_global_device_ids=true | all-gather | bytes 1492992 | tf_op jit(solution)/shard_map/all_gather | solution.py:264
  1341.2 1.4 convert_element_type.223
  (211 shorter events, 39.4 us)
Async XLA Ops:
  7.2 75.9 %copy-start.2 = (bf16[2,128,1152]{2,1,0:T(8,128)(2,1)S(1)}, bf16[2,128,1152]{2,1,0:T(8,128)(2,1)}, u32[]{:S(2)}) copy-start(bf16[2,128,1152]{2,1,0:T(8,128)(2,1)} %param.15) | copy-start | bytes 1769476
  7.2 127.8 %copy-start.30 = (bf16[2,1152]{1,0:T(2,128)(2,1)S(1)}, bf16[2,1152]{1,0:T(2,128)(2,1)}, u32[]{:S(2)}) copy-start(bf16[2,1152]{1,0:T(2,128)(2,1)} %param.16) | copy-start | bytes 13828
  7.2 127.8 %all-gather.15.cloned.1.call-start = ((), (), s32[]{:S(2)}) async-start(), calls=%async_computation.11 | async-start | bytes 16920576 | tf_op jit(solution)/shard_map/all_gather | solution.py:80
  7.9 199.8 %all-gather.17.cloned.1.call-start = ((), (), s32[]{:S(2)}) async-start(), calls=%async_computation.12 | async-start | bytes 8460288 | tf_op jit(solution)/shard_map/all_gather | solution.py:82
  8.7 228.8 %all-gather.21.cloned.1.call-start = ((), (), s32[]{:S(2)}) async-start(), calls=%async_computation.14 | async-start | bytes 1769472 | tf_op jit(solution)/shard_map/all_gather | solution.py:122
  83.3 60.1 %copy-start.36 = (f32[2,128]{1,0:T(2,128)}, f32[2,128]{1,0:T(2,128)S(1)}, u32[]{:S(2)}) copy-start(f32[2,128]{1,0:T(2,128)S(1)} %broadcast_multiply_fusion.5) | copy-start | bytes 3076
  83.6 59.8 %copy-start.43 = (f32[2,128]{1,0:T(2,128)}, f32[2,128]{1,0:T(2,128)S(1)}, u32[]{:S(2)}) copy-start(f32[2,128]{1,0:T(2,128)S(1)} %add_rsqrt_fusion.1) | copy-start | bytes 3076
  83.8 59.0 %copy-start.26 = (f32[2,576]{1,0:T(2,128)}, f32[2,576]{1,0:T(2,128)S(1)}, u32[]{:S(2)}) copy-start(f32[2,576]{1,0:T(2,128)S(1)} %get-tuple-element.61) | copy-start | bytes 13828
  83.8 59.0 %copy-start.28 = (f32[2,576]{1,0:T(2,128)}, f32[2,576]{1,0:T(2,128)S(1)}, u32[]{:S(2)}) copy-start(f32[2,576]{1,0:T(2,128)S(1)} %get-tuple-element.62) | copy-start | bytes 13828
  143.4 80.2 %copy-start.32 = (f32[2,1152]{1,0:T(2,128)}, f32[2,1152]{1,0:T(2,128)S(1)}, u32[]{:S(2)}) copy-start(f32[2,1152]{1,0:T(2,128)S(1)} %get-tuple-element.53) | copy-start | bytes 27652
  144.3 69.2 %copy-start.7 = (bf16[2,128,1152]{2,1,0:T(8,128)(2,1)}, bf16[2,128,1152]{2,1,0:T(8,128)(2,1)S(1)}, u32[]{:S(2)}) copy-start(bf16[2,128,1152]{2,1,0:T(8,128)(2,1)S(1)} %fusion.43) | copy-start | bytes 1769476
  213.5 1.8 copy-start.3
  216.2 46.1 %all-gather.19.cloned.1.call-start = ((), (), s32[]{:S(2)}) async-start(), calls=%async_computation.13 | async-start | bytes 1769472 | tf_op jit(solution)/shard_map/all_gather | solution.py:123
  218.9 4.8 copy-start.12
  218.9 88.7 %all-gather.23.cloned.1.call-start = ((), (), s32[]{:S(2)}) async-start(), calls=%async_computation.15 | async-start | bytes 2820096 | tf_op jit(solution)/shard_map/all_gather | solution.py:84
  219.5 177.7 %all-gather.25.cloned.1.call-start = ((), (), s32[]{:S(2)}) async-start(), calls=%async_computation.16 | async-start | bytes 11280384 | tf_op jit(solution)/shard_map/all_gather | solution.py:86
  220.1 266.3 %all-gather.27.cloned.1.call-start = ((), (), s32[]{:S(2)}) async-start(), calls=%async_computation.17 | async-start | bytes 11280384 | tf_op jit(solution)/shard_map/all_gather | solution.py:88
  220.8 329.0 %all-gather.31.cloned.1.call-start = ((), (), s32[]{:S(2)}) async-start(), calls=%async_computation.22 | async-start | bytes 1769472 | tf_op jit(solution)/shard_map/all_gather | solution.py:237
  223.3 2.0 copy-start.48
  223.6 40.2 %copy-start.8 = (bf16[2,128,1152]{1,2,0:T(8,128)(2,1)}, bf16[2,128,1152]{1,2,0:T(8,128)(2,1)S(1)}, u32[]{:S(2)}) copy-start(bf16[2,128,1152]{1,2,0:T(8,128)(2,1)S(1)} %copy.94) | copy-start | bytes 1769476
  239.0 25.8 %copy-start.4 = (bf16[2,256,1152]{1,2,0:T(8,128)(2,1)}, bf16[2,256,1152]{1,2,0:T(8,128)(2,1)S(1)}, u32[]{:S(2)}) copy-start(bf16[2,256,1152]{1,2,0:T(8,128)(2,1)S(1)} %copy.95) | copy-start | bytes 3538948
  264.8 1.9 copy-start
  268.1 43.4 %copy-start.5 = (bf16[2,16,72,128]{3,2,1,0:T(8,128)(2,1)}, bf16[2,16,72,128]{3,2,1,0:T(8,128)(2,1)S(1)}, u32[]{:S(2)}) copy-start(bf16[2,16,72,128]{3,2,1,0:T(8,128)(2,1)S(1)} %convolution_convert_fusion.1) | copy-start | bytes 1769476
  311.5 1.4 copy-start.34
  312.3 246.5 %reduce-scatter.12.cloned.1.call-start = ((), (), s32[]{:S(2)}) async-start(), calls=%async_computation.18 | async-start | bytes 1769472 | tf_op jit(solution)/shard_map/reduce_scatter | solution.py:201
  313.9 93.4 %copy-start.16 = (bf16[2,128,1152]{2,1,0:T(8,128)(2,1)}, bf16[2,128,1152]{2,1,0:T(8,128)(2,1)S(1)}, u32[]{:S(2)}) copy-start(bf16[2,128,1152]{2,1,0:T(8,128)(2,1)S(1)} %add_convert_fusion) | copy-start | bytes 1769476
  486.3 10.0 copy-start.50
  496.4 4.3 copy-start.19
  496.4 4.3 copy-start.13
  500.6 10.1 copy-start.20
  500.6 10.1 copy-start.22
  500.6 10.1 copy-start.25
  500.6 10.1 copy-start.35
  500.7 10.1 copy-start.42
  500.7 10.1 copy-start.49
  510.7 3.1 copy-start.6
  515.2 3.8 copy-start.1
  519.0 1.5 copy-start.9
  524.4 49.5 %reduce-scatter.14.cloned.1.call-start = ((), (), s32[]{:S(2)}) async-start(), calls=%async_computation.19 | async-start | bytes 1769472 | tf_op jit(solution)/shard_map/reduce_scatter | solution.py:204
  531.1 2.1 copy-start.15
  531.1 86.1 %all-gather.29.cloned.1.call-start = ((), (), s32[]{:S(2)}) async-start(), calls=%async_computation.20 | async-start | bytes 1769472 | tf_op jit(solution)/shard_map/all_gather | solution.py:236
  531.8 149.2 %all-gather.33.cloned.1.call-start = ((), (), s32[]{:S(2)}) async-start(), calls=%async_computation.23 | async-start | bytes 1769472 | tf_op jit(solution)/shard_map/all_gather | solution.py:238
  532.4 185.6 %all-gather.35.cloned.1.call-start = ((), (), s32[]{:S(2)}) async-start(), calls=%async_computation.25 | async-start | bytes 7077888 | tf_op jit(solution)/shard_map/all_gather | solution.py:239
  533.2 299.0 %reduce-scatter.24.cloned.1.call-start = ((), (), s32[]{:S(2)}) async-start(), calls=%async_computation.28 | async-start | bytes 3133440
  553.8 340.4 %reduce-scatter.16.cloned.1.call-start = ((), (), s32[]{:S(2)}) async-start(), calls=%async_computation.21 | async-start | bytes 8773632 | tf_op jit(solution)/shard_map/reduce_scatter | solution.py:254
  624.2 394.0 %reduce-scatter.18.cloned.1.call-start = ((), (), s32[]{:S(2)}) async-start(), calls=%async_computation.24 | async-start | bytes 11280384 | tf_op jit(solution)/shard_map/reduce_scatter | solution.py:258
  688.3 461.7 %reduce-scatter.20.cloned.1.call-start = ((), (), s32[]{:S(2)}) async-start(), calls=%async_computation.26 | async-start | bytes 12533760 | tf_op jit(solution)/shard_map/reduce_scatter | solution.py:260
  728.6 1.8 copy-start.21
  728.6 1.8 copy-start.24
  728.6 1.8 copy-start.37
  728.7 597.4 %reduce-scatter.22.cloned.1.call-start = ((), (), s32[]{:S(2)}) async-start(), calls=%async_computation.27 | async-start | bytes 16920576
  730.4 6.5 copy-start.10
  730.4 6.5 copy-start.11
  730.5 6.5 copy-start.44
  737.0 1.8 copy-start.47
  737.0 1.8 copy-start.46
  737.0 1.8 copy-start.45
  737.0 1.8 copy-start.33
  737.0 1.8 copy-start.38
  737.0 1.8 copy-start.39
  737.1 1.8 copy-start.41
  737.1 9.3 copy-start.27
  737.1 9.3 copy-start.29
  737.1 9.3 copy-start.31
  (5 other events, 4.3 us)
Sparse Core Ops, SparseCore 0:
  10.2 124.7 all-gather.14
  137.2 70.4 all-gather.16
  216.3 21.1 all-gather.20
  239.4 22.7 all-gather.18
  264.2 43.3 all-gather.22
  309.8 87.3 all-gather.24
  399.4 86.8 all-gather.26
  488.4 20.9 all-gather.30
  524.5 21.7 reduce-scatter.11
  549.1 24.7 reduce-scatter.13
  575.4 34.3 all-gather.28
  611.2 23.1 all-gather.32
  636.0 82.0 all-gather.34
  721.8 65.2 reduce-scatter.23
  791.0 103.1 reduce-scatter.15
  898.1 119.9 reduce-scatter.17
  1022.1 127.7 reduce-scatter.19
  1154.5 171.5 reduce-scatter.21
where the time goes:
time: 1360 us; the launch traced here: 1350 us
  waiting for transfers between devices  830 us (61%)
  blocking collectives  296 us (22%)
  matrix products  122 us (9%)
  local copies, waits for them, and re-layouts  50.4 us (4%)
  other arithmetic  28.4 us (2%)
  between operations  21.4 us (2%)
    unnamed x20, waiting for transfers between devices  167 us
    unnamed x2, blocking collectives  127 us
    reduce_scatter x1, waiting for transfers between devices, on_device(): lax.psum_scatter(grad_fc2_part, 'wide', scatter_dimension=0, tiled=True)  119 us
    reduce_scatter x1, waiting for transfers between devices, on_device(): lax.psum_scatter(grad_fc1_part, 'wide', scatter_dimension=0, tiled=True)  112 us
    all_gather x1, waiting for transfers between devices, on_device(): lax.all_gather(w_fc1, 'wide', axis=0, tiled=True)  83.2 us
    all_gather x1, waiting for transfers between devices, on_device(): lax.all_gather(w_fc2, 'wide', axis=0, tiled=True)  79 us
    all_gather x1, waiting for transfers between devices, on_device(): lax.all_gather(w_qkv, 'wide', axis=0, tiled=True)  63.4 us
    reduce_scatter x1, waiting for transfers between devices, on_device(): lax.psum_scatter(grad_qkv_part, 'wide', scatter_dimension=0, tiled=True)  54.7 us
  transfers between devices with their start and end apart: 18, of which 13 were waited for; matrix products, arithmetic and copies ran while one was open for 14% of the time, Pallas kernels for 0%

commit v1 on v0

v1 whole, which is shorter than its diff:
```python
import math

import jax
import jax.numpy as jnp
from jax import lax
from jax.sharding import PartitionSpec as P

HEADS = 16
HEAD_DIM = 72

F32 = jnp.float32
BF16 = jnp.bfloat16
eps_norm = 1e-06


def norm_rows(value):
    center = value - jnp.mean(value, axis=-1, keepdims=True)
    inv_std = lax.rsqrt(jnp.mean(center * center, axis=-1, keepdims=True) + eps_norm)
    return (center * inv_std, inv_std)


def norm_back(grad, normed, inv_std):
    return inv_std * (
        grad
        - jnp.mean(grad, axis=-1, keepdims=True)
        - normed * jnp.mean(grad * normed, axis=-1, keepdims=True)
    )


def gelu_tanh(value):
    return (
        0.5
        * value
        * (1.0 + jnp.tanh(0.7978845608028654 * (value + 0.044715 * value * value * value)))
    )


def gelu_tanh_grad(value):
    inner = 0.7978845608028654 * (value + 0.044715 * value * value * value)
    tan = jnp.tanh(inner)
    slope = 0.7978845608028654 * (1.0 + 3.0 * 0.044715 * value * value)
    return 0.5 * (1.0 + tan) + 0.5 * value * (1.0 - tan * tan) * slope


def time_features(steps, width):
    half_width = width // 2
    freqs = jnp.exp(-math.log(10000.0) * jnp.arange(half_width).astype(F32) / half_width)
    angles = steps.astype(F32)[:, None] * freqs[None, :]
    return jnp.concatenate([jnp.cos(angles), jnp.sin(angles)], axis=-1)


def mm(left, right):
    return jnp.einsum("sk,kn->sn", left, right, preferred_element_type=F32)


def mm_back(grad, weight):
    return jnp.einsum("sn,kn->sk", grad, weight, preferred_element_type=F32)


def outer_sum(left, right):
    return jnp.einsum("sk,sn->kn", left, right, preferred_element_type=F32)


def gather_wide(value, axis=0):
    return lax.all_gather(value, "wide", axis=axis, tiled=True)


def on_device(
    tokens,
    cond,
    timesteps,
    counts,
    w_ada,
    b_ada,
    w_qkv,
    b_qv,
    w_proj,
    b_proj,
    w_fc1,
    b_fc1,
    w_fc2,
    b_fc2,
    cotangent,
):
    slots, half_len, width = tokens.shape
    pair = lax.axis_size("narrow")
    n_wide = lax.axis_size("wide")
    me = lax.axis_index("narrow")
    here = lax.axis_index("wide")
    seq = half_len * pair
    rows = slots * half_len
    all_rows = slots * seq
    wh = width // pair
    heads = HEADS // pair
    mlp = w_fc1.shape[1]
    mh = mlp // pair
    shard = w_ada.shape[0]
    head_scale = 1.0 / math.sqrt(HEAD_DIM)

    qkv_half = lax.dynamic_index_in_dim(
        w_qkv.reshape(-1, 3, pair, wh), me, 2, keepdims=False
    ).reshape(-1, 3 * wh)
    fc1_half = lax.dynamic_index_in_dim(
        w_fc1.reshape(-1, n_wide, pair, mh // n_wide), me, 2, keepdims=False
    ).reshape(-1, mh)
    fc2_half = lax.dynamic_index_in_dim(
        w_fc2.reshape(pair, -1, width), me, 0, keepdims=False
    )

    cond_vec = cond.astype(F32) + time_features(timesteps, width)
    cond_sig = jax.nn.sigmoid(cond_vec)
    silu_low = (cond_vec * cond_sig).astype(BF16)
    silu_all = gather_wide(silu_low)
    silu_cols = lax.dynamic_slice_in_dim(silu_all, here * shard, shard, 1)
    mod_part = jnp.dot(silu_cols, w_ada, preferred_element_type=F32)
    biases = gather_wide(jnp.concatenate([b_ada, b_qv, b_proj, b_fc1, b_fc2])[None])
    cuts = []
    at = 0
    for piece in (b_ada, b_qv, b_proj, b_fc1, b_fc2):
        cuts.append(biases[:, at : at + piece.shape[0]].astype(F32))
        at += piece.shape[0]
    ada_bias, qv_bias, proj_bias, fc1_bias, fc2_bias = [c.reshape(-1) for c in cuts]
    fc1_bias_half = lax.dynamic_index_in_dim(
        fc1_bias.reshape(n_wide, pair, -1), me, 1, keepdims=False
    ).reshape(-1)
    qv_bias_half = lax.dynamic_index_in_dim(qv_bias.reshape(2, pair, wh), me, 1, keepdims=False)

    modulate = lax.psum_scatter(mod_part, "wide", scatter_dimension=0, tiled=True) + ada_bias
    shift_one, scale_one, gate_one, shift_two, scale_two, gate_two = [
        modulate[:, None, i * width : (i + 1) * width] for i in range(6)
    ]

    qkv_w = gather_wide(qkv_half)
    proj_w = gather_wide(w_proj)
    fc1_w = gather_wide(fc1_half)
    fc2_w = gather_wide(fc2_half)

    def both_halves(value):
        value = value.reshape(slots, half_len, -1)
        return lax.all_gather(value, "narrow", axis=1, tiled=True).reshape(all_rows, -1)

    def sum_halves(value):
        value = value.astype(BF16).reshape(slots, seq, -1)
        return (
            lax.psum_scatter(value, "narrow", scatter_dimension=1, tiled=True)
            .astype(F32)
            .reshape(slots, half_len, -1)
        )

    live_slot = (jnp.arange(slots, dtype=jnp.int32) < counts[0]).astype(F32)[:, None, None]
    tok_float = tokens.astype(F32)
    normed_one, inv_one = norm_rows(tok_float)
    a_in = (normed_one * (1.0 + scale_one) + shift_one).astype(BF16).reshape(rows, width)
    a_full = both_halves(a_in)
    qkv = mm(a_full, qkv_w)
    query = (qkv[:, :wh] + qv_bias_half[0]).astype(BF16)
    keys = qkv[:, wh : 2 * wh].astype(BF16)
    values = (qkv[:, 2 * wh :] + qv_bias_half[1]).astype(BF16)

    def to_heads(value):
        return value.reshape(slots, seq, heads, HEAD_DIM)

    query_heads, key_heads, value_heads = to_heads(query), to_heads(keys), to_heads(values)
    scores = (
        jnp.einsum("cqhe,ckhe->chqk", query_heads, key_heads, preferred_element_type=F32)
        * head_scale
    )
    log_total = jax.nn.logsumexp(scores, axis=-1, keepdims=True)
    probs = jnp.exp(scores - log_total)
    probs_low = probs.astype(BF16)
    attended = (
        jnp.einsum("chqk,ckhe->cqhe", probs_low, value_heads, preferred_element_type=F32)
        .astype(BF16)
        .reshape(slots, seq, wh)
    )
    att_own = lax.all_to_all(attended, "narrow", split_axis=1, concat_axis=2, tiled=True)
    att_own = att_own.reshape(rows, width)
    attn_out = (mm(att_own, proj_w) + proj_bias).reshape(slots, half_len, width)
    mid = tok_float + gate_one * attn_out
    normed_two, inv_two = norm_rows(mid)
    m_in = (normed_two * (1.0 + scale_two) + shift_two).astype(BF16).reshape(rows, width)
    m_full = both_halves(m_in)
    hidden = mm(m_full, fc1_w) + fc1_bias_half
    act_low = gelu_tanh(hidden).astype(BF16)
    mlp_out = sum_halves(mm(act_low, fc2_w)) + fc2_bias
    out = (live_slot * (mid + gate_two * mlp_out)).astype(BF16)

    grad_out = live_slot * cotangent.astype(F32)
    d_mlp = (gate_two * grad_out).astype(BF16).reshape(rows, width)
    d_mlp_full = both_halves(d_mlp)
    d_gate_two = jnp.sum(grad_out * mlp_out, axis=1)
    fc2_bias_sum = jnp.sum(d_mlp.astype(F32), axis=0)
    grad_fc2_part = outer_sum(act_low, d_mlp_full)
    d_hidden = (mm_back(d_mlp_full, fc2_w) * gelu_tanh_grad(hidden)).astype(BF16)
    fc1_bias_sum = jnp.sum(d_hidden.astype(F32), axis=0)
    grad_fc1_part = outer_sum(m_full, d_hidden)
    d_m_in = sum_halves(mm_back(d_hidden, fc1_w))
    d_scale_two = jnp.sum(d_m_in * normed_two, axis=1)
    d_shift_two = jnp.sum(d_m_in, axis=1)
    d_mid = grad_out + norm_back(d_m_in * (1.0 + scale_two), normed_two, inv_two)
    d_attn = (gate_one * d_mid).astype(BF16).reshape(rows, width)
    d_gate_one = jnp.sum(d_mid * attn_out, axis=1)
    proj_bias_sum = jnp.sum(d_attn.astype(F32), axis=0)
    grad_proj_part = outer_sum(att_own, d_attn)
    d_att_own = mm_back(d_attn, proj_w).astype(BF16).reshape(slots, half_len, width)
    d_att = lax.all_to_all(d_att_own, "narrow", split_axis=2, concat_axis=1, tiled=True)
    d_att = to_heads(d_att)
    d_probs = jnp.einsum("cqhe,ckhe->chqk", d_att, value_heads, preferred_element_type=F32)
    d_scores = (probs * (d_probs - jnp.sum(probs * d_probs, axis=-1, keepdims=True))).astype(BF16)
    d_query = (
        jnp.einsum("chqk,ckhe->cqhe", d_scores, key_heads, preferred_element_type=F32)
        * head_scale
    ).astype(BF16).reshape(all_rows, wh)
    d_keys = (
        jnp.einsum("chqk,cqhe->ckhe", d_scores, query_heads, preferred_element_type=F32)
        * head_scale
    ).astype(BF16).reshape(all_rows, wh)
    d_values = (
        jnp.einsum("chqk,cqhe->ckhe", probs_low, d_att, preferred_element_type=F32)
        .astype(BF16)
        .reshape(all_rows, wh)
    )
    d_qkv = jnp.concatenate([d_query, d_keys, d_values], axis=-1)
    qv_bias_sum = jnp.stack(
        [jnp.sum(d_query.astype(F32), axis=0), jnp.sum(d_values.astype(F32), axis=0)]
    )
    grad_qkv_part = outer_sum(a_full, d_qkv)
    d_a_in = sum_halves(mm_back(d_qkv, qkv_w))
    d_scale_one = jnp.sum(d_a_in * normed_one, axis=1)
    d_shift_one = jnp.sum(d_a_in, axis=1)
    grad_tokens = d_mid + norm_back(d_a_in * (1.0 + scale_one), normed_one, inv_one)

    d_modulate = jnp.concatenate(
        [d_shift_one, d_scale_one, d_gate_one, d_shift_two, d_scale_two, d_gate_two], axis=-1
    )
    def place(half, shape, axis):
        spread = jnp.zeros(shape, F32)
        return lax.dynamic_update_index_in_dim(spread, half, me, axis)

    qv_sum = place(qv_bias_sum, (2, pair, wh), 1).reshape(n_wide, -1)
    fc1_sum = place(fc1_bias_sum.reshape(n_wide, -1), (n_wide, pair, mh // n_wide), 1).reshape(
        n_wide, -1
    )
    bias_sums = jnp.concatenate(
        [
            qv_sum,
            proj_bias_sum.reshape(n_wide, -1),
            fc1_sum,
            fc2_bias_sum.reshape(n_wide, -1),
        ],
        axis=1,
    )
    bias_own = lax.psum(
        lax.psum_scatter(bias_sums, "wide", scatter_dimension=0, tiled=True), "narrow"
    ).reshape(-1)
    bias_grads = []
    at = 0
    for piece in (b_qv, b_proj, b_fc1, b_fc2):
        bias_grads.append(bias_own[at : at + piece.shape[0]])
        at += piece.shape[0]

    d_mod_low = lax.psum(d_modulate, "narrow").astype(BF16)
    d_mod_all = gather_wide(d_mod_low)
    grad_ada = outer_sum(silu_cols, d_mod_all)
    ada_cut = b_ada.shape[0]
    grad_ada_bias = jnp.sum(
        lax.dynamic_slice_in_dim(d_mod_all, here * ada_cut, ada_cut, 1).astype(F32), axis=0
    )
    d_silu_cols = mm_back(d_mod_all, w_ada)
    d_silu = lax.all_to_all(d_silu_cols, "wide", split_axis=0, concat_axis=1, tiled=True)
    grad_cond = d_silu * (cond_sig + cond_vec * cond_sig * (1.0 - cond_sig))

    def scatter_wide(part):
        return lax.psum_scatter(part.astype(BF16), "wide", scatter_dimension=0, tiled=True)

    def join_pair(piece):
        return lax.all_gather(piece, "narrow", axis=0, tiled=False).astype(F32)

    fc2_own = join_pair(scatter_wide(grad_fc2_part)).reshape(-1, width)
    fc1_own = join_pair(scatter_wide(grad_fc1_part)).reshape(pair, shard, n_wide, -1)
    fc1_own = fc1_own.transpose(1, 2, 0, 3).reshape(shard, mlp)
    proj_own = jnp.sum(join_pair(scatter_wide(grad_proj_part)), axis=0)
    qkv_own = join_pair(scatter_wide(grad_qkv_part)).reshape(pair, shard, 3, wh)
    qkv_own = qkv_own.transpose(1, 2, 0, 3).reshape(shard, 3 * width)

    return (
        out,
        grad_tokens,
        grad_cond,
        grad_ada,
        grad_ada_bias,
        qkv_own,
        bias_grads[0],
        proj_own,
        bias_grads[1],
        fc1_own,
        bias_grads[2],
        fc2_own,
        bias_grads[3],
    )


def solution(mesh):
    in_specs = (
        P("wide", "narrow", None),
        P("wide", None),
        P("wide"),
        P("wide"),
        P("wide", None),
        P("wide"),
        P("wide", None),
        P("wide"),
        P("wide", None),
        P("wide"),
        P("wide", None),
        P("wide"),
        P("wide", None),
        P("wide"),
        P("wide", "narrow", None),
    )
    out_specs = (
        P("wide", "narrow", None),
        P("wide", "narrow", None),
        P("wide", None),
        P("wide", None),
        P("wide"),
        P("wide", None),
        P("wide"),
        P("wide", None),
        P("wide"),
        P("wide", None),
        P("wide"),
        P("wide", None),
        P("wide"),
    )
    return jax.shard_map(
        on_device, mesh=mesh, in_specs=in_specs, out_specs=out_specs, check_vma=False
    )
```

time: 1360 us -> 866 us (0.64)
  waiting for transfers between devices: 830 us -> 452 us
  blocking collectives: 296 us -> 212 us
  matrix products: 122 us -> 78.1 us
    all_gather x11 -> x7, waiting for transfers between devices: 362 us -> 220 us  [the longest x4 185 us: gather_wide(): return lax.all_gather(value, 'wide', axis=axis, tiled=True)]
    unnamed x20 -> x17, waiting for transfers between devices: 167 us -> 30 us
    reduce_scatter x5 -> x6, waiting for transfers between devices: 301 us -> 191 us  [the longest x3 158 us: scatter_wide(): lax.psum_scatter(part.astype(BF16), 'wide', scatter_dimension=0, tiled=True)]
    all_to_all x4 -> x1, blocking collectives: 113 us -> 11.5 us  [on_device(): lax.all_to_all(d_att_own, 'narrow', split_axis=2, concat_axis=1, tiled=True)]
    dot_general x16, matrix products: 111 us -> 74 us  [the longest x5 25.5 us: outer_sum(): return jnp.einsum('sk,sn->kn', left, right, preferred_element_type=F32)]
    reshape x0 -> x20, local copies, waits for them, and re-layouts: none -> 32.6 us  [the longest x3 11.9 us: on_device(): fc1_own = fc1_own.transpose(1, 2, 0, 3).reshape(shard, mlp)]
    all_gather x5 -> x6, blocking collectives: 48.7 us -> 74.2 us  [the longest x2 41.7 us: gather_wide(): return lax.all_gather(value, 'wide', axis=axis, tiled=True)]
    convert_element_type x14 -> x3, local copies, waits for them, and re-layouts: 20.8 us -> 1.83 us  [the longest x1 0.61 us: on_device(): d_values = jnp.einsum('chqk,cqhe->ckhe', probs_low, d_att, preferred_elem...]
  transfers between devices with their start and end apart: 18 -> 17, of which waited for: 13 -> 15; matrix products, arithmetic and copies ran while one was open for 14% -> 13% of each run, Pallas kernels for 0% -> 0%
where the time goes in v1:
time: 866 us; the launch traced here: 857 us
  waiting for transfers between devices  452 us (52%)
  blocking collectives  212 us (24%)
  matrix products  78.1 us (9%)
  local copies, waits for them, and re-layouts  60.2 us (7%)
  other arithmetic  27.5 us (3%)
  between operations  17.3 us (2%)
  starting transfers between devices  8.71 us (1%)
    all_gather x4, waiting for transfers between devices, gather_wide(): return lax.all_gather(value, 'wide', axis=axis, tiled=True)  185 us
    reduce_scatter x3, waiting for transfers between devices, scatter_wide(): lax.psum_scatter(part.astype(BF16), 'wide', scatter_dimension=0, tiled=True)  158 us
    unnamed x2, blocking collectives  119 us
    all_gather x2, blocking collectives, gather_wide(): return lax.all_gather(value, 'wide', axis=axis, tiled=True)  41.7 us
    all_gather x3, waiting for transfers between devices, both_halves(): lax.all_gather(value, 'narrow', axis=1, tiled=True).reshape(all_rows, -1)  34.3 us
    reduce_scatter x3, waiting for transfers between devices, sum_halves(): lax.psum_scatter(value, 'narrow', scatter_dimension=1, tiled=True)  33.5 us
    all_gather x4, blocking collectives, join_pair(): return lax.all_gather(piece, 'narrow', axis=0, tiled=False).astype(F32)  32.5 us
    unnamed x17, waiting for transfers between devices  30 us
  transfers between devices with their start and end apart: 17, of which 15 were waited for; matrix products, arithmetic and copies ran while one was open for 13% of the time, Pallas kernels for 0%

profile of v1, /device:TPU:0, one launch (start us, length us, event | category | flops | bytes accessed | tf_op | source)
XLA Modules:
  0.0 856.6 jit_solution(5851021819470463203)
XLA Ops:
  9.1 23.3 %all-gather.6 = bf16[16,2,1152]{2,1,0:T(2,128)(2,1)S(1)} all-gather(bf16[1,2,1152]{2,1,0:T(2,128)(2,1)S(1)} %convert_bitcast_fusion.1), channel_id=1, replica_groups=mesh['wide'=16,'narrow'=2] {'wide'}, dimensions={0}, use_global_device_ids=true | all-gather | bytes 78336 | tf_op jit(solution)/shard_map/all_gather | solution.py:65
  32.4 1.3 fusion.66
  35.4 58.0 %all-reduce = bf16[16128]{0:T(1024)(128)(2,1)S(1)} all-reduce(bf16[16128]{0:T(1024)(128)(2,1)S(1)} %dynamic-update-slice), channel_id=2, replica_groups=mesh['wide'=16,'narrow'=2] {'wide'}, use_global_device_ids=true, to_apply=%add | all-reduce | flops 16128 | bytes 64512
  94.7 29.3 %all-reduce.7.cloned.1.call-done = f32[32,6912]{1,0:T(8,128)} async-done(((f32[32,6912]{1,0:T(8,128)}), f32[32,6912]{1,0:T(8,128)}) %all-reduce.7.cloned.1.call-update) | async-done | bytes 884752
  127.3 1.9 dynamic-slice_reduce_fusion.1
  130.9 17.7 %all-gather.16.cloned.1.call-done = bf16[2,256,1152]{2,1,0:T(8,128)(2,1)} async-done(((bf16[2,128,1152]{2,1,0:T(8,128)(2,1)}), bf16[2,256,1152]{2,1,0:T(8,128)(2,1)}) %all-gather.16.cloned.1.call-update) | async-done | bytes 1179664 | tf_op jit(solution)/shard_map/all_gather | solution.py:140
  148.7 53.2 %all-gather.18.cloned.1.call-done = bf16[1152,1728]{1,0:T(8,128)(2,1)} async-done(((bf16[72,1728]{1,0:T(8,128)(2,1)}), bf16[1152,1728]{1,0:T(8,128)(2,1)}) %all-gather.18.cloned.1.call-update) | async-done | bytes 3981328 | tf_op jit(solution)/shard_map/all_gather | solution.py:65
  201.9 5.1 fusion.76
  208.4 2.2 reshape.241
  212.2 1.2 copy-done.1
  214.3 1.8 copy.87
  216.0 3.5 all-to-all-start
  220.6 9.0 %all-to-all-done = bf16[2,256,576]{2,0,1:T(2,128)(2,1)S(1)} async-done(((bf16[2,256,576]{2,0,1:T(2,128)(2,1)}), bf16[2,256,576]{2,0,1:T(2,128)(2,1)S(1)}, u32[]{:S(2)}, u32[]{:S(2)}) %all-to-all-start) | async-done | bytes 589856 | tf_op jit(solution)/shard_map/all_to_all | solution.py:176
  229.6 2.1 copy.89
  231.7 14.0 %all-gather.20.cloned.1.call-done = bf16[1152,1152]{1,0:T(8,128)(2,1)} async-done(((bf16[72,1152]{1,0:T(8,128)(2,1)}), bf16[1152,1152]{1,0:T(8,128)(2,1)}) %all-gather.20.cloned.1.call-update) | async-done | bytes 2654224 | tf_op jit(solution)/shard_map/all_gather | solution.py:65
  245.7 3.0 convolution_add_fusion.1
  250.9 5.7 reshape.248
  256.6 5.9 dynamic-slice_reduce_fusion
  262.5 2.5 reshape.249
  265.8 2.7 convert_reduce_fusion.4
  268.6 1.7 constant_dynamic-slice_fusion
  271.1 1.4 all-gather.22.cloned.1.call-done
  272.5 59.0 %all-gather.24.cloned.1.call-done = bf16[1152,2304]{1,0:T(8,128)(2,1)} async-done(((bf16[72,2304]{1,0:T(8,128)(2,1)}), bf16[1152,2304]{1,0:T(8,128)(2,1)}) %all-gather.24.cloned.1.call-update) | async-done | bytes 5308432 | tf_op jit(solution)/shard_map/all_gather | solution.py:65
  331.5 8.3 convolution_add_fusion
  339.8 15.2 %all-gather.26.cloned.1.call-done = bf16[2,256,1152]{2,1,0:T(8,128)(2,1)} async-done(((bf16[2,128,1152]{2,1,0:T(8,128)(2,1)}), bf16[2,256,1152]{2,1,0:T(8,128)(2,1)}) %all-gather.26.cloned.1.call-update) | async-done | bytes 1179664 | tf_op jit(solution)/shard_map/all_gather | solution.py:140
  355.0 59.1 %all-gather.28.cloned.1.call-done = bf16[1,2304,1152]{2,1,0:T(8,128)(2,1)} async-done(((bf16[1,144,1152]{2,1,0:T(8,128)(2,1)}), bf16[1,2304,1152]{2,1,0:T(8,128)(2,1)}) %all-gather.28.cloned.1.call-update) | async-done | bytes 5308432 | tf_op jit(solution)/shard_map/all_gather | solution.py:65
  414.1 8.6 convert_reduce_fusion
  422.7 4.3 convolution_convert_fusion.5
  427.0 9.0 %fusion.16 = bf16[512,1152]{1,0:T(8,128)(2,1)} fusion(bf16[1,2304,1152]{2,1,0:T(8,128)(2,1)} %all-gather.28.cloned.1.call-done, f32[512,2304]{1,0:T(8,128)} %convolution_add_fusion), kind=kOutput, calls=%fused_computation.26 | convolution fusion | flops 2729115648 | bytes 11206656 | tf_op jit(solution)/shard_map/sk,kn->sn/dot_general | solution.py:53
  436.2 11.2 %reduce-scatter.12.cloned.1.call-done = bf16[2,128,1152]{2,1,0:T(8,128)(2,1)} async-done(((bf16[2,256,1152]{2,1,0:T(8,128)(2,1)}), bf16[2,128,1152]{2,1,0:T(8,128)(2,1)}) %reduce-scatter.12.cloned.1.call-update) | async-done | bytes 589840 | tf_op jit(solution)/shard_map/reduce_scatter | solution.py:145
  447.5 1.7 fusion.46
  449.8 22.3 %reduce-scatter.10.cloned.1.call-done = bf16[2,128,1152]{2,1,0:T(8,128)(2,1)} async-done(((bf16[2,256,1152]{2,1,0:T(8,128)(2,1)}), bf16[2,128,1152]{2,1,0:T(8,128)(2,1)}) %reduce-scatter.10.cloned.1.call-update) | async-done | bytes 589840 | tf_op jit(solution)/shard_map/reduce_scatter | solution.py:145
  472.0 4.4 convert_reduce_fusion.5
  478.1 11.5 %all_to_all.49 = bf16[2,128,1152]{1,0,2:T(2,128)(2,1)S(1)} all-to-all(bf16[2,128,1152]{1,0,2:T(2,128)(2,1)S(1)} %copy.91), channel_id=1, replica_groups=mesh['wide'=16,'narrow'=2] {'narrow'}, dimensions={2} | all-to-all | bytes 1179648 | tf_op jit(solution)/shard_map/all_to_all | solution.py:206
  490.7 3.3 convert_reduce_fusion.6
  494.2 1.2 multiply_reduce_fusion
  500.3 1.9 copy-done.40
  502.3 3.6 convolution_convert_fusion.4
  506.0 2.4 convolution_convert_fusion.2
  509.6 6.9 convolution_convert_fusion.1
  516.7 1.2 copy-done.44
  517.9 8.4 convolution_convert_fusion
  526.4 1.2 copy-done.42
  527.6 5.9 convolution_convert_fusion.3
  535.1 60.9 %all-reduce.2 = f32[16,576]{1,0:T(8,128)S(1)} all-reduce(f32[16,576]{1,0:T(8,128)S(1)} %pad_maximum_fusion), channel_id=13, replica_groups=mesh['wide'=16,'narrow'=2] {'wide'}, use_global_device_ids=true, to_apply=%region_29.30.clone | all-reduce | flops 9216 | bytes 73728
  596.7 1.9 fusion.47
  598.6 2.7 multiply_reduce_fusion.3
  601.4 7.9 all-reduce.4
  609.3 18.4 %all-gather.7 = bf16[16,2,6912]{2,1,0:T(2,128)(2,1)S(1)} all-gather(bf16[1,2,6912]{2,1,0:T(2,128)(2,1)S(1)} %bitcast.141), channel_id=1, replica_groups=mesh['wide'=16,'narrow'=2] {'wide'}, dimensions={0}, use_global_device_ids=true | all-gather | bytes 470016 | tf_op jit(solution)/shard_map/all_gather | solution.py:65
  628.9 3.7 all-to-all-start.2
  633.3 1.8 fusion.64
  637.0 2.4 all-to-all-done.2
  640.2 6.7 all-gather.3
  647.6 31.4 %reduce-scatter.18.cloned.1.call-done = bf16[72,2304]{1,0:T(8,128)(2,1)} async-done(((bf16[1152,2304]{1,0:T(8,128)(2,1)}), bf16[72,2304]{1,0:T(8,128)(2,1)}) %reduce-scatter.18.cloned.1.call-update) | async-done | bytes 331792 | tf_op jit(solution)/shard_map/reduce_scatter | solution.py:274
  679.0 9.1 %all-gather.4 = bf16[144,2304]{1,0:T(8,128)(2,1)S(1)} all-gather(bf16[72,2304]{1,0:T(8,128)(2,1)} %reduce-scatter.18.cloned.1.call-done), channel_id=6, replica_groups=mesh['wide'=16,'narrow'=2] {'narrow'}, dimensions={0}, use_global_device_ids=true | all-gather | bytes 995328 | tf_op jit(solution)/shard_map/all_gather | solution.py:277
  688.1 3.5 reshape.289
  691.6 4.0 copy.105
  695.5 4.5 reshape.281
  700.0 61.5 %reduce-scatter.20.cloned.1.call-done = bf16[144,1152]{1,0:T(8,128)(2,1)} async-done(((bf16[2304,1152]{1,0:T(8,128)(2,1)}), bf16[144,1152]{1,0:T(8,128)(2,1)}) %reduce-scatter.20.cloned.1.call-update) | async-done | bytes 331792 | tf_op jit(solution)/shard_map/reduce_scatter | solution.py:274
  761.5 9.0 %all-gather.5 = bf16[288,1152]{1,0:T(8,128)(2,1)S(1)} all-gather(bf16[144,1152]{1,0:T(8,128)(2,1)} %reduce-scatter.20.cloned.1.call-done), channel_id=7, replica_groups=mesh['wide'=16,'narrow'=2] {'narrow'}, dimensions={0}, use_global_device_ids=true | all-gather | bytes 995328 | tf_op jit(solution)/shard_map/all_gather | solution.py:277
  771.7 64.8 %reduce-scatter.16.cloned.1.call-done = bf16[72,1728]{1,0:T(8,128)(2,1)} async-done(((bf16[1152,1728]{1,0:T(8,128)(2,1)}), bf16[72,1728]{1,0:T(8,128)(2,1)}) %reduce-scatter.16.cloned.1.call-update) | async-done | bytes 248848 | tf_op jit(solution)/shard_map/reduce_scatter | solution.py:274
  836.5 7.7 all-gather.2
  844.8 1.8 copy.104
  846.7 2.9 reshape.279
  (219 shorter events, 35.6 us)
Async XLA Ops:
  7.2 25.2 %copy-start = (bf16[72,6912]{1,0:T(8,128)(2,1)S(1)}, bf16[72,6912]{1,0:T(8,128)(2,1)}, u32[]{:S(2)}) copy-start(bf16[72,6912]{1,0:T(8,128)(2,1)} %param.19) | copy-start | bytes 2985988
  7.2 26.5 %copy-start.33 = (u32[32]{0:T(128)S(1)}, u32[32]{0:T(128)}, u32[]{:S(2)}) copy-start(u32[32]{0:T(128)} %constant.100) | copy-start | bytes 388
  7.2 27.8 %copy-start.34 = (bf16[432]{0:T(512)(128)(2,1)S(1)}, bf16[432]{0:T(512)(128)(2,1)}, u32[]{:S(2)}) copy-start(bf16[432]{0:T(512)(128)(2,1)} %param.20) | copy-start | bytes 2596
  7.2 27.8 %copy-start.36 = (bf16[144]{0:T(256)(128)(2,1)S(1)}, bf16[144]{0:T(256)(128)(2,1)}, u32[]{:S(2)}) copy-start(bf16[144]{0:T(256)(128)(2,1)} %param.22) | copy-start | bytes 868
  7.2 27.8 %copy-start.37 = (bf16[72]{0:T(256)(128)(2,1)S(1)}, bf16[72]{0:T(256)(128)(2,1)}, u32[]{:S(2)}) copy-start(bf16[72]{0:T(256)(128)(2,1)} %param.24) | copy-start | bytes 436
  7.2 27.8 %copy-start.35 = (bf16[288]{0:T(512)(128)(2,1)S(1)}, bf16[288]{0:T(512)(128)(2,1)}, u32[]{:S(2)}) copy-start(bf16[288]{0:T(512)(128)(2,1)} %param.26) | copy-start | bytes 1732
  7.2 27.8 %copy-start.38 = (bf16[72]{0:T(256)(128)(2,1)S(1)}, bf16[72]{0:T(256)(128)(2,1)}, u32[]{:S(2)}) copy-start(bf16[72]{0:T(256)(128)(2,1)} %param.28) | copy-start | bytes 436
  7.3 86.2 %copy-start.3 = (bf16[2,128,1152]{2,1,0:T(8,128)(2,1)S(1)}, bf16[2,128,1152]{2,1,0:T(8,128)(2,1)}, u32[]{:S(2)}) copy-start(bf16[2,128,1152]{2,1,0:T(8,128)(2,1)} %param.15) | copy-start | bytes 1769476
  7.3 116.8 %all-reduce.7.cloned.1.call-start = ((), (), s32[]{:S(2)}) async-start(), calls=%async_computation.23 | async-start | bytes 1769472
  8.2 0.8 copy-start.16
  8.3 0.8 copy-start.18
  33.7 93.1 %copy-start.14 = (bf16[72,3456]{1,0:T(8,128)(2,1)S(1)}, bf16[72,3456]{1,0:T(8,128)(2,1)}, u32[]{:S(2)}) copy-start(bf16[72,3456]{1,0:T(8,128)(2,1)} %param.21) | copy-start | bytes 1492996
  33.7 115.0 %all-gather.16.cloned.1.call-start = ((), (), s32[]{:S(2)}) async-start(), calls=%async_computation.10 | async-start | bytes 1769472 | tf_op jit(solution)/shard_map/all_gather | solution.py:140
  94.7 34.5 %copy-start.27 = (f32[2,128]{1,0:T(2,128)}, f32[2,128]{1,0:T(2,128)S(1)}, u32[]{:S(2)}) copy-start(f32[2,128]{1,0:T(2,128)S(1)} %add_rsqrt_fusion.1) | copy-start | bytes 3076
  126.8 75.1 %all-gather.18.cloned.1.call-start = ((), (), s32[]{:S(2)}) async-start(), calls=%async_computation.11 | async-start | bytes 4386816 | tf_op jit(solution)/shard_map/all_gather | solution.py:65
  130.2 115.5 %all-gather.20.cloned.1.call-start = ((), (), s32[]{:S(2)}) async-start(), calls=%async_computation.12 | async-start | bytes 2820096 | tf_op jit(solution)/shard_map/all_gather | solution.py:65
  208.2 3.2 copy-start.6
  208.4 3.0 copy-start.4
  211.4 2.0 copy-start.1
  216.0 13.6 %all-to-all-start = ((bf16[2,256,576]{2,0,1:T(2,128)(2,1)}), bf16[2,256,576]{2,0,1:T(2,128)(2,1)S(1)}, u32[]{:S(2)}, u32[]{:S(2)}) async-start(bf16[2,256,576]{2,0,1:T(2,128)(2,1)} %copy.87), calls=%async_computation | async-start | bytes 1310720 | tf_op jit(solution)/shard_map/all_to_all | solution.py:176
  219.6 52.9 %all-gather.22.cloned.1.call-start = ((), (), s32[]{:S(2)}) async-start(), calls=%async_computation.13 | async-start | bytes 1769472 | tf_op jit(solution)/shard_map/all_gather | solution.py:140
  248.7 1.0 copy-start.8
  248.7 1.0 copy-start.20
  249.0 7.7 copy-start.24
  249.7 6.9 copy-start.29
  250.9 80.6 %all-gather.24.cloned.1.call-start = ((), (), s32[]{:S(2)}) async-start(), calls=%async_computation.14 | async-start | bytes 5640192 | tf_op jit(solution)/shard_map/all_gather | solution.py:65
  265.1 89.9 %all-gather.26.cloned.1.call-start = ((), (), s32[]{:S(2)}) async-start(), calls=%async_computation.16 | async-start | bytes 1769472 | tf_op jit(solution)/shard_map/all_gather | solution.py:140
  265.8 4.6 copy-start.32
  268.5 145.6 %all-gather.28.cloned.1.call-start = ((), (), s32[]{:S(2)}) async-start(), calls=%async_computation.22 | async-start | bytes 5640192 | tf_op jit(solution)/shard_map/all_gather | solution.py:65
  270.3 177.1 %reduce-scatter.12.cloned.1.call-start = ((), (), s32[]{:S(2)}) async-start(), calls=%async_computation.17 | async-start | bytes 1769472 | tf_op jit(solution)/shard_map/reduce_scatter | solution.py:145
  414.1 8.6 copy-start.39
  422.7 4.3 copy-start.45
  427.0 9.2 %copy-start.23 = (f32[16,72]{1,0:T(8,128)S(1)}, f32[16,72]{1,0:T(8,128)}, u32[]{:S(2)}) copy-start(f32[16,72]{1,0:T(8,128)} %get-tuple-element.44) | copy-start | bytes 13828
  427.0 20.5 %copy-start.25 = (f32[2,128]{1,0:T(2,128)S(1)}, f32[2,128]{1,0:T(2,128)}, u32[]{:S(2)}) copy-start(f32[2,128]{1,0:T(2,128)} %copy-done.24) | copy-start | bytes 3076
  427.0 20.5 %copy-start.30 = (f32[2,128]{1,0:T(2,128)S(1)}, f32[2,128]{1,0:T(2,128)}, u32[]{:S(2)}) copy-start(f32[2,128]{1,0:T(2,128)} %copy-done.29) | copy-start | bytes 3076
  427.0 45.0 %reduce-scatter.10.cloned.1.call-start = ((), (), s32[]{:S(2)}) async-start(), calls=%async_computation.15 | async-start | bytes 1769472 | tf_op jit(solution)/shard_map/reduce_scatter | solution.py:145
  436.1 160.6 %reduce-scatter.14.cloned.1.call-start = ((), (), s32[]{:S(2)}) async-start(), calls=%async_computation.18 | async-start | bytes 1769472 | tf_op jit(solution)/shard_map/reduce_scatter | solution.py:145
  472.0 4.4 copy-start.41
  476.4 1.0 copy-start.12
  490.7 3.5 copy-start.2
  495.3 1.1 copy-start.7
  496.4 1.1 copy-start.5
  500.1 2.2 copy-start.40
  502.3 3.6 copy-start.15
  502.3 3.7 copy-start.11
  502.3 3.7 copy-start.13
  505.9 134.3 %reduce-scatter.22.cloned.1.call-start = ((), (), s32[]{:S(2)}) async-start(), calls=%async_computation.24 | async-start | bytes 2820096
  508.4 1.3 copy-start.43
  508.4 170.6 %reduce-scatter.18.cloned.1.call-start = ((), (), s32[]{:S(2)}) async-start(), calls=%async_computation.20 | async-start | bytes 5640192 | tf_op jit(solution)/shard_map/reduce_scatter | solution.py:274
  516.6 1.3 copy-start.44
  516.6 244.9 %reduce-scatter.20.cloned.1.call-start = ((), (), s32[]{:S(2)}) async-start(), calls=%async_computation.21 | async-start | bytes 5640192 | tf_op jit(solution)/shard_map/reduce_scatter | solution.py:274
  526.3 1.3 copy-start.42
  526.3 310.2 %reduce-scatter.16.cloned.1.call-start = ((), (), s32[]{:S(2)}) async-start(), calls=%async_computation.19 | async-start | bytes 4386816 | tf_op jit(solution)/shard_map/reduce_scatter | solution.py:274
  533.5 0.7 copy-start.21
  533.5 0.8 copy-start.31
  533.5 1.1 copy-start.22
  533.5 63.2 %copy-start.28 = (f32[2,128]{1,0:T(2,128)S(1)}, f32[2,128]{1,0:T(2,128)}, u32[]{:S(2)}) copy-start(f32[2,128]{1,0:T(2,128)} %copy-done.27) | copy-start | bytes 3076
  533.5 65.1 %copy-start.9 = (f32[256,1152]{1,0:T(8,128)S(1)}, f32[256,1152]{1,0:T(8,128)}, u32[]{:S(2)}) copy-start(f32[256,1152]{1,0:T(8,128)} %copy-done.8) | copy-start | bytes 3538948
  596.7 1.9 copy-start.10
  627.9 11.6 %copy-start.17 = (f32[2,576]{1,0:T(2,128)S(1)}, f32[2,576]{1,0:T(2,128)}, u32[]{:S(2)}) copy-start(f32[2,576]{1,0:T(2,128)} %copy-done.16) | copy-start | bytes 13828
  627.9 11.6 %copy-start.19 = (f32[2,576]{1,0:T(2,128)S(1)}, f32[2,576]{1,0:T(2,128)}, u32[]{:S(2)}) copy-start(f32[2,576]{1,0:T(2,128)} %copy-done.18) | copy-start | bytes 13828
  627.9 11.6 %copy-start.26 = (bf16[2,1152]{1,0:T(2,128)(2,1)S(1)}, bf16[2,1152]{1,0:T(2,128)(2,1)}, u32[]{:S(2)}) copy-start(bf16[2,1152]{1,0:T(2,128)(2,1)} %param.16) | copy-start | bytes 13828
  628.9 10.5 %all-to-all-start.2 = ((f32[16,2,72]{2,1,0:T(2,128)}), f32[16,2,72]{2,1,0:T(2,128)S(1)}, u32[]{:S(2)}, u32[]{:S(2)}) async-start(f32[16,2,72]{2,1,0:T(2,128)} %bitcast.25), calls=%async_computation.5 | async-start | bytes 32768 | tf_op jit(solution)/shard_map/all_to_all | solution.py:270
Sparse Core Ops, SparseCore 0:
  33.8 90.1 all-reduce.6
  126.9 21.7 all-gather.15
  151.5 50.2 all-gather.17
  203.9 41.7 all-gather.19
  251.0 21.4 all-gather.21
  275.1 56.3 all-gather.23
  333.6 21.3 all-gather.25
  357.7 56.3 all-gather.27
  427.1 20.3 reduce-scatter.11
  450.2 21.7 reduce-scatter.9
  506.0 21.7 reduce-scatter.13
  532.1 64.0 reduce-scatter.21
  600.3 78.7 reduce-scatter.17
  682.9 78.5 reduce-scatter.19
  765.3 71.1 reduce-scatter.15

commit v2 on v1

--- a/solution.py
+++ b/solution.py
@@ -3,6 +3,8 @@
 import jax
 import jax.numpy as jnp
 from jax import lax
+from jax.experimental import pallas as pl
+from jax.experimental.pallas import tpu as pltpu
 from jax.sharding import PartitionSpec as P
 
 HEADS = 16
@@ -300,6 +302,1010 @@
     )
 
 
+MESH = pl.DeviceIdType.MESH
+NZ = 4
+GELU_C = 0.7978845608028654
+HBM_SPEC = pl.BlockSpec(memory_space=pl.ANY)
+VMEM_SPEC = pl.BlockSpec(memory_space=pltpu.VMEM)
+VMEM_LIMIT = 63 << 20
+
+
+def dot_nn(a, b):
+    return lax.dot_general(a, b, (((1,), (0,)), ((), ())), preferred_element_type=F32)
+
+
+def dot_nt(a, b):
+    return lax.dot_general(a, b, (((1,), (1,)), ((), ())), preferred_element_type=F32)
+
+
+def dot_tn(a, b):
+    return lax.dot_general(a, b, (((0,), (0,)), ((), ())), preferred_element_type=F32)
+
+
+def do_when(cond, fn):
+    if cond is True:
+        fn()
+    else:
+        pl.when(cond)(fn)
+
+
+def both(a, b):
+    if a is True:
+        return b
+    if b is True:
+        return a
+    return jnp.logical_and(a, b)
+
+
+def greet(peers):
+    barrier = pltpu.get_barrier_semaphore()
+    total = 0
+    for cond, dev in peers:
+        do_when(
+            cond,
+            lambda dev=dev: pl.semaphore_signal(
+                barrier, inc=1, device_id=dev, device_id_type=MESH
+            ),
+        )
+        total = total + (1 if cond is True else cond.astype(jnp.int32))
+    pl.semaphore_wait(barrier, total)
+
+
+def plane_exchange(source, target, send, recv, base, n_wide, w, y):
+    copies = []
+    for k in range(1, n_wide):
+        peer = lax.rem(w + k, n_wide)
+        copy = pltpu.make_async_remote_copy(
+            src_ref=source(peer),
+            dst_ref=target.at[w],
+            send_sem=send.at[base + k],
+            recv_sem=recv.at[base + k],
+            device_id=(peer, y),
+            device_id_type=MESH,
+        )
+        copy.start()
+        copies.append(copy)
+
+    def finish():
+        for copy in copies:
+            copy.wait_recv()
+        for copy in copies:
+            copy.wait_send()
+
+    return finish
+
+
+def swap(source, target, send, recv, index, dev):
+    copy = pltpu.make_async_remote_copy(
+        src_ref=source,
+        dst_ref=target,
+        send_sem=send.at[index],
+        recv_sem=recv.at[index],
+        device_id=dev,
+        device_id_type=MESH,
+    )
+    copy.start()
+    return copy
+
+
+def plane_peers(n_wide, w, y):
+    peers = [(True, (lax.rem(w + k, n_wide), y)) for k in range(1, n_wide)]
+    return peers + [(True, (w, 1 - y))]
+
+
+def head_kernel(parcel_ref, wada_ref, got_ref, mod_ref, left, part, parts, tot, send, recv):
+    n_wide = parcel_ref.shape[0]
+    shard = wada_ref.shape[0]
+    half = mod_ref.shape[2]
+    w, y = lax.axis_index("wide"), lax.axis_index("narrow")
+    greet(plane_peers(n_wide, w, y))
+    wait = plane_exchange(lambda p: parcel_ref.at[p], got_ref, send, recv, 0, n_wide, w, y)
+    got_ref[w] = parcel_ref[w]
+    wait()
+    for s in range(n_wide):
+        left[2 * s : 2 * s + 2, :] = got_ref[s, 0:2, 0:128]
+    lhs = left[...][:, :shard].astype(BF16)
+    cols = pl.ds(pl.multiple_of(y * half, 128), half)
+    res = dot_nn(lhs, wada_ref[:, cols])
+    for s in range(n_wide):
+        part[s] = res[2 * s : 2 * s + 2, :]
+    wait = plane_exchange(lambda p: part.at[p], parts, send, recv, n_wide, n_wide, w, y)
+    parts[w] = part[w]
+    wait()
+    total = parts[0]
+    for s in range(1, n_wide):
+        total = total + parts[s]
+    tot[...] = total
+    mod_ref[y] = total
+    copy = swap(tot, mod_ref.at[y], send, recv, 0, (w, 1 - y))
+    copy.wait()
+
+
+def tail_kernel(
+    dmod_ref, v_ref, silu_ref, wada_ref,
+    ada_ref, bsum_ref, vout_ref, dsil_ref,
+    dm_pair, dm_low, dm_all, v_all, v_half, v_pair, dm_rows, ds_send, send, recv,
+):
+    n_wide = v_ref.shape[0]
+    shard = wada_ref.shape[0]
+    w, y = lax.axis_index("wide"), lax.axis_index("narrow")
+    greet(plane_peers(n_wide, w, y))
+    copy = swap(dmod_ref, dm_pair, send, recv, 0, (w, 1 - y))
+    wait_v = plane_exchange(lambda p: v_ref.at[p], v_all, send, recv, n_wide, n_wide, w, y)
+    v_all[w] = v_ref[w]
+    copy.wait()
+    dm_low[...] = (dmod_ref[...] + dm_pair[...]).astype(BF16)
+    wait_dm = plane_exchange(lambda p: dm_low, dm_all, send, recv, 2 * n_wide, n_wide, w, y)
+    dm_all[w] = dm_low[...]
+    wait_v()
+    total = v_all[0]
+    for s in range(1, n_wide):
+        total = total + v_all[s]
+    v_half[...] = total
+    copy = swap(v_half, v_pair, send, recv, n_wide, (w, 1 - y))
+    wait_dm()
+    for s in range(n_wide):
+        dm_rows[2 * s : 2 * s + 2, :] = dm_all[s].astype(F32)
+    dm32 = dm_rows[...]
+    dmb = dm32.astype(BF16)
+    res = dot_nt(dmb, wada_ref[...])
+    for s in range(n_wide):
+        ds_send[s, :, 0:shard] = res[2 * s : 2 * s + 2, :]
+    wait_ds = plane_exchange(lambda p: ds_send.at[p], dsil_ref, send, recv, 3 * n_wide, n_wide, w, y)
+    dsil_ref[w] = ds_send[w]
+    bsum_ref[...] = jnp.sum(dm32, axis=0, keepdims=True)
+    ada_ref[...] = dot_tn(silu_ref[...], dmb)
+    copy.wait()
+    vout_ref[...] = v_half[...] + v_pair[...]
+    wait_ds()
+
+
+class Sems:
+    def __init__(self, send, recv):
+        self.send, self.recv, self.n = send, recv, 0
+
+    def take(self, count):
+        at = self.n
+        self.n += count
+        return at
+
+
+class Links:
+    def __init__(self, sems):
+        self.sems = sems
+        self.sent = []
+
+    def copy(self, src, dst, index, dev):
+        return pltpu.make_async_remote_copy(
+            src_ref=src,
+            dst_ref=dst,
+            send_sem=self.sems.send.at[index],
+            recv_sem=self.sems.recv.at[index],
+            device_id=dev,
+            device_id_type=MESH,
+        )
+
+    def start(self, cond, src, dst, send_index, recv_index, dev):
+        copy = pltpu.make_async_remote_copy(
+            src_ref=src,
+            dst_ref=dst,
+            send_sem=self.sems.send.at[send_index],
+            recv_sem=self.sems.recv.at[recv_index],
+            device_id=dev,
+            device_id_type=MESH,
+        )
+        do_when(cond, copy.start)
+        self.sent.append((cond, copy))
+        return copy
+
+    def arrived(self, cond, ref, index, dev):
+        copy = self.copy(ref, ref, index, dev)
+        do_when(cond, copy.wait_recv)
+
+    def left(self, copy):
+        copy.wait_send()
+        self.sent = [entry for entry in self.sent if entry[1] is not copy]
+
+    def drain(self):
+        for cond, copy in self.sent:
+            do_when(cond, copy.wait_send)
+        self.sent = []
+
+
+class Gather:
+    def __init__(self, links, pos, block, source, sink):
+        self.links, self.pos, self.block = links, pos, block
+        self.source, self.sink = source, sink
+        take = links.sems.take
+        self.z_at, self.x_at, self.up_at, self.down_at = take(4), take(4), take(4), take(4)
+
+    def forward(self, cond, s, up, down):
+        z, x, c, y = self.pos["z"], self.pos["x"], self.pos["c"], self.pos["y"]
+        ref = self.block(s, x)
+        if up:
+            self.links.start(
+                both(cond, z < NZ - 1), ref, ref, self.up_at + s, self.z_at + s,
+                self.pos["dev"](z + 1, x, c, y),
+            )
+        if down:
+            self.links.start(
+                both(cond, z > 0), ref, ref, self.down_at + s, self.z_at + s,
+                self.pos["dev"](z - 1, x, c, y),
+            )
+        self.links.start(
+            cond, ref, ref, self.x_at + s, self.x_at + s, self.pos["dev"](z, 1 - x, c, y)
+        )
+
+    def own(self):
+        self.forward(self.source, self.pos["z"], True, True)
+
+    def step(self, d):
+        z, x = self.pos["z"], self.pos["x"]
+        cond = both(self.source, z >= d)
+        s = jnp.maximum(z - d, 0)
+        self.links.arrived(cond, self.block(s, x), self.z_at + s, self.pos["me"])
+        self.forward(cond, s, True, False)
+        cond = both(self.source, z <= NZ - 1 - d)
+        s = jnp.minimum(z + d, NZ - 1)
+        self.links.arrived(cond, self.block(s, x), self.z_at + s, self.pos["me"])
+        self.forward(cond, s, False, True)
+
+    def finish(self):
+        x = self.pos["x"]
+        for s in range(NZ):
+            self.links.arrived(self.sink, self.block(s, 1 - x), self.x_at + s, self.pos["me"])
+
+
+class Scatter:
+    def __init__(self, links, pos, block, sums_x, sums_z, source, sink):
+        self.links, self.pos, self.block = links, pos, block
+        self.sums_x, self.sums_z = sums_x, sums_z
+        self.source, self.sink = source, sink
+        take = links.sems.take
+        self.x_at, self.z_at, self.up_at, self.down_at = take(4), take(5), take(4), take(4)
+
+    def begin(self):
+        z, x, c, y = self.pos["z"], self.pos["x"], self.pos["c"], self.pos["y"]
+        for s in (3, 0, 2, 1):
+            self.links.start(
+                self.source, self.block(s, 1 - x), self.sums_x.at[s], self.x_at + s,
+                self.x_at + s, self.pos["dev"](z, 1 - x, c, y),
+            )
+
+    def add_x(self, s):
+        self.links.arrived(True, self.sums_x.at[s], self.x_at + s, self.pos["me"])
+        return self.block(s, self.pos["x"])[...].astype(F32) + self.sums_x[s].astype(F32)
+
+    def hop(self, s, up):
+        z, x, c, y = self.pos["z"], self.pos["x"], self.pos["c"], self.pos["y"]
+        cond = both(self.sink, (z < s) if up else (z > s))
+
+        def run():
+            ref = self.block(s, x)
+            ref[...] = self.add_x(s).astype(BF16)
+            inner = (z > 0) if up else (z < NZ - 1)
+
+            @pl.when(inner)
+            def _():
+                self.links.arrived(True, self.sums_z.at[s], self.z_at + s, self.pos["me"])
+                ref[...] = (ref[...].astype(F32) + self.sums_z[s].astype(F32)).astype(BF16)
+
+        do_when(cond, run)
+        near = (z == s - 1) if up else (z == s + 1)
+        slot = s if up else jnp.where(near, 4, s)
+        to = self.pos["dev"](z + 1 if up else z - 1, x, c, y)
+        at = (self.up_at if up else self.down_at) + s
+        self.links.start(
+            cond, self.block(s, x), self.sums_z.at[slot], at, self.z_at + slot, to
+        )
+
+    def finish(self, store):
+        z, x = self.pos["z"], self.pos["x"]
+        keep = self.block(z, x)
+
+        def run():
+            total = keep[...].astype(F32)
+            self.links.arrived(True, self.sums_x.at[z], self.x_at + z, self.pos["me"])
+            total = total + self.sums_x[z].astype(F32)
+            keep[...] = total.astype(BF16)
+
+            @pl.when(z > 0)
+            def _():
+                self.links.arrived(True, self.sums_z.at[z], self.z_at + z, self.pos["me"])
+                keep[...] = (keep[...].astype(F32) + self.sums_z[z].astype(F32)).astype(BF16)
+
+            @pl.when(z < NZ - 1)
+            def _():
+                self.links.arrived(True, self.sums_z.at[4], self.z_at + 4, self.pos["me"])
+                keep[...] = (keep[...].astype(F32) + self.sums_z[4].astype(F32)).astype(BF16)
+
+            store(keep)
+
+        do_when(self.sink, run)
+
+    def hops(self):
+        out = []
+        for k in range(3):
+            out.append(lambda k=k: self.hop(3 - k, True))
+            out.append(lambda k=k: self.hop(k, False))
+        return out
+
+
+class GroupGather:
+    def __init__(self, links, pos, full):
+        self.links, self.pos, self.full = links, pos, full
+        self.at = links.sems.take(3)
+
+    def begin(self):
+        z, x, c, y = self.pos["z"], self.pos["x"], self.pos["c"], self.pos["y"]
+        ref = self.full.at[pl.ds(2 * c, 2), y]
+        self.links.start(True, ref, ref, self.at, self.at, self.pos["dev"](z, x, c, 1 - y))
+        self.links.start(True, ref, ref, self.at + 1, self.at + 1, self.pos["dev"](z, x, 1 - c, y))
+
+    def relay(self):
+        z, x, c, y = self.pos["z"], self.pos["x"], self.pos["c"], self.pos["y"]
+        ref = self.full.at[pl.ds(2 * c, 2), 1 - y]
+        self.links.arrived(True, ref, self.at, self.pos["me"])
+        self.links.start(True, ref, ref, self.at + 2, self.at + 2, self.pos["dev"](z, x, 1 - c, y))
+
+    def finish(self):
+        c, y = self.pos["c"], self.pos["y"]
+        other = pl.ds(2 * (1 - c), 2)
+        self.links.arrived(True, self.full.at[other, y], self.at + 1, self.pos["me"])
+        self.links.arrived(True, self.full.at[other, 1 - y], self.at + 2, self.pos["me"])
+
+
+class GroupSum:
+    def __init__(self, links, pos, full, from_core, to_pair, from_pair):
+        self.links, self.pos, self.full = links, pos, full
+        self.from_core, self.to_pair, self.from_pair = from_core, to_pair, from_pair
+        self.at = links.sems.take(2)
+
+    def begin(self):
+        z, x, c, y = self.pos["z"], self.pos["x"], self.pos["c"], self.pos["y"]
+        self.core_copy = self.links.start(
+            True, self.full.at[pl.ds(2 * (1 - c), 2)], self.from_core, self.at, self.at,
+            self.pos["dev"](z, x, 1 - c, y),
+        )
+
+    def relay(self):
+        z, x, c, y = self.pos["z"], self.pos["x"], self.pos["c"], self.pos["y"]
+        self.links.arrived(True, self.from_core, self.at, self.pos["me"])
+        for s in range(2):
+            self.to_pair[s] = (
+                self.full[2 * c + s, 1 - y].astype(F32) + self.from_core[s, 1 - y].astype(F32)
+            ).astype(BF16)
+        self.pair_copy = self.links.start(
+            True, self.to_pair, self.from_pair, self.at + 1, self.at + 1,
+            self.pos["dev"](z, x, c, 1 - y),
+        )
+
+    def arrived(self):
+        self.links.arrived(True, self.from_pair, self.at + 1, self.pos["me"])
+
+    def total(self, s):
+        c, y = self.pos["c"], self.pos["y"]
+        return (
+            self.full[2 * c + s, y].astype(F32)
+            + self.from_core[s, y].astype(F32)
+            + self.from_pair[s].astype(F32)
+        )
+
+
+def gelu_both(u):
+    inner = GELU_C * (u + 0.044715 * u * u * u)
+    tan = jnp.tanh(inner)
+    slope = GELU_C * (1.0 + 3.0 * 0.044715 * u * u)
+    act = 0.5 * u * (1.0 + tan)
+    grad = 0.5 * (1.0 + tan) + 0.5 * u * (1.0 - tan * tan) * slope
+    return act, grad
+
+
+def block_kernel(
+    tok_ref, cot_ref, mod_ref, bqkv_ref, bproj_ref, bfc1_ref, bfc2_ref,
+    src_qkv, src_proj, src_fc1, src_fc2,
+    out_ref, gtok_ref, dmod_ref, bias_ref, j_qkv, j_fc1, j_fc2, j_proj,
+    g_qkv, g_proj, g_fc1, g_fc2,
+    i_qkv, i_fc1, i_fc2, own_qkv, own_fc1, own_fc2,
+    x_qkv, x_proj, x_fc1, x_fc2, z_qkv, z_proj, z_fc1, z_fc2,
+    t_qkv, t_fc1, t_fc2, t_proj,
+    a_all, m_all, d_all, da_all, qkv_all, att_all, act_all, gp_all, dqkv_all,
+    sum_a, sum_b, core_a, core_b, to_a, to_b, from_a, from_b,
+    attn_own, mid_own, dmid_own, mlp_own,
+    send, recv, local,
+):
+    w, y = lax.axis_index("wide"), lax.axis_index("narrow")
+    z, x, c = w // 4, (w // 2) % 2, w % 2
+    chip = 2 * z + x
+
+    def dev(z, x, c, y):
+        return ((z * 2 + x) * 2 + c, y)
+
+    pos = {"z": z, "x": x, "c": c, "y": y, "dev": dev, "me": dev(z, x, 1 - c, y)}
+    sems = Sems(send, recv)
+    links = Links(sems)
+    half_len = tok_ref.shape[1]
+    width = tok_ref.shape[2]
+    hw = HEAD_DIM * 4
+    shard = own_qkv.shape[0]
+    rows2 = 2 * shard
+    head_scale = 1.0 / math.sqrt(HEAD_DIM)
+
+    sib = dev(z, x, 1 - c, y)
+    greet(
+        [
+            (True, sib),
+            (True, dev(z, x, c, 1 - y)),
+            (True, dev(z, x, 1 - c, 1 - y)),
+            (True, dev(z, 1 - x, c, y)),
+            (z < NZ - 1, dev(z + 1, x, c, y)),
+            (z > 0, dev(z - 1, x, c, y)),
+        ]
+    )
+
+    init = sems.take(3)
+    pieces = (
+        (src_qkv, i_qkv, own_qkv, g_qkv),
+        (src_fc1, i_fc1, own_fc1, g_fc1),
+        (src_fc2, i_fc2, own_fc2, g_fc2),
+    )
+    locals_ = []
+    for k, (src, inbox, own, full) in enumerate(pieces):
+        links.start(True, src.at[2 * y + 1 - c], inbox, init + k, init + k, sib)
+        copy = pltpu.make_async_copy(src.at[2 * y + c], own, local.at[k])
+        copy.start()
+        locals_.append(copy)
+    proj_copy = pltpu.make_async_copy(src_proj, g_proj.at[z], local.at[3])
+    on_column = x == y
+    do_when(on_column, proj_copy.start)
+
+    def place_own(k):
+        src, inbox, own, full = pieces[k]
+        locals_[k].wait()
+        links.arrived(True, inbox, init + k, sib)
+        mine, other = own[...].astype(F32), inbox[...].astype(F32)
+        first = jnp.where(c == 0, mine, other)
+        second = jnp.where(c == 0, other, mine)
+        at = pl.ds(pl.multiple_of(chip * rows2, 16), rows2)
+        full[at, :] = jnp.concatenate([first, second], axis=0).astype(BF16)
+
+    def rows_of(full):
+        return lambda s, xx: full.at[pl.ds(pl.multiple_of((2 * s + xx) * rows2, 16), rows2), :]
+
+    def head_of(s, xx):
+        return g_proj.at[s]
+
+    not_column = jnp.logical_not(on_column)
+    ga_qkv = Gather(links, pos, rows_of(g_qkv), True, True)
+    ga_proj = Gather(links, pos, head_of, on_column, not_column)
+    ga_fc1 = Gather(links, pos, rows_of(g_fc1), True, True)
+    ga_fc2 = Gather(links, pos, rows_of(g_fc2), True, True)
+
+    def mod(k, s):
+        return mod_ref[s, k : k + 1, :]
+
+    def norm(value):
+        center = value - jnp.mean(value, axis=-1, keepdims=True)
+        inv = lax.rsqrt(jnp.mean(center * center, axis=-1, keepdims=True) + eps_norm)
+        return center * inv, inv
+
+    def norm_grad(grad, normed, inv):
+        return inv * (
+            grad
+            - jnp.mean(grad, axis=-1, keepdims=True)
+            - normed * jnp.mean(grad * normed, axis=-1, keepdims=True)
+        )
+
+    place_own(0)
+    ga_qkv.own()
+    for s in range(2):
+        normed, inv = norm(tok_ref[s].astype(F32))
+        a_all[2 * c + s, y] = (normed * (1.0 + mod(1, s)) + mod(0, s)).astype(BF16)
+    gg_a = GroupGather(links, pos, a_all)
+    gg_a.begin()
+    do_when(on_column, proj_copy.wait)
+    ga_proj.own()
+    for s in range(2):
+        d_all[2 * c + s, y] = (mod(5, s) * cot_ref[s].astype(F32)).astype(BF16)
+    ga_qkv.step(1)
+    place_own(1)
+    ga_fc1.own()
+    gg_a.relay()
+    ga_qkv.step(2)
+    gg_d = GroupGather(links, pos, d_all)
+    gg_d.begin()
+    ga_qkv.step(3)
+    place_own(2)
+    ga_proj.step(1)
+    ga_fc1.step(1)
+    ga_fc2.own()
+    ga_proj.step(2)
+    ga_proj.step(3)
+    gg_d.relay()
+    gg_a.finish()
+    ga_qkv.finish()
+
+    rows = 2 * half_len
+
+    @pl.loop(0, 4)
+    def _(i):
+        res = dot_nn(a_all[i].reshape(rows, width), g_qkv[...]) + bqkv_ref[...]
+        qkv_all[i] = res.astype(BF16)
+
+    ga_fc1.step(2)
+    ga_fc1.step(3)
+    ga_fc2.step(1)
+    ga_proj.finish()
+
+    def head_parts(packed, h):
+        return [packed[:, t * hw + h * HEAD_DIM : t * hw + (h + 1) * HEAD_DIM] for t in range(3)]
+
+    def softmax(q, k):
+        scores = dot_nt(q, k) * head_scale
+        top = jnp.max(scores, axis=-1, keepdims=True)
+        e = jnp.exp(scores - top)
+        return e * (1.0 / jnp.sum(e, axis=-1, keepdims=True))
+
+    @pl.loop(0, 4)
+    def _(i):
+        packed = qkv_all[i]
+        acc = None
+        for h in range(4):
+            q, k, v = head_parts(packed, h)
+            p = softmax(q, k).astype(BF16)
+            o = dot_nn(p, v).astype(BF16)
+            att_all[h, i] = o
+            term = dot_nn(o, g_proj[h])
+            acc = term if acc is None else acc + term
+        sum_a[i] = acc.astype(BF16).reshape(2, half_len, width)
+
+    gs_attn = GroupSum(links, pos, sum_a, core_a, to_a, from_a)
+    gs_attn.begin()
+    ga_fc2.step(2)
+    gs_attn.relay()
+    ga_fc2.step(3)
+    gs_attn.arrived()
+    for s in range(2):
+        attn = gs_attn.total(s) + bproj_ref[...]
+        attn_own[s] = attn
+        mid = tok_ref[s].astype(F32) + mod(2, s) * attn
+        mid_own[s] = mid
+        normed, inv = norm(mid)
+        m_all[2 * c + s, y] = (normed * (1.0 + mod(4, s)) + mod(3, s)).astype(BF16)
+    gg_m = GroupGather(links, pos, m_all)
+    gg_m.begin()
+    gg_d.finish()
+    ga_fc1.finish()
+    gg_m.relay()
+    gg_m.finish()
+
+    @pl.loop(0, 4)
+    def _(i):
+        u = dot_nn(m_all[i].reshape(rows, width), g_fc1[...]) + bfc1_ref[...]
+        act, grad = gelu_both(u)
+        act_all[i] = act.astype(BF16)
+        gp_all[i] = grad.astype(BF16)
+
+    ga_fc2.finish()
+
+    @pl.loop(0, 4)
+    def _(i):
+        res = dot_nn(act_all[i], g_fc2[...])
+        sum_b[i] = res.astype(BF16).reshape(2, half_len, width)
+
+    gs_mlp = GroupSum(links, pos, sum_b, core_b, to_b, from_b)
+    gs_mlp.begin()
+
+    bias_ref[...] = jnp.zeros_like(bias_ref)
+
+    def d_hidden_of(i):
+        d_act = dot_nt(d_all[i].reshape(rows, width), g_fc2[...])
+        d_hidden = (d_act * gp_all[i].astype(F32)).astype(BF16)
+        gp_all[i] = d_hidden
+        bias_ref[0:1, :] += jnp.sum(d_hidden.astype(F32), axis=0, keepdims=True)
+
+    pl.loop(0, 4)(d_hidden_of)
+    links.drain()
+    gs_mlp.relay()
+
+    @pl.loop(0, 4)
+    def _(i):
+        res = dot_nt(gp_all[i], g_fc1[...])
+        sum_a[i] = res.astype(BF16).reshape(2, half_len, width)
+
+    gs_dm = GroupSum(links, pos, sum_a, core_a, to_a, from_a)
+    gs_dm.begin()
+
+    def outer(left, right, full, lanes):
+        @pl.loop(0, width // lanes)
+        def _(j):
+            at = pl.ds(pl.multiple_of(j * lanes, 128), lanes)
+            res = dot_tn(left(at), right())
+            full[at, :] = res.astype(BF16)
+
+    all_rows = 4 * rows
+    lanes = width // 3
+    outer(
+        lambda at: act_all[:, :, at].reshape(all_rows, lanes),
+        lambda: d_all[...].reshape(all_rows, width),
+        g_fc2,
+        lanes,
+    )
+    sc_fc2 = Scatter(links, pos, rows_of(g_fc2), x_fc2, z_fc2, True, True)
+    sc_fc2.begin()
+    gs_dm.relay()
+    outer(
+        lambda at: m_all[:, :, :, at].reshape(all_rows, lanes),
+        lambda: gp_all[...].reshape(all_rows, width),
+        g_fc1,
+        lanes,
+    )
+    sc_fc1 = Scatter(links, pos, rows_of(g_fc1), x_fc1, z_fc1, True, True)
+    sc_fc1.begin()
+    gs_mlp.arrived()
+    for s in range(2):
+        mlp = gs_mlp.total(s) + bfc2_ref[...]
+        mid = mid_own[s]
+        out_ref[s] = (mid + mod(5, s) * mlp).astype(BF16)
+        grad_out = cot_ref[s].astype(F32)
+        dmod_ref[5, s : s + 1, :] = jnp.sum(grad_out * mlp, axis=0, keepdims=True)
+        bias_ref[2:3, :] += jnp.sum(
+            d_all[2 * c + s, y].astype(F32), axis=0, keepdims=True
+        )
+    gs_dm.arrived()
+    for s in range(2):
+        d_m = gs_dm.total(s)
+        normed, inv = norm(mid_own[s])
+        dmod_ref[4, s : s + 1, :] = jnp.sum(d_m * normed, axis=0, keepdims=True)
+        dmod_ref[3, s : s + 1, :] = jnp.sum(d_m, axis=0, keepdims=True)
+        d_mid = cot_ref[s].astype(F32) + norm_grad(d_m * (1.0 + mod(4, s)), normed, inv)
+        dmid_own[s] = d_mid
+        d_attn = (mod(2, s) * d_mid).astype(BF16)
+        da_all[2 * c + s, y] = d_attn
+        dmod_ref[2, s : s + 1, :] = jnp.sum(d_mid * attn_own[s], axis=0, keepdims=True)
+        bias_ref[1:2, :] += jnp.sum(d_attn.astype(F32), axis=0, keepdims=True)
+    gg_da = GroupGather(links, pos, da_all)
+    gg_da.begin()
+    h_fc2, h_fc1 = sc_fc2.hops(), sc_fc1.hops()
+    h_fc2[0]()
+    h_fc2[1]()
+    gg_da.relay()
+    h_fc2[2]()
+    h_fc2[3]()
+    gg_da.finish()
+
+    @pl.loop(0, 4)
+    def _(i):
+        packed = qkv_all[i]
+        d_attn = da_all[i].reshape(rows, width)
+        grads = [[], [], []]
+        for h in range(4):
+            q, k, v = head_parts(packed, h)
+            p = softmax(q, k)
+            p_low = p.astype(BF16)
+            d_att = dot_nt(d_attn, g_proj[h]).astype(BF16)
+            d_p = dot_nt(d_att, v)
+            d_s = (p * (d_p - jnp.sum(p * d_p, axis=-1, keepdims=True))).astype(BF16)
+            grads[0].append(dot_nn(d_s, k) * head_scale)
+            grads[1].append(dot_tn(d_s, q) * head_scale)
+            grads[2].append(dot_tn(p_low, d_att))
+        d_qkv = jnp.concatenate(grads[0] + grads[1] + grads[2], axis=1).astype(BF16)
+        dqkv_all[i] = d_qkv
+        bias_ref[3:4, 0 : 3 * hw] += jnp.sum(d_qkv.astype(F32), axis=0, keepdims=True)
+
+    h_fc2[4]()
+    h_fc2[5]()
+
+    @pl.loop(0, 4)
+    def _(i):
+        res = dot_nt(dqkv_all[i], g_qkv[...])
+        sum_b[i] = res.astype(BF16).reshape(2, half_len, width)
+
+    gs_da = GroupSum(links, pos, sum_b, core_b, to_b, from_b)
+    gs_da.begin()
+    h_fc1[0]()
+    h_fc1[1]()
+    outer(
+        lambda at: a_all[:, :, :, at].reshape(all_rows, lanes),
+        lambda: dqkv_all[...].reshape(all_rows, 3 * hw),
+        g_qkv,
+        lanes,
+    )
+    sc_qkv = Scatter(links, pos, rows_of(g_qkv), x_qkv, z_qkv, True, True)
+    sc_qkv.begin()
+    links.left(gs_mlp.pair_copy)
+    gs_da.relay()
+
+    @pl.loop(0, 4)
+    def _(h):
+        left = att_all[h].reshape(all_rows, HEAD_DIM)
+        g_proj[h] = dot_tn(left, da_all[...].reshape(all_rows, width)).astype(BF16)
+
+    sc_proj = Scatter(links, pos, head_of, x_proj, z_proj, not_column, on_column)
+    sc_proj.begin()
+    h_fc1[2]()
+    h_fc1[3]()
+    h_fc1[4]()
+    h_fc1[5]()
+
+    joins = []
+
+    def join(scatter, pack, target):
+        at = sems.take(4)
+
+        def store(keep):
+            total = keep[...].astype(F32)
+            pack[0] = total[:shard].astype(BF16)
+            pack[1] = total[shard:].astype(BF16)
+
+        scatter.finish(store)
+        q = 2 * y + c
+        links.start(True, pack.at[1 - c], target.at[q], at, at, dev(z, x, 1 - c, y))
+        links.start(True, pack.at[c], target.at[q], at + 1, at + 1, dev(z, x, c, 1 - y))
+        links.start(True, pack.at[1 - c], target.at[q], at + 2, at + 2, dev(z, x, 1 - c, 1 - y))
+        keep_copy = pltpu.make_async_copy(pack.at[c], target.at[q], local.at[len(joins)])
+        keep_copy.start()
+
+        def done():
+            keep_copy.wait()
+            links.arrived(True, target.at[2 * y + 1 - c], at, sib)
+            links.arrived(True, target.at[2 * (1 - y) + c], at + 1, sib)
+            links.arrived(True, target.at[2 * (1 - y) + 1 - c], at + 2, sib)
+
+        joins.append(done)
+
+    join(sc_fc2, t_fc2, j_fc2)
+    h_qkv, h_proj = sc_qkv.hops(), sc_proj.hops()
+    gs_da.arrived()
+    for s in range(2):
+        d_a = gs_da.total(s)
+        normed, inv = norm(tok_ref[s].astype(F32))
+        dmod_ref[1, s : s + 1, :] = jnp.sum(d_a * normed, axis=0, keepdims=True)
+        dmod_ref[0, s : s + 1, :] = jnp.sum(d_a, axis=0, keepdims=True)
+        gtok_ref[s] = dmid_own[s] + norm_grad(d_a * (1.0 + mod(1, s)), normed, inv)
+    h_qkv[0]()
+    h_qkv[1]()
+    join(sc_fc1, t_fc1, j_fc1)
+    for k in range(2, 6):
+        h_qkv[k]()
+    for k in range(6):
+        h_proj[k]()
+
+    join(sc_qkv, t_qkv, j_qkv)
+
+    at = sems.take(1)
+
+    def keep_proj(keep):
+        t_proj[...] = keep[...]
+
+    sc_proj.finish(keep_proj)
+    links.start(on_column, t_proj, t_proj, at, at, dev(z, x, c, 1 - y))
+    links.arrived(not_column, t_proj, at, sib)
+    j_proj[...] = t_proj[...]
+    for done in joins:
+        done()
+    links.drain()
+
+
+def fast_device(
+    tokens,
+    cond,
+    timesteps,
+    counts,
+    w_ada,
+    b_ada,
+    w_qkv,
+    b_qv,
+    w_proj,
+    b_proj,
+    w_fc1,
+    b_fc1,
+    w_fc2,
+    b_fc2,
+    cotangent,
+):
+    slots, half_len, width = tokens.shape
+    n_wide = lax.axis_size("wide")
+    w, y = lax.axis_index("wide"), lax.axis_index("narrow")
+    c = w % 2
+    quarter = 2 * y + c
+    shard = w_ada.shape[0]
+    mlp = w_fc1.shape[1]
+    hq = HEADS // 4
+    hw = hq * HEAD_DIM
+    nq = 3 * hw
+    rows = slots * half_len
+    mq = mlp // 4
+
+    cond_vec = cond.astype(F32) + time_features(timesteps, width)
+    cond_sig = jax.nn.sigmoid(cond_vec)
+    silu = (cond_vec * cond_sig).astype(BF16).astype(F32)
+    chunks = jnp.pad(
+        silu.reshape(slots, n_wide, shard).transpose(1, 0, 2),
+        ((0, 0), (0, 0), (0, width - shard)),
+    )
+    sizes = [b.shape[0] for b in (b_qv, b_proj, b_fc1, b_fc2, b_ada)]
+    vector = jnp.concatenate([b_qv, b_proj, b_fc1, b_fc2, b_ada]).astype(F32)
+    vector = jnp.pad(vector, (0, width - vector.shape[0]))
+    parcel = jnp.concatenate(
+        [chunks, jnp.broadcast_to(vector, (n_wide, 2, width))], axis=1
+    )
+    half = w_ada.shape[1] // 2
+    got, mod_halves = pl.pallas_call(
+        head_kernel,
+        out_shape=(
+            jax.ShapeDtypeStruct((n_wide, 4, width), F32),
+            jax.ShapeDtypeStruct((2, slots, half), F32),
+        ),
+        in_specs=[VMEM_SPEC, VMEM_SPEC],
+        out_specs=(VMEM_SPEC, VMEM_SPEC),
+        scratch_shapes=[
+            pltpu.VMEM((n_wide * slots, 128), F32),
+            pltpu.VMEM((n_wide, slots, half), F32),
+            pltpu.VMEM((n_wide, slots, half), F32),
+            pltpu.VMEM((slots, half), F32),
+            pltpu.SemaphoreType.DMA((2 * n_wide,)),
+            pltpu.SemaphoreType.DMA((2 * n_wide,)),
+        ],
+        compiler_params=pltpu.CompilerParams(
+            collective_id=0, has_side_effects=True, vmem_limit_bytes=48 << 20
+        ),
+    )(parcel, w_ada)
+    cuts = []
+    at = 0
+    for size in sizes:
+        cuts.append(got[:, 2, at : at + size])
+        at += size
+    qv_bias, proj_bias, fc1_bias, fc2_bias, ada_bias = cuts
+    modulate = mod_halves.transpose(1, 0, 2).reshape(slots, -1) + ada_bias.reshape(-1)
+    modulate = modulate.reshape(slots, 6, width)
+    qv_quarter = lax.dynamic_index_in_dim(
+        qv_bias.reshape(2, hq, 4, HEAD_DIM), quarter, 2, keepdims=False
+    ).reshape(2, hw)
+    bqkv = jnp.concatenate([qv_quarter[0], jnp.zeros((hw,), F32), qv_quarter[1]])[None]
+    bfc1 = lax.dynamic_index_in_dim(
+        fc1_bias.reshape(n_wide, 4, -1), quarter, 1, keepdims=False
+    ).reshape(1, mq)
+
+    live = (jnp.arange(slots, dtype=jnp.int32) < counts[0])[:, None, None]
+    cot_live = jnp.where(live, cotangent, jnp.zeros_like(cotangent))
+    src_qkv = (
+        w_qkv.reshape(shard, 3, hq, 4, HEAD_DIM).transpose(3, 0, 1, 2, 4).reshape(4, shard, nq)
+    )
+    src_fc1 = (
+        w_fc1.reshape(shard, n_wide, 4, mq // n_wide).transpose(2, 0, 1, 3).reshape(4, shard, mq)
+    )
+    src_fc2 = w_fc2.reshape(4, shard, width)
+
+    v16 = lambda *shape: pltpu.VMEM(shape, BF16)
+    v32 = lambda *shape: pltpu.VMEM(shape, F32)
+    pair_rows = 2 * shard
+    full = (4, 2, half_len, width)
+    scratch = [
+        v16(width, nq), v16(hq, shard, width), v16(width, mq), v16(mq, width),
+        v16(shard, nq), v16(shard, mq), v16(shard, width),
+        v16(shard, nq), v16(shard, mq), v16(shard, width),
+        v16(4, pair_rows, nq), v16(4, shard, width), v16(4, pair_rows, mq), v16(4, pair_rows, width),
+        v16(5, pair_rows, nq), v16(5, shard, width), v16(5, pair_rows, mq), v16(5, pair_rows, width),
+        v16(2, shard, nq), v16(2, shard, mq), v16(2, shard, width), v16(shard, width),
+        v16(*full), v16(*full), v16(*full), v16(*full),
+        v16(4, rows, nq), v16(hq, 4, rows, HEAD_DIM), v16(4, rows, mq), v16(4, rows, mq),
+        v16(4, rows, nq),
+        v16(*full), v16(*full),
+        v16(2, 2, half_len, width), v16(2, 2, half_len, width),
+        v16(2, half_len, width), v16(2, half_len, width),
+        v16(2, half_len, width), v16(2, half_len, width),
+        v32(slots, half_len, width), v32(slots, half_len, width),
+        v32(slots, half_len, width), v32(slots, half_len, width),
+        pltpu.SemaphoreType.DMA((200,)),
+        pltpu.SemaphoreType.DMA((200,)),
+        pltpu.SemaphoreType.DMA((4,)),
+    ]
+    out, gtok, dmod, bias_sums, j_qkv, j_fc1, j_fc2, j_proj = pl.pallas_call(
+        block_kernel,
+        out_shape=(
+            jax.ShapeDtypeStruct(tokens.shape, BF16),
+            jax.ShapeDtypeStruct(tokens.shape, F32),
+            jax.ShapeDtypeStruct((6, slots, width), F32),
+            jax.ShapeDtypeStruct((4, width), F32),
+            jax.ShapeDtypeStruct((4, shard, nq), BF16),
+            jax.ShapeDtypeStruct((4, shard, mq), BF16),
+            jax.ShapeDtypeStruct((4, shard, width), BF16),
+            jax.ShapeDtypeStruct((shard, width), BF16),
+        ),
+        in_specs=[VMEM_SPEC] * 7 + [HBM_SPEC] * 4,
+        out_specs=(VMEM_SPEC,) * 4 + (HBM_SPEC,) * 3 + (VMEM_SPEC,),
+        scratch_shapes=scratch,
+        compiler_params=pltpu.CompilerParams(
+            collective_id=1, has_side_effects=True, vmem_limit_bytes=VMEM_LIMIT
+        ),
+    )(
+        tokens, cot_live, modulate, bqkv, proj_bias.reshape(1, width), bfc1,
+        fc2_bias.reshape(1, width), src_qkv, w_proj, src_fc1, src_fc2,
+    )
+    out = jnp.where(live, out, jnp.zeros_like(out))
+
+    def spread(part, count):
+        part = part.reshape(count, 1, -1)
+        mine = (jnp.arange(4) == quarter).astype(F32)[None, :, None]
+        return (part * mine).reshape(n_wide, -1)
+
+    qv_sum = jnp.concatenate([bias_sums[3, :hw], bias_sums[3, 2 * hw : nq]])
+    v_rows = jnp.concatenate(
+        [
+            spread(qv_sum, 2 * hq),
+            bias_sums[1].reshape(n_wide, -1),
+            spread(bias_sums[0], n_wide),
+            bias_sums[2].reshape(n_wide, -1),
+        ],
+        axis=1,
+    )
+    v_size = v_rows.shape[1]
+    v_pad = -(-v_size // 128) * 128
+    v_rows = jnp.pad(v_rows, ((0, 0), (0, v_pad - v_size)))[:, None, :]
+    silu_cols = got[:, 0:2, :shard].reshape(n_wide * slots, shard).astype(BF16)
+    dmod = dmod.transpose(1, 0, 2).reshape(slots, 6 * width)
+    grad_ada, ada_sum, v_out, d_silu = pl.pallas_call(
+        tail_kernel,
+        out_shape=(
+            jax.ShapeDtypeStruct(w_ada.shape, F32),
+            jax.ShapeDtypeStruct((1, w_ada.shape[1]), F32),
+            jax.ShapeDtypeStruct((1, v_pad), F32),
+            jax.ShapeDtypeStruct((n_wide, slots, 128), F32),
+        ),
+        in_specs=[VMEM_SPEC] * 4,
+        out_specs=(VMEM_SPEC,) * 4,
+        scratch_shapes=[
+            v32(slots, 6 * width), v16(slots, 6 * width), v16(n_wide, slots, 6 * width),
+            v32(n_wide, 1, v_pad), v32(1, v_pad), v32(1, v_pad),
+            v32(n_wide * slots, 6 * width), v32(n_wide, slots, 128),
+            pltpu.SemaphoreType.DMA((4 * n_wide,)),
+            pltpu.SemaphoreType.DMA((4 * n_wide,)),
+        ],
+        compiler_params=pltpu.CompilerParams(
+            collective_id=2, has_side_effects=True, vmem_limit_bytes=48 << 20
+        ),
+    )(dmod, v_rows, silu_cols, w_ada)
+    ada_cut = b_ada.shape[0]
+    grad_b_ada = lax.dynamic_slice_in_dim(ada_sum[0], w * ada_cut, ada_cut, 0)
+    d_silu = d_silu[:, :, :shard].transpose(1, 0, 2).reshape(slots, width)
+    grad_cond = d_silu * (cond_sig + cond_vec * cond_sig * (1.0 - cond_sig))
+    bias_grads = []
+    at = 0
+    for size in sizes[:4]:
+        bias_grads.append(v_out[0, at : at + size])
+        at += size
+
+    grad_qkv = (
+        j_qkv.astype(F32)
+        .reshape(4, shard, 3, hq, HEAD_DIM)
+        .transpose(1, 2, 3, 0, 4)
+        .reshape(w_qkv.shape)
+    )
+    grad_fc1 = (
+        j_fc1.astype(F32)
+        .reshape(4, shard, n_wide, mq // n_wide)
+        .transpose(1, 2, 0, 3)
+        .reshape(w_fc1.shape)
+    )
+    grad_fc2 = j_fc2.astype(F32).reshape(w_fc2.shape)
+    return (
+        out,
+        gtok,
+        grad_cond,
+        grad_ada,
+        grad_b_ada,
+        grad_qkv,
+        bias_grads[0],
+        j_proj.astype(F32),
+        bias_grads[1],
+        grad_fc1,
+        bias_grads[2],
+        grad_fc2,
+        bias_grads[3],
+    )
+
+
 def solution(mesh):
     in_specs = (
         P("wide", "narrow", None),
@@ -333,6 +1339,8 @@
         P("wide", None),
         P("wide"),
     )
+    small = mesh.shape["wide"] == 16 and mesh.shape["narrow"] == 2
+    per_device = fast_device if small else on_device
     return jax.shard_map(
-        on_device, mesh=mesh, in_specs=in_specs, out_specs=out_specs, check_vma=False
-    )
+        per_device, mesh=mesh, in_specs=in_specs, out_specs=out_specs, check_vma=False
+    )

time: 866 us -> 388 us (0.45)
  waiting for transfers between devices: 452 us -> 0 us
  Pallas kernels: 0 us -> 324 us
  blocking collectives: 212 us -> 0 us
  matrix products: 78.1 us -> 0 us
  other arithmetic: 27.5 us -> 7.29 us
  between operations: 17.3 us -> 2.14 us
  local copies, waits for them, and re-layouts: 60.2 us -> 48 us
  starting transfers between devices: 8.71 us -> 0 us
    pallas_call x0 -> x3, Pallas kernels: none -> 324 us  [the longest x1 276 us: fast_device(): pl.pallas_call(block_kernel, out_shape=(jax.ShapeDtypeStruct(tokens.shape...]
    all_gather x7 -> x0, waiting for transfers between devices: 220 us -> none  [the longest x4 185 us: gather_wide(): return lax.all_gather(value, 'wide', axis=axis, tiled=True)]
    reduce_scatter x6 -> x0, waiting for transfers between devices: 191 us -> none  [the longest x3 158 us: scatter_wide(): lax.psum_scatter(part.astype(BF16), 'wide', scatter_dimension=0, tiled=True)]
    unnamed x2 -> x0, blocking collectives: 119 us -> none
    dot_general x21 -> x0, matrix products: 78.1 us -> none  [the longest x5 25.5 us: outer_sum(): return jnp.einsum('sk,sn->kn', left, right, preferred_element_type=F32)]
    all_gather x6 -> x0, blocking collectives: 74.2 us -> none  [the longest x2 41.7 us: gather_wide(): return lax.all_gather(value, 'wide', axis=axis, tiled=True)]
    unnamed x17 -> x0, waiting for transfers between devices: 30 us -> none
    reduce_sum x12 -> x0, other arithmetic: 16.6 us -> none  [the longest x1 4.42 us: on_device(): proj_bias_sum = jnp.sum(d_attn.astype(F32), axis=0)]
  transfers between devices with their start and end apart: 17 -> 0, of which waited for: 15 -> 0; matrix products, arithmetic and copies ran while one was open for 13% -> 0% of each run, Pallas kernels for 0% -> 0%
where the time goes in v2:
time: 388 us; the launch traced here: 381 us
  Pallas kernels  324 us (84%)
  local copies, waits for them, and re-layouts  48 us (12%)
  other arithmetic  7.29 us (2%)
    pallas_call x1, Pallas kernels, fast_device(): pl.pallas_call(block_kernel, out_shape=(jax.ShapeDtypeStruct(tokens.shape...  276 us
    pallas_call x1, Pallas kernels, fast_device(): pl.pallas_call(head_kernel, out_shape=(jax.ShapeDtypeStruct((n_wide, 4, w...  24.9 us
    pallas_call x1, Pallas kernels, fast_device(): pl.pallas_call(tail_kernel, out_shape=(jax.ShapeDtypeStruct(w_ada.shape,...  23.4 us
    reshape x3, local copies, waits for them, and re-layouts, fast_device(): grad_fc1 = j_fc1.astype(F32).reshape(4, shard, n_wide, mq // n_wide).tran...  12.9 us
    reshape x3, local copies, waits for them, and re-layouts, fast_device(): grad_qkv = j_qkv.astype(F32).reshape(4, shard, 3, hq, HEAD_DIM).transpose...  10.2 us

profile of v2, /device:TPU:0, one launch (start us, length us, event | category | flops | bytes accessed | tf_op | source)
XLA Modules:
  0.0 381.4 jit_solution(7061555389054648346)
XLA Ops:
  0.6 0.0 copy-start
  0.7 0.7 convert_element_type.42
  1.4 0.2 multiply_cosine_fusion
  1.6 0.8 multiply_convert_fusion
  2.4 0.1 reshape.130
  2.5 3.5 concatenate.24
  6.1 0.1 pad_maximum_fusion.parcel_ref
  6.2 24.9 %shard_map.246 = (f32[16,4,1152]{2,1,0:T(4,128)S(1)}, f32[2,2,3456]{2,1,0:T(2,128)S(1)}) custom-call(f32[16,4,1152]{2,1,0:T(4,128)S(1)} %pad_maximum_fusion.parcel_ref, bf16[72,6912]{1,0:T(8,128)(2,1)S(1)} %copy-done), custom_call_target="tpu_custom_call" | custom-call | tf_op jit(solution)/shard_map/pallas_call | solution.py:1134
  31.1 0.1 slice_reduce_fusion.2
  31.2 0.1 reshape_squeeze.19
  31.3 0.1 squeeze.29
  31.4 0.1 squeeze.30
  31.5 0.1 pad_maximum_fusion.1
  31.5 0.6 broadcast_in_dim.31.bqkv_ref
  32.1 0.1 slice_reduce_fusion.1
  32.3 0.1 reshape_squeeze.21
  32.4 0.7 reshape.132.bfc1_ref
  33.1 0.1 slice_reduce_fusion
  33.2 0.1 add.44
  33.4 0.6 broadcast_add_fusion.mod_ref
  34.0 0.1 slice_reduce_fusion.3
  34.2 0.7 reshape_squeeze.20.bproj_ref
  34.8 0.7 reshape_squeeze.22.bfc2_ref
  36.2 0.9 broadcast_select_fusion.1.cot_ref
  37.1 2.6 reshape.135
  39.8 0.2 copy.46
  40.0 2.3 reshape.136.src_fc1
  42.3 1.6 reshape.133
  43.8 0.3 copy.47
  44.2 1.3 reshape.134.src_qkv
  45.5 275.8 %shard_map.247 = (bf16[2,128,1152]{2,1,0:T(8,128)(2,1)}, f32[2,128,1152]{2,1,0:T(8,128)}, f32[6,2,1152]{2,1,0:T(2,128)}, f32[4,1152]{1,0:T(4,128)}, bf16[4,72,86...) custom-call(bf16[2,128,1152]{2,1,0:T(8,128)(2,1)} %tok_ref.1, ...), custom_call_target="tpu_custom_call" | custom-call | tf_op jit(solution)/shard_map/pallas_call | solution.py:1204
  321.2 0.8 slice_reduce_fusion.10
  322.0 0.1 concatenate.27
  322.1 0.1 concatenate.28
  322.2 0.1 broadcast_multiply_fusion.1
  322.3 0.1 mul.82
  322.4 0.9 slice_reduce_fusion.7
  323.3 0.1 mul.83
  323.4 0.1 mul.85
  323.4 0.1 mul.86
  323.5 0.1 mul.87
  323.6 0.1 reshape_squeeze.23
  323.7 0.1 reshape_squeeze.24
  323.8 0.1 select_maximum_fusion
  323.9 1.2 copy-done.1
  325.1 0.8 copy-done.2
  326.0 23.4 %shard_map.248 = (f32[72,6912]{1,0:T(8,128)S(1)}, f32[1,6912]{1,0:T(1,128)S(1)}, f32[1,640]{1,0:T(1,128)S(1)}, f32[16,2,128]{2,1,0:T(2,128)S(1)}) custom-call(f32[2,6912]{1,0:T(2,128)S(1)} %bitcast.38, f32[16,1,640]{2,1,0:T(1,128)S(1)} %broadcast_in_dim.32.v_ref, bf16[32,72]{1,0:T(8,128)(2,1)S(1)} %bitcast.39, bf16[72,6912]{1,0:T(8,128)(2,1)S(1)} %copy-done.1), custom_call_target="tpu_custom_call" | custom-call | tf_op jit(solution)/shard_map/pallas_call | solution.py:1248
  349.4 3.4 reshape.159
  352.7 4.6 %copy.41 = f32[72,16,4,72]{3,2,1,0:T(4,128)} copy(f32[72,16,4,72]{3,1,0,2:T(8,128)} %bitcast.40) | data formatting | bytes 2654208 | tf_op jit(solution)/shard_map/reshape | solution.py:1289
  357.3 5.0 %reshape.151 = f32[72,4608]{1,0:T(8,128)} reshape(f32[72,16,4,72]{3,2,1,0:T(4,128)} %copy.41) | data formatting | bytes 2654208 | tf_op jit(solution)/shard_map/reshape | solution.py:1289
  362.3 2.4 reshape.157
  364.7 3.8 %copy.40 = f32[72,3,4,4,72]{4,3,2,1,0:T(4,128)} copy(f32[72,3,4,4,72]{4,2,1,0,3:T(4,128)} %bitcast.41) | data formatting | bytes 1990656 | tf_op jit(solution)/shard_map/reshape | solution.py:1283
  368.5 4.0 %reshape.149 = f32[72,3456]{1,0:T(8,128)} reshape(f32[72,3,4,4,72]{4,3,2,1,0:T(4,128)} %copy.40) | data formatting | bytes 1990656 | tf_op jit(solution)/shard_map/reshape | solution.py:1283
  372.5 0.1 reshape.139
  372.6 0.7 add_multiply_fusion
  373.3 0.7 constant_dynamic-slice_fusion
  373.9 0.7 slice_reduce_fusion.8
  374.6 0.6 slice_bitcast_fusion.1
  375.2 0.6 slice.71
  375.8 1.2 bitcast_convert_fusion
  377.0 0.9 broadcast_select_fusion
  377.9 0.7 convert_element_type.47
  378.6 1.0 copy.52
  379.7 1.3 copy.53
  (42 shorter events, 0.4 us)
Async XLA Ops:
  0.6 5.6 %copy-start = (bf16[72,6912]{1,0:T(8,128)(2,1)S(1)}, bf16[72,6912]{1,0:T(8,128)(2,1)}, u32[]{:S(2)}) copy-start(bf16[72,6912]{1,0:T(8,128)(2,1)} %wada_ref.3) | copy-start | bytes 2985988
  6.1 30.1 %copy-start.7 = (bf16[2,128,1152]{2,1,0:T(8,128)(2,1)S(1)}, bf16[2,128,1152]{2,1,0:T(8,128)(2,1)}, u32[]{:S(2)}) copy-start(bf16[2,128,1152]{2,1,0:T(8,128)(2,1)} %param.29) | copy-start | bytes 1769476
  31.1 6.0 %copy-start.4 = (bf16[72,4608]{1,0:T(8,128)(2,1)S(1)}, bf16[72,4608]{1,0:T(8,128)(2,1)}, u32[]{:S(2)}) copy-start(bf16[72,4608]{1,0:T(8,128)(2,1)} %param.25) | copy-start | bytes 1990660
  39.9 2.3 copy-start.10
  323.9 1.2 copy-start.1
  325.1 0.8 copy-start.2
  325.9 23.4 %copy-start.6 = (bf16[4,72,1152]{2,1,0:T(8,128)(2,1)S(1)}, bf16[4,72,1152]{2,1,0:T(8,128)(2,1)}, u32[]{:S(2)}) copy-start(bf16[4,72,1152]{2,1,0:T(8,128)(2,1)} %get-tuple-element.39) | copy-start | bytes 1990660
  357.3 5.0 %copy-start.9 = (bf16[4,72,864]{2,1,0:T(8,128)(2,1)S(1)}, bf16[4,72,864]{2,1,0:T(8,128)(2,1)}, u32[]{:S(2)}) copy-start(bf16[4,72,864]{2,1,0:T(8,128)(2,1)} %get-tuple-element.36) | copy-start | bytes 1492996
  368.5 4.1 %copy-start.12 = (bf16[2,1152]{1,0:T(2,128)(2,1)S(1)}, bf16[2,1152]{1,0:T(2,128)(2,1)}, u32[]{:S(2)}) copy-start(bf16[2,1152]{1,0:T(2,128)(2,1)} %param.16) | copy-start | bytes 13828
  368.5 7.2 %copy-start.5 = (bf16[4,72,1152]{2,1,0:T(8,128)(2,1)S(1)}, bf16[4,72,1152]{2,1,0:T(8,128)(2,1)}, u32[]{:S(2)}) copy-start(bf16[4,72,1152]{2,1,0:T(8,128)(2,1)} %get-tuple-element.40) | copy-start | bytes 1990660
  372.5 4.5 %copy-start.8 = (bf16[2,128,1152]{2,1,0:T(8,128)(2,1)S(1)}, bf16[2,128,1152]{2,1,0:T(8,128)(2,1)}, u32[]{:S(2)}) copy-start(bf16[2,128,1152]{2,1,0:T(8,128)(2,1)} %get-tuple-element.29) | copy-start | bytes 1769476
  375.7 2.1 copy-start.11
  377.0 1.7 copy-start.3

commit v3 on v1

--- a/solution.py
+++ b/solution.py
@@ -1,8 +1,11 @@
+import functools
 import math
 
 import jax
 import jax.numpy as jnp
 from jax import lax
+from jax.experimental import pallas as pl
+from jax.experimental.pallas import tpu as pltpu
 from jax.sharding import PartitionSpec as P
 
 HEADS = 16
@@ -300,6 +303,1125 @@
     )
 
 
+MESH = pl.DeviceIdType.MESH
+NZ = 4
+GELU_C = 0.7978845608028654
+HBM_SPEC = pl.BlockSpec(memory_space=pl.ANY)
+VMEM_SPEC = pl.BlockSpec(memory_space=pltpu.VMEM)
+VMEM_LIMIT = 63 << 20
+
+
+def dot_nn(a, b):
+    return lax.dot_general(a, b, (((1,), (0,)), ((), ())), preferred_element_type=F32)
+
+
+def dot_nt(a, b):
+    return lax.dot_general(a, b, (((1,), (1,)), ((), ())), preferred_element_type=F32)
+
+
+def dot_tn(a, b):
+    return lax.dot_general(a, b, (((0,), (0,)), ((), ())), preferred_element_type=F32)
+
+
+def do_when(cond, fn):
+    if cond is True:
+        fn()
+    else:
+        pl.when(cond)(fn)
+
+
+def both(a, b):
+    if a is True:
+        return b
+    if b is True:
+        return a
+    return jnp.logical_and(a, b)
+
+
+def greet(peers):
+    barrier = pltpu.get_barrier_semaphore()
+    total = 0
+    for cond, dev in peers:
+        do_when(
+            cond,
+            lambda dev=dev: pl.semaphore_signal(
+                barrier, inc=1, device_id=dev, device_id_type=MESH
+            ),
+        )
+        total = total + (1 if cond is True else cond.astype(jnp.int32))
+    pl.semaphore_wait(barrier, total)
+
+
+class Sems:
+    def __init__(self, send, recv):
+        self.send, self.recv, self.n = send, recv, 0
+
+    def take(self, count):
+        at = self.n
+        self.n += count
+        return at
+
+
+class Links:
+    def __init__(self, sems):
+        self.sems = sems
+        self.sent = []
+
+    def copy(self, src, dst, index, dev):
+        return pltpu.make_async_remote_copy(
+            src_ref=src,
+            dst_ref=dst,
+            send_sem=self.sems.send.at[index],
+            recv_sem=self.sems.recv.at[index],
+            device_id=dev,
+            device_id_type=MESH,
+        )
+
+    def start(self, cond, src, dst, send_index, recv_index, dev):
+        copy = pltpu.make_async_remote_copy(
+            src_ref=src,
+            dst_ref=dst,
+            send_sem=self.sems.send.at[send_index],
+            recv_sem=self.sems.recv.at[recv_index],
+            device_id=dev,
+            device_id_type=MESH,
+        )
+        do_when(cond, copy.start)
+        self.sent.append((cond, copy))
+        return copy
+
+    def arrived(self, cond, ref, index, dev):
+        copy = self.copy(ref, ref, index, dev)
+        do_when(cond, copy.wait_recv)
+
+    def left(self, copy):
+        for cond, one in self.sent:
+            if one is copy:
+                do_when(cond, one.wait_send)
+        self.sent = [entry for entry in self.sent if entry[1] is not copy]
+
+    def drain(self):
+        for cond, copy in self.sent:
+            do_when(cond, copy.wait_send)
+        self.sent = []
+
+
+class Gather:
+    def __init__(self, links, pos, block, source, sink):
+        self.links, self.pos, self.block = links, pos, block
+        self.source, self.sink = source, sink
+        take = links.sems.take
+        self.z_at, self.x_at, self.up_at, self.down_at = take(4), take(4), take(4), take(4)
+        self.mine = []
+
+    def along_z(self, cond, s, up, down):
+        z, x, c, y = self.pos["z"], self.pos["x"], self.pos["c"], self.pos["y"]
+        ref = self.block(s, x)
+        for wanted, inside, at, to in (
+            (up, z < NZ - 1, self.up_at, z + 1),
+            (down, z > 0, self.down_at, z - 1),
+        ):
+            if wanted:
+                self.mine.append(
+                    self.links.start(
+                        both(cond, inside), ref, ref, at + s, self.z_at + s,
+                        self.pos["dev"](to, x, c, y),
+                    )
+                )
+
+    def forward(self, cond, s, up, down):
+        z, x, c, y = self.pos["z"], self.pos["x"], self.pos["c"], self.pos["y"]
+        self.along_z(cond, s, up, down)
+        ref = self.block(s, x)
+        self.mine.append(
+            self.links.start(
+                cond, ref, ref, self.x_at + s, self.x_at + s, self.pos["dev"](z, 1 - x, c, y)
+            )
+        )
+
+    def own(self):
+        self.forward(self.source, self.pos["z"], True, True)
+
+    def step(self, d):
+        z, x = self.pos["z"], self.pos["x"]
+        cond = both(self.source, z >= d)
+        s = jnp.maximum(z - d, 0)
+        self.links.arrived(cond, self.block(s, x), self.z_at + s, self.pos["me"])
+        self.forward(cond, s, True, False)
+        cond = both(self.source, z <= NZ - 1 - d)
+        s = jnp.minimum(z + d, NZ - 1)
+        self.links.arrived(cond, self.block(s, x), self.z_at + s, self.pos["me"])
+        self.forward(cond, s, False, True)
+
+    def finish(self):
+        x = self.pos["x"]
+        for s in range(NZ):
+            self.links.arrived(self.sink, self.block(s, 1 - x), self.x_at + s, self.pos["me"])
+
+
+class GatherAcross(Gather):
+    def __init__(self, links, pos, block, on_column, not_column):
+        super().__init__(links, pos, block, True, True)
+        self.on_column, self.not_column = on_column, not_column
+
+    def forward(self, cond, s, up, down):
+        self.along_z(cond, s, up, down)
+
+    def across(self):
+        z, x, c, y = self.pos["z"], self.pos["x"], self.pos["c"], self.pos["y"]
+        ref = self.block(z, x)
+        self.mine.append(
+            self.links.start(
+                self.on_column, ref, ref, self.x_at, self.x_at, self.pos["dev"](z, 1 - x, c, y)
+            )
+        )
+
+    def own(self):
+        z, x = self.pos["z"], self.pos["x"]
+        self.links.arrived(self.not_column, self.block(z, x), self.x_at, self.pos["me"])
+        self.forward(True, z, True, True)
+
+    def finish(self):
+        pass
+
+
+class Scatter:
+    def __init__(self, links, pos, block, sums_x, sums_z, source, sink):
+        self.links, self.pos, self.block = links, pos, block
+        self.sums_x, self.sums_z = sums_x, sums_z
+        self.source, self.sink = source, sink
+        take = links.sems.take
+        self.x_at, self.z_at, self.up_at, self.down_at = take(4), take(5), take(4), take(4)
+
+    def begin(self):
+        z, x, c, y = self.pos["z"], self.pos["x"], self.pos["c"], self.pos["y"]
+        for s in (3, 0, 2, 1):
+            self.links.start(
+                self.source, self.block(s, 1 - x), self.sums_x.at[s], self.x_at + s,
+                self.x_at + s, self.pos["dev"](z, 1 - x, c, y),
+            )
+
+    def add_x(self, s):
+        self.links.arrived(True, self.sums_x.at[s], self.x_at + s, self.pos["me"])
+        return self.block(s, self.pos["x"])[...].astype(F32) + self.sums_x[s].astype(F32)
+
+    def hop(self, s, up):
+        z, x, c, y = self.pos["z"], self.pos["x"], self.pos["c"], self.pos["y"]
+        cond = both(self.sink, (z < s) if up else (z > s))
+
+        def run():
+            ref = self.block(s, x)
+            ref[...] = self.add_x(s).astype(BF16)
+            inner = (z > 0) if up else (z < NZ - 1)
+
+            @pl.when(inner)
+            def _():
+                self.links.arrived(True, self.sums_z.at[s], self.z_at + s, self.pos["me"])
+                ref[...] = (ref[...].astype(F32) + self.sums_z[s].astype(F32)).astype(BF16)
+
+        do_when(cond, run)
+        near = (z == s - 1) if up else (z == s + 1)
+        slot = s if up else jnp.where(near, 4, s)
+        to = self.pos["dev"](z + 1 if up else z - 1, x, c, y)
+        at = (self.up_at if up else self.down_at) + s
+        self.links.start(
+            cond, self.block(s, x), self.sums_z.at[slot], at, self.z_at + slot, to
+        )
+
+    def finish(self, store):
+        z, x = self.pos["z"], self.pos["x"]
+        keep = self.block(z, x)
+
+        def run():
+            total = keep[...].astype(F32)
+            self.links.arrived(True, self.sums_x.at[z], self.x_at + z, self.pos["me"])
+            total = total + self.sums_x[z].astype(F32)
+            keep[...] = total.astype(BF16)
+
+            @pl.when(z > 0)
+            def _():
+                self.links.arrived(True, self.sums_z.at[z], self.z_at + z, self.pos["me"])
+                keep[...] = (keep[...].astype(F32) + self.sums_z[z].astype(F32)).astype(BF16)
+
+            @pl.when(z < NZ - 1)
+            def _():
+                self.links.arrived(True, self.sums_z.at[4], self.z_at + 4, self.pos["me"])
+                keep[...] = (keep[...].astype(F32) + self.sums_z[4].astype(F32)).astype(BF16)
+
+            store(keep)
+
+        do_when(self.sink, run)
+
+    def hops(self):
+        out = []
+        for k in range(3):
+            out.append(lambda k=k: self.hop(3 - k, True))
+            out.append(lambda k=k: self.hop(k, False))
+        return out
+
+
+class ScatterAcross(Scatter):
+    def begin(self):
+        pass
+
+    def add_x(self, s):
+        return self.block(s, self.pos["x"])[...].astype(F32)
+
+    def finish(self, not_column, on_column):
+        z, x, c, y = self.pos["z"], self.pos["x"], self.pos["c"], self.pos["y"]
+        keep = self.block(z, x)
+
+        @pl.when(z > 0)
+        def _():
+            self.links.arrived(True, self.sums_z.at[z], self.z_at + z, self.pos["me"])
+            keep[...] = (keep[...].astype(F32) + self.sums_z[z].astype(F32)).astype(BF16)
+
+        @pl.when(z < NZ - 1)
+        def _():
+            self.links.arrived(True, self.sums_z.at[4], self.z_at + 4, self.pos["me"])
+            keep[...] = (keep[...].astype(F32) + self.sums_z[4].astype(F32)).astype(BF16)
+
+        self.links.start(
+            not_column, keep, self.sums_x.at[0], self.x_at, self.x_at,
+            self.pos["dev"](z, 1 - x, c, y),
+        )
+
+    def land(self, on_column, target):
+        keep = self.block(self.pos["z"], self.pos["x"])
+
+        @pl.when(on_column)
+        def _():
+            self.links.arrived(True, self.sums_x.at[0], self.x_at, self.pos["me"])
+            target[...] = (keep[...].astype(F32) + self.sums_x[0].astype(F32)).astype(BF16)
+
+
+class PlaneExchange:
+    def __init__(self, links, n_wide, w, y):
+        self.links, self.n_wide, self.w, self.y = links, n_wide, w, y
+        self.at = links.sems.take(n_wide)
+
+    def begin(self, source, target):
+        self.copies = []
+        for k in range(1, self.n_wide):
+            peer = lax.rem(self.w + k, self.n_wide)
+            self.copies.append(
+                self.links.start(
+                    True, source(peer), target.at[self.w], self.at + k, self.at + k,
+                    (peer, self.y),
+                )
+            )
+
+    def finish(self):
+        for copy in self.copies:
+            copy.wait_recv()
+
+
+class GroupGather:
+    def __init__(self, links, pos, full):
+        self.links, self.pos, self.full = links, pos, full
+        self.at = links.sems.take(3)
+
+    def begin(self):
+        z, x, c, y = self.pos["z"], self.pos["x"], self.pos["c"], self.pos["y"]
+        ref = self.full.at[pl.ds(2 * c, 2), y]
+        self.links.start(True, ref, ref, self.at, self.at, self.pos["dev"](z, x, c, 1 - y))
+        self.links.start(True, ref, ref, self.at + 1, self.at + 1, self.pos["dev"](z, x, 1 - c, y))
+
+    def relay(self):
+        z, x, c, y = self.pos["z"], self.pos["x"], self.pos["c"], self.pos["y"]
+        ref = self.full.at[pl.ds(2 * c, 2), 1 - y]
+        self.links.arrived(True, ref, self.at, self.pos["me"])
+        self.links.start(True, ref, ref, self.at + 2, self.at + 2, self.pos["dev"](z, x, 1 - c, y))
+
+    def finish(self):
+        c, y = self.pos["c"], self.pos["y"]
+        other = pl.ds(2 * (1 - c), 2)
+        self.links.arrived(True, self.full.at[other, y], self.at + 1, self.pos["me"])
+        self.links.arrived(True, self.full.at[other, 1 - y], self.at + 2, self.pos["me"])
+
+
+class GroupSum:
+    def __init__(self, links, pos, full, from_core, to_pair, from_pair):
+        self.links, self.pos, self.full = links, pos, full
+        self.from_core, self.to_pair, self.from_pair = from_core, to_pair, from_pair
+        self.at = links.sems.take(2)
+
+    def begin(self):
+        z, x, c, y = self.pos["z"], self.pos["x"], self.pos["c"], self.pos["y"]
+        self.core_copy = self.links.start(
+            True, self.full.at[pl.ds(2 * (1 - c), 2)], self.from_core, self.at, self.at,
+            self.pos["dev"](z, x, 1 - c, y),
+        )
+
+    def relay(self):
+        z, x, c, y = self.pos["z"], self.pos["x"], self.pos["c"], self.pos["y"]
+        self.links.arrived(True, self.from_core, self.at, self.pos["me"])
+        for s in range(2):
+            self.to_pair[s] = (
+                self.full[2 * c + s, 1 - y].astype(F32) + self.from_core[s, 1 - y].astype(F32)
+            ).astype(BF16)
+        self.pair_copy = self.links.start(
+            True, self.to_pair, self.from_pair, self.at + 1, self.at + 1,
+            self.pos["dev"](z, x, c, 1 - y),
+        )
+
+    def arrived(self):
+        self.links.arrived(True, self.from_pair, self.at + 1, self.pos["me"])
+
+    def total(self, s):
+        c, y = self.pos["c"], self.pos["y"]
+        return (
+            self.full[2 * c + s, y].astype(F32)
+            + self.from_core[s, y].astype(F32)
+            + self.from_pair[s].astype(F32)
+        )
+
+
+def gelu_both(u):
+    inner = GELU_C * (u + 0.044715 * u * u * u)
+    tan = jnp.tanh(inner)
+    slope = GELU_C * (1.0 + 3.0 * 0.044715 * u * u)
+    act = 0.5 * u * (1.0 + tan)
+    grad = 0.5 * (1.0 + tan) + 0.5 * u * (1.0 - tan * tan) * slope
+    return act, grad
+
+
+def block_kernel(
+    order, n_wide,
+    tok_ref, cot_ref, parcel_ref, wada_ref, bada_ref,
+    wqkv_ref, wfc1_ref, src_fc2, src_proj,
+    out_ref, gtok_ref, got_ref, dmall_ref, vout_ref, dsil_ref,
+    p_qkv, p_fc1, j_fc2, j_proj,
+    g_qkv, g_proj, g_fc1, g_fc2, w_fc2,
+    i_qkv, i_fc1, i_fc2, own_qkv, own_fc1, own_fc2, o_qkv, o_fc1,
+    x_qkv, x_proj, x_fc1, x_fc2, z_qkv, z_proj, z_fc1, z_fc2,
+    t_qkv, t_fc1, t_fc2, t_proj, j_qkv, j_fc1,
+    a_all, m_all, d_all, qkv_all, att_all, act_all, gp_all,
+    sum_a, sum_b, core_a, core_b, to_a, to_b, from_a, from_b,
+    attn_own, mid_own, dmid_own,
+    left, part, parts, tot, modh, mods, bqkv, brow, bias,
+    dmod, dm_pair, dm_low, dm_all, v_send, v_all, dm_rows, ds_send,
+    send, recv, local,
+):
+    w, y = lax.axis_index("wide"), lax.axis_index("narrow")
+    z, x, c = w // 4, (w // 2) % 2, w % 2
+    chip = 2 * z + x
+    quarter = 2 * y + c
+
+    def dev(z, x, c, y):
+        return ((z * 2 + x) * 2 + c, y)
+
+    sib, pair = dev(z, x, 1 - c, y), dev(z, x, c, 1 - y)
+    pos = {"z": z, "x": x, "c": c, "y": y, "dev": dev, "me": sib}
+    links = Links(Sems(send, recv))
+    sems = links.sems
+    half_len = tok_ref.shape[1]
+    width = tok_ref.shape[2]
+    hd = HEAD_DIM
+    hq = g_proj.shape[0]
+    hw = hd * hq
+    shard = own_qkv.shape[0]
+    rows2 = 2 * shard
+    rows = 2 * half_len
+    all_rows = 4 * rows
+    half = modh.shape[2]
+    head_scale = 1.0 / math.sqrt(HEAD_DIM)
+    da_all = act_all
+
+    greet(
+        [(True, (lax.rem(w + k, n_wide), y)) for k in range(1, n_wide)]
+        + [(True, pair), (True, dev(z, x, 1 - c, 1 - y))]
+    )
+
+    def rows_of(full):
+        return lambda s, xx: full.at[pl.ds(pl.multiple_of((2 * s + xx) * rows2, 16), rows2), :]
+
+    def head_of(s, xx):
+        return g_proj.at[s]
+
+    on_column = x == y
+    not_column = jnp.logical_not(on_column)
+    init = sems.take(3)
+    ga_qkv = Gather(links, pos, rows_of(g_qkv), True, True)
+    ga_proj = GatherAcross(links, pos, head_of, on_column, not_column)
+    ga_fc1 = Gather(links, pos, rows_of(g_fc1), True, True)
+    ga_fc2 = Gather(links, pos, rows_of(g_fc2), True, True)
+    gg_a = GroupGather(links, pos, a_all)
+    gg_d = GroupGather(links, pos, d_all)
+    gg_m = GroupGather(links, pos, m_all)
+    gg_da = GroupGather(links, pos, da_all)
+    gs_attn = GroupSum(links, pos, sum_a, core_a, to_a, from_a)
+    gs_mlp = GroupSum(links, pos, sum_b, core_b, to_b, from_b)
+    gs_dm = GroupSum(links, pos, sum_a, core_a, to_a, from_a)
+    gs_da = GroupSum(links, pos, sum_b, core_b, to_b, from_b)
+    sc_fc2 = Scatter(links, pos, rows_of(w_fc2), x_fc2, z_fc2, True, True)
+    sc_fc1 = Scatter(links, pos, rows_of(g_fc2), x_fc1, z_fc1, True, True)
+    sc_qkv = Scatter(links, pos, rows_of(g_qkv), x_qkv, z_qkv, True, True)
+    sc_proj = ScatterAcross(links, pos, head_of, x_proj, z_proj, True, True)
+    ex_head = PlaneExchange(links, n_wide, w, y)
+    ex_mod = PlaneExchange(links, n_wide, w, y)
+    ex_dm = PlaneExchange(links, n_wide, w, y)
+    ex_v = PlaneExchange(links, n_wide, w, y)
+    ex_ds = PlaneExchange(links, n_wide, w, y)
+    swap_mod, swap_dm, swap_v, swap_proj = sems.take(1), sems.take(1), sems.take(1), sems.take(1)
+    steps = {}
+
+    def step(fn):
+        steps[fn.__name__] = fn
+        return fn
+
+    def norm(value):
+        center = value - jnp.mean(value, axis=-1, keepdims=True)
+        inv = lax.rsqrt(jnp.mean(center * center, axis=-1, keepdims=True) + eps_norm)
+        return center * inv, inv
+
+    def norm_grad(grad, normed, inv):
+        return inv * (
+            grad
+            - jnp.mean(grad, axis=-1, keepdims=True)
+            - normed * jnp.mean(grad * normed, axis=-1, keepdims=True)
+        )
+
+    def mod(k, s):
+        return mods[k, s : s + 1, :]
+
+    def pick(source, count, which):
+        return jnp.concatenate(
+            [source[:, (4 * j + which) * hd : (4 * j + which + 1) * hd] for j in range(count)],
+            axis=1,
+        )
+
+    fc2_copy = pltpu.make_async_copy(src_fc2.at[quarter], own_fc2, local.at[0])
+    proj_copy = pltpu.make_async_copy(src_proj, g_proj.at[z], local.at[1])
+
+    @step
+    def init0():
+        fc2_copy.start()
+        do_when(on_column, proj_copy.start)
+        ex_head.begin(lambda p: parcel_ref.at[p], got_ref)
+        got_ref[w] = parcel_ref[w]
+        value = wqkv_ref[...]
+        for q in range(4):
+
+            @pl.when(quarter == q)
+            def _():
+                own_qkv[...] = pick(value, 3 * hq, q)
+
+            @pl.when(2 * y + 1 - c == q)
+            def _():
+                o_qkv[...] = pick(value, 3 * hq, q)
+
+        links.start(True, o_qkv, i_qkv, init, init, sib)
+
+    @step
+    def init1():
+        links.start(True, src_fc2.at[2 * y + 1 - c], i_fc2, init + 2, init + 2, sib)
+        value = wfc1_ref[...]
+        for q in range(4):
+
+            @pl.when(quarter == q)
+            def _():
+                own_fc1[...] = pick(value, n_wide, q)
+
+            @pl.when(2 * y + 1 - c == q)
+            def _():
+                o_fc1[...] = pick(value, n_wide, q)
+
+        links.start(True, o_fc1, i_fc1, init + 1, init + 1, sib)
+
+    def place(own, inbox, full, index):
+        links.arrived(True, inbox, init + index, sib)
+        mine, other = own[...].astype(F32), inbox[...].astype(F32)
+        first = jnp.where(c == 0, mine, other)
+        second = jnp.where(c == 0, other, mine)
+        at = pl.ds(pl.multiple_of(chip * rows2, 16), rows2)
+        full[at, :] = jnp.concatenate([first, second], axis=0).astype(BF16)
+
+    @step
+    def q0():
+        place(own_qkv, i_qkv, g_qkv, 0)
+        ga_qkv.own()
+
+    @step
+    def f0():
+        place(own_fc1, i_fc1, g_fc1, 1)
+        ga_fc1.own()
+
+    @step
+    def e0():
+        fc2_copy.wait()
+        place(own_fc2, i_fc2, g_fc2, 2)
+        ga_fc2.own()
+
+    @step
+    def px():
+        do_when(on_column, proj_copy.wait)
+        ga_proj.across()
+
+    steps["p0"] = ga_proj.own
+    for letter, gather in (("q", ga_qkv), ("p", ga_proj), ("f", ga_fc1), ("e", ga_fc2)):
+        for d in range(1, NZ):
+            steps[letter + str(d)] = lambda gather=gather, d=d: gather.step(d)
+
+    @step
+    def h1():
+        ex_head.finish()
+        for s in range(n_wide):
+            left[2 * s : 2 * s + 2, :] = got_ref[s, 0:2, 0:128]
+        lhs = left[...][:, :shard].astype(BF16)
+        cols = pl.ds(pl.multiple_of(y * half, 128), half)
+        res = dot_nn(lhs, wada_ref[:, cols]) + bada_ref[:, cols]
+        for s in range(n_wide):
+            part[s] = res[2 * s : 2 * s + 2, :]
+        parts[w] = part[w]
+        ex_mod.begin(lambda p: part.at[p], parts)
+
+    @step
+    def hb():
+        def row(lane, owners):
+            return jnp.concatenate([got_ref[o, 2:3, lane : lane + hd] for o in owners], axis=1)
+
+        every = range(n_wide)
+        brow[0:1, :] = row(0, every)
+        brow[1:2, :] = row(128, every)
+        brow[2:3, :] = row(256, every)
+        bqkv[...] = jnp.concatenate(
+            [
+                row(384, [2 * j + y for j in range(hq)]),
+                jnp.zeros((1, hw), F32),
+                row(384, [n_wide // 2 + 2 * j + y for j in range(hq)]),
+            ],
+            axis=1,
+        )
+
+    @step
+    def h2():
+        ex_mod.finish()
+        total = parts[0]
+        for s in range(1, n_wide):
+            total = total + parts[s]
+        tot[...] = total
+        modh[y] = total
+        links.start(True, tot, modh.at[y], swap_mod, swap_mod, pair)
+
+    @step
+    def h3():
+        links.arrived(True, modh.at[1 - y], swap_mod, sib)
+        for k in range(6):
+            at = (k % 3) * width
+            mods[k] = modh[k // 3, :, at : at + width]
+
+    @step
+    def ln1():
+        for s in range(2):
+            normed, inv = norm(tok_ref[s].astype(F32))
+            a_all[2 * c + s, y] = (normed * (1.0 + mod(1, s)) + mod(0, s)).astype(BF16)
+        gg_a.begin()
+
+    steps["ar"], steps["af"] = gg_a.relay, gg_a.finish
+
+    @step
+    def d0():
+        for s in range(2):
+            d_all[2 * c + s, y] = (mod(5, s) * cot_ref[s].astype(F32)).astype(BF16)
+        gg_d.begin()
+
+    steps["dr"], steps["df"] = gg_d.relay, gg_d.finish
+
+    @step
+    def qkv():
+        ga_qkv.finish()
+
+        @pl.loop(0, 4)
+        def _(i):
+            res = dot_nn(a_all[i].reshape(rows, width), g_qkv[...]) + bqkv[...]
+            qkv_all[i] = res.astype(BF16)
+
+    def head_parts(packed, h):
+        return [packed[:, t * hw + h * hd : t * hw + (h + 1) * hd] for t in range(3)]
+
+    def softmax(q, k):
+        scores = dot_nt(q, k) * head_scale
+        top = jnp.max(scores, axis=-1, keepdims=True)
+        e = jnp.exp(scores - top)
+        return e * (1.0 / jnp.sum(e, axis=-1, keepdims=True))
+
+    @step
+    def att():
+        @pl.loop(0, 4)
+        def _(i):
+            packed = qkv_all[i]
+            acc = None
+            for h in range(hq):
+                q, k, v = head_parts(packed, h)
+                p = softmax(q, k).astype(BF16)
+                o = dot_nn(p, v).astype(BF16)
+                att_all[h, i] = o
+                term = dot_nn(o, g_proj[h])
+                acc = term if acc is None else acc + term
+            sum_a[i] = acc.astype(BF16).reshape(2, half_len, width)
+
+        gs_attn.begin()
+
+    steps["sr"] = gs_attn.relay
+
+    @step
+    def ln2():
+        gs_attn.arrived()
+        for s in range(2):
+            attn = gs_attn.total(s) + brow[1:2, :]
+            attn_own[s] = attn
+            mid = tok_ref[s].astype(F32) + mod(2, s) * attn
+            mid_own[s] = mid
+            normed, inv = norm(mid)
+            m_all[2 * c + s, y] = (normed * (1.0 + mod(4, s)) + mod(3, s)).astype(BF16)
+        gg_m.begin()
+
+    steps["mr"], steps["mf"] = gg_m.relay, gg_m.finish
+
+    @step
+    def fc1():
+        ga_fc1.finish()
+
+        @pl.loop(0, 4)
+        def _(i):
+            u = dot_nn(m_all[i].reshape(rows, width), g_fc1[...]) + brow[0:1, :]
+            act, grad = gelu_both(u)
+            act_all[i] = act.astype(BF16).reshape(2, half_len, width)
+            gp_all[i] = grad.astype(BF16)
+
+    steps["ef"] = ga_fc2.finish
+
+    @step
+    def fc2():
+        @pl.loop(0, 4)
+        def _(i):
+            res = dot_nn(act_all[i].reshape(rows, width), g_fc2[...])
+            sum_b[i] = res.astype(BF16).reshape(2, half_len, width)
+
+        gs_mlp.begin()
+
+    steps["ur"] = gs_mlp.relay
+
+    def outer(left, right, full):
+        lanes = width // 3
+
+        @pl.loop(0, 3)
+        def _(j):
+            at = pl.ds(pl.multiple_of(j * lanes, 128), lanes)
+            full[at, :] = dot_tn(left(at).reshape(all_rows, lanes), right()).astype(BF16)
+
+    @step
+    def w2():
+        outer(
+            lambda at: act_all[:, :, :, at], lambda: d_all[...].reshape(all_rows, width), w_fc2
+        )
+        sc_fc2.begin()
+
+    @step
+    def dh():
+        bias[...] = jnp.zeros_like(bias)
+
+        @pl.loop(0, 4)
+        def _(i):
+            d_act = dot_nt(d_all[i].reshape(rows, width), g_fc2[...])
+            d_hidden = (d_act * gp_all[i].astype(F32)).astype(BF16)
+            gp_all[i] = d_hidden
+            bias[0:1, :] += jnp.sum(d_hidden.astype(F32), axis=0, keepdims=True)
+
+    @step
+    def dm():
+        links.left(gs_attn.core_copy)
+
+        @pl.loop(0, 4)
+        def _(i):
+            res = dot_nt(gp_all[i], g_fc1[...])
+            sum_a[i] = res.astype(BF16).reshape(2, half_len, width)
+
+        gs_dm.begin()
+
+    @step
+    def w1():
+        for copy in ga_fc2.mine:
+            links.left(copy)
+        outer(
+            lambda at: m_all[:, :, :, at], lambda: gp_all[...].reshape(all_rows, width), g_fc2
+        )
+        sc_fc1.begin()
+
+    @step
+    def tr():
+        links.left(gs_attn.pair_copy)
+        gs_dm.relay()
+
+    @step
+    def res():
+        gs_mlp.arrived()
+        for s in range(2):
+            mlp = gs_mlp.total(s) + brow[2:3, :]
+            out_ref[s] = (mid_own[s] + mod(5, s) * mlp).astype(BF16)
+            grad_out = cot_ref[s].astype(F32)
+            dmod[5, s : s + 1, :] = jnp.sum(grad_out * mlp, axis=0, keepdims=True)
+            bias[2:3, :] += jnp.sum(d_all[2 * c + s, y].astype(F32), axis=0, keepdims=True)
+
+    @step
+    def ln2b():
+        gs_dm.arrived()
+        for s in range(2):
+            d_m = gs_dm.total(s)
+            normed, inv = norm(mid_own[s])
+            dmod[4, s : s + 1, :] = jnp.sum(d_m * normed, axis=0, keepdims=True)
+            dmod[3, s : s + 1, :] = jnp.sum(d_m, axis=0, keepdims=True)
+            d_mid = cot_ref[s].astype(F32) + norm_grad(d_m * (1.0 + mod(4, s)), normed, inv)
+            dmid_own[s] = d_mid
+            d_attn = (mod(2, s) * d_mid).astype(BF16)
+            da_all[2 * c + s, y] = d_attn
+            dmod[2, s : s + 1, :] = jnp.sum(d_mid * attn_own[s], axis=0, keepdims=True)
+            bias[1:2, :] += jnp.sum(d_attn.astype(F32), axis=0, keepdims=True)
+        gg_da.begin()
+
+    steps["gr"], steps["gf"] = gg_da.relay, gg_da.finish
+
+    @step
+    def attb():
+        @pl.loop(0, 4)
+        def _(i):
+            packed = qkv_all[i]
+            d_attn = da_all[i].reshape(rows, width)
+            grads = [[], [], []]
+            for h in range(hq):
+                q, k, v = head_parts(packed, h)
+                p = softmax(q, k)
+                p_low = p.astype(BF16)
+                d_att = dot_nt(d_attn, g_proj[h]).astype(BF16)
+                d_p = dot_nt(d_att, v)
+                d_s = (p * (d_p - jnp.sum(p * d_p, axis=-1, keepdims=True))).astype(BF16)
+                grads[0].append(dot_nn(d_s, k) * head_scale)
+                grads[1].append(dot_tn(d_s, q) * head_scale)
+                grads[2].append(dot_tn(p_low, d_att))
+            d_qkv = jnp.concatenate(grads[0] + grads[1] + grads[2], axis=1).astype(BF16)
+            qkv_all[i] = d_qkv
+            bias[3:4, 0 : 3 * hw] += jnp.sum(d_qkv.astype(F32), axis=0, keepdims=True)
+
+    @step
+    def dam():
+        links.left(gs_mlp.core_copy)
+
+        @pl.loop(0, 4)
+        def _(i):
+            res = dot_nt(qkv_all[i], g_qkv[...])
+            sum_b[i] = res.astype(BF16).reshape(2, half_len, width)
+
+        gs_da.begin()
+
+    @step
+    def wq():
+        for copy in ga_qkv.mine:
+            links.left(copy)
+        outer(
+            lambda at: a_all[:, :, :, at], lambda: qkv_all[...].reshape(all_rows, 3 * hw), g_qkv
+        )
+        sc_qkv.begin()
+
+    @step
+    def xr():
+        links.left(gs_mlp.pair_copy)
+        gs_da.relay()
+
+    @step
+    def wp():
+        for copy in ga_proj.mine:
+            links.left(copy)
+
+        @pl.loop(0, hq)
+        def _(h):
+            value = att_all[h].reshape(all_rows, hd)
+            g_proj[h] = dot_tn(value, da_all[...].reshape(all_rows, width)).astype(BF16)
+
+    for letter, scatter in (("E", sc_fc2), ("F", sc_fc1), ("Q", sc_qkv), ("P", sc_proj)):
+        for k, fn in enumerate(scatter.hops()):
+            steps[letter + str(k)] = fn
+
+    def join(scatter, pack, target, index):
+        at = sems.take(3)
+        keep_copy = pltpu.make_async_copy(pack.at[c], target.at[quarter], local.at[index])
+
+        def begin():
+            def store(keep):
+                total = keep[...].astype(F32)
+                pack[0] = total[:shard].astype(BF16)
+                pack[1] = total[shard:].astype(BF16)
+
+            scatter.finish(store)
+            links.start(True, pack.at[1 - c], target.at[quarter], at, at, sib)
+            links.start(True, pack.at[c], target.at[quarter], at + 1, at + 1, pair)
+            links.start(
+                True, pack.at[1 - c], target.at[quarter], at + 2, at + 2, dev(z, x, 1 - c, 1 - y)
+            )
+            keep_copy.start()
+
+        def finish():
+            keep_copy.wait()
+            links.arrived(True, target.at[2 * y + 1 - c], at, sib)
+            links.arrived(True, target.at[2 * (1 - y) + c], at + 1, sib)
+            links.arrived(True, target.at[2 * (1 - y) + 1 - c], at + 2, sib)
+
+        return begin, finish
+
+    def spread(source, target, count):
+        target[...] = jnp.concatenate(
+            [source[k % 4, :, (k // 4) * hd : (k // 4 + 1) * hd] for k in range(4 * count)],
+            axis=1,
+        )
+
+    steps["EJ"], steps["EG"] = join(sc_fc2, t_fc2, j_fc2, 2)
+    steps["FJ"], fc1_joined = join(sc_fc1, t_fc1, j_fc1, 3)
+    steps["QJ"], qkv_joined = join(sc_qkv, t_qkv, j_qkv, 4)
+
+    @step
+    def FG():
+        fc1_joined()
+        spread(j_fc1, p_fc1, n_wide)
+
+    @step
+    def QG():
+        qkv_joined()
+        spread(j_qkv, p_qkv, 3 * hq)
+
+    steps["PJ"] = lambda: sc_proj.finish(not_column, on_column)
+
+    @step
+    def PK():
+        sc_proj.land(on_column, t_proj)
+        links.start(on_column, t_proj, t_proj, swap_proj, swap_proj, pair)
+
+    @step
+    def PG():
+        links.arrived(not_column, t_proj, swap_proj, sib)
+        j_proj[...] = t_proj[...]
+
+    @step
+    def ln1b():
+        gs_da.arrived()
+        for s in range(2):
+            d_a = gs_da.total(s)
+            normed, inv = norm(tok_ref[s].astype(F32))
+            dmod[1, s : s + 1, :] = jnp.sum(d_a * normed, axis=0, keepdims=True)
+            dmod[0, s : s + 1, :] = jnp.sum(d_a, axis=0, keepdims=True)
+            gtok_ref[s] = dmid_own[s] + norm_grad(d_a * (1.0 + mod(1, s)), normed, inv)
+        links.start(True, dmod, dm_pair, swap_dm, swap_dm, pair)
+
+    @step
+    def t1():
+        links.arrived(True, dm_pair, swap_dm, sib)
+        for k in range(6):
+            dm_low[:, k * width : (k + 1) * width] = (dmod[k] + dm_pair[k]).astype(BF16)
+        dm_all[w] = dm_low[...]
+        ex_dm.begin(lambda p: dm_low, dm_all)
+
+    @step
+    def t2():
+        ex_dm.finish()
+        res = None
+        for k in range(6):
+            at = slice(k * width, (k + 1) * width)
+            for s in range(n_wide):
+                dm_rows[2 * s : 2 * s + 2, :] = dm_all[s, :, at].astype(F32)
+            low = dm_rows[...].astype(BF16)
+            dmall_ref[:, at] = low
+            term = dot_nt(low, wada_ref[:, at])
+            res = term if res is None else res + term
+        ds_send[...] = jnp.zeros_like(ds_send)
+        for s in range(n_wide):
+            ds_send[s, :, 0:shard] = res[2 * s : 2 * s + 2, :]
+        dsil_ref[w] = ds_send[w]
+        ex_ds.begin(lambda p: ds_send.at[p], dsil_ref)
+
+    steps["t3"] = ex_ds.finish
+
+    @step
+    def v1():
+        v_send[...] = jnp.zeros_like(v_send)
+        for s in range(n_wide):
+            at = slice(s * hd, (s + 1) * hd)
+            v_send[s, pl.ds(c, 1), 0:hd] = bias[0:1, at]
+            v_send[s, 2:4, 0:hd] = bias[1:3, at]
+        for j in range(hq):
+            v_send[2 * j + y, pl.ds(4 + c, 1), 0:hd] = bias[3:4, j * hd : (j + 1) * hd]
+            v_send[n_wide // 2 + 2 * j + y, pl.ds(4 + c, 1), 0:hd] = bias[
+                3:4, 2 * hw + j * hd : 2 * hw + (j + 1) * hd
+            ]
+        v_all[w] = v_send[w]
+        ex_v.begin(lambda p: v_send.at[p], v_all)
+
+    @step
+    def v2():
+        ex_v.finish()
+        total = v_all[0]
+        for s in range(1, n_wide):
+            total = total + v_all[s]
+        vout_ref[y] = total
+        links.start(True, vout_ref.at[y], vout_ref.at[y], swap_v, swap_v, pair)
+
+    steps["v3"] = lambda: links.arrived(True, vout_ref.at[1 - y], swap_v, sib)
+    steps["end"] = links.drain
+
+    for name in order:
+        steps[name]()
+
+
+ORDER = (
+    "init0", "px", "q0", "h1", "hb", "p0", "q1", "h2", "h3", "ln1", "q2", "p1", "q3",
+    "init1", "p2", "ar", "f0", "d0", "af", "qkv", "e0", "p3", "att", "f1", "sr", "dr", "e1",
+    "f2", "e2", "ln2", "f3", "e3", "mr", "mf", "df", "fc1", "ef", "fc2", "w2", "ur", "dh",
+    "dm", "w1", "tr", "E0", "res", "ln2b", "F0", "gr", "E1", "E2", "gf", "attb", "F1", "F2",
+    "E3", "dam", "wq", "v1", "F3", "E4", "F4", "xr", "F5", "Q0", "FJ", "wp", "P0", "P1",
+    "P2", "E5", "v2", "EJ", "Q1", "Q2", "P3", "P4", "Q3", "P5", "PJ", "ln1b", "t1", "PK",
+    "Q4", "EG", "Q5", "QJ", "FG", "PG", "v3", "t2", "t3", "QG", "end",
+)
+
+
+def fast_device(
+    tokens,
+    cond,
+    timesteps,
+    counts,
+    w_ada,
+    b_ada,
+    w_qkv,
+    b_qv,
+    w_proj,
+    b_proj,
+    w_fc1,
+    b_fc1,
+    w_fc2,
+    b_fc2,
+    cotangent,
+):
+    slots, half_len, width = tokens.shape
+    n_wide = lax.axis_size("wide")
+    w, y = lax.axis_index("wide"), lax.axis_index("narrow")
+    shard = w_ada.shape[0]
+    mlp = w_fc1.shape[1]
+    hq = HEADS // 4
+    nq = 3 * hq * HEAD_DIM
+    rows = slots * half_len
+    mq = mlp // 4
+    half = w_ada.shape[1] // 2
+
+    cond_vec = cond.astype(F32) + time_features(timesteps, width)
+    cond_sig = jax.nn.sigmoid(cond_vec)
+    silu = (cond_vec * cond_sig).astype(BF16).astype(F32)
+    chunks = jnp.pad(
+        silu.reshape(slots, n_wide, shard).transpose(1, 0, 2), ((0, 0), (0, 0), (0, 640 - shard))
+    )
+
+    def tile(piece):
+        return jnp.pad(piece.astype(F32), ((0, 0), (0, 128 - piece.shape[1])))
+
+    fc1_pieces = lax.dynamic_slice_in_dim(b_fc1.reshape(4, shard), 2 * y, 2, 0)
+    vector = jnp.concatenate(
+        [
+            tile(fc1_pieces),
+            tile(jnp.broadcast_to(b_proj, (2, shard))),
+            tile(jnp.broadcast_to(b_fc2, (2, shard))),
+            tile(b_qv.reshape(2, shard)),
+            jnp.zeros((2, 128), F32),
+        ],
+        axis=1,
+    )
+    vector = jnp.broadcast_to(vector[None], (n_wide // 2, 2, 640)).reshape(n_wide, 1, 640)
+    parcel = jnp.concatenate([chunks, vector, jnp.zeros_like(vector)], axis=1)
+    ada_cut = b_ada.shape[0]
+    ada_bias = lax.dynamic_update_slice_in_dim(
+        jnp.zeros((1, w_ada.shape[1]), F32), b_ada.astype(F32)[None], w * ada_cut, 1
+    )
+    live = (jnp.arange(slots, dtype=jnp.int32) < counts[0])[:, None, None]
+    cot_live = jnp.where(live, cotangent, jnp.zeros_like(cotangent))
+
+    def v16(*shape):
+        return pltpu.VMEM(shape, BF16)
+
+    def v32(*shape):
+        return pltpu.VMEM(shape, F32)
+
+    two = 2 * shard
+    full = (4, 2, half_len, width)
+    own = (slots, half_len, width)
+    scratch = [
+        v16(width, nq), v16(hq, shard, width), v16(width, mq), v16(mq, width), v16(mq, width),
+        v16(shard, nq), v16(shard, mq), v16(shard, width),
+        v16(shard, nq), v16(shard, mq), v16(shard, width), v16(shard, nq), v16(shard, mq),
+        v16(4, two, nq), v16(1, shard, width), v16(4, two, mq), v16(4, two, width),
+        v16(5, two, nq), v16(5, shard, width), v16(5, two, mq), v16(5, two, width),
+        v16(2, shard, nq), v16(2, shard, mq), v16(2, shard, width), v16(shard, width),
+        v16(4, shard, nq), v16(4, shard, mq),
+        v16(*full), v16(*full), v16(*full),
+        v16(4, rows, nq), v16(hq, 4, rows, HEAD_DIM), v16(*full), v16(4, rows, mq),
+        v16(*full), v16(*full),
+        v16(2, 2, half_len, width), v16(2, 2, half_len, width),
+        v16(*own), v16(*own), v16(*own), v16(*own),
+        v32(*own), v32(*own), v32(*own),
+        v32(n_wide * slots, 128), v32(n_wide, slots, half), v32(n_wide, slots, half),
+        v32(slots, half), v32(2, slots, half), v32(6, slots, width), v32(1, nq), v32(4, width),
+        v32(4, width),
+        v32(6, slots, width), v32(6, slots, width), v16(slots, 6 * width),
+        v16(n_wide, slots, 6 * width), v32(n_wide, 8, 128), v32(n_wide, 8, 128),
+        v32(n_wide * slots, width), v32(n_wide, slots, 128),
+        pltpu.SemaphoreType.DMA((300,)),
+        pltpu.SemaphoreType.DMA((300,)),
+        pltpu.SemaphoreType.DMA((5,)),
+    ]
+    out, gtok, got, dm_all, v_out, d_silu, p_qkv, p_fc1, j_fc2, j_proj = pl.pallas_call(
+        functools.partial(block_kernel, ORDER, n_wide),
+        out_shape=(
+            jax.ShapeDtypeStruct(own, BF16),
+            jax.ShapeDtypeStruct(own, F32),
+            jax.ShapeDtypeStruct((n_wide, 4, 640), F32),
+            jax.ShapeDtypeStruct((n_wide * slots, 6 * width), BF16),
+            jax.ShapeDtypeStruct((2, 8, 128), F32),
+            jax.ShapeDtypeStruct((n_wide, slots, 128), F32),
+            jax.ShapeDtypeStruct(w_qkv.shape, BF16),
+            jax.ShapeDtypeStruct(w_fc1.shape, BF16),
+            jax.ShapeDtypeStruct((4, shard, width), BF16),
+            jax.ShapeDtypeStruct((shard, width), BF16),
+        ),
+        in_specs=[VMEM_SPEC] * 7 + [HBM_SPEC] * 2,
+        out_specs=(VMEM_SPEC,) * 8 + (HBM_SPEC, VMEM_SPEC),
+        scratch_shapes=scratch,
+        compiler_params=pltpu.CompilerParams(
+            collective_id=0, has_side_effects=True, vmem_limit_bytes=VMEM_LIMIT
+        ),
+    )(
+        tokens, cot_live, parcel, w_ada, ada_bias, w_qkv, w_fc1,
+        w_fc2.reshape(4, shard, width), w_proj,
+    )
+    out = jnp.where(live, out, jnp.zeros_like(out))
+    silu_cols = got[:, 0:2, :shard].reshape(n_wide * slots, shard).astype(BF16)
+    grad_ada = outer_sum(silu_cols, dm_all)
+    grad_b_ada = jnp.sum(
+        lax.dynamic_slice_in_dim(dm_all, w * ada_cut, ada_cut, 1).astype(F32), axis=0
+    )
+    d_silu = d_silu[:, :, :shard].transpose(1, 0, 2).reshape(slots, width)
+    grad_cond = d_silu * (cond_sig + cond_vec * cond_sig * (1.0 - cond_sig))
+    v_sum = (v_out[0] + v_out[1])[:, :shard]
+    return (
+        out,
+        gtok,
+        grad_cond,
+        grad_ada,
+        grad_b_ada,
+        p_qkv.astype(F32),
+        v_sum[4:6].reshape(-1),
+        j_proj.astype(F32),
+        v_sum[2],
+        p_fc1.astype(F32),
+        v_out[:, 0:2, :shard].reshape(-1),
+        j_fc2.astype(F32).reshape(w_fc2.shape),
+        v_sum[3],
+    )
+
+
 def solution(mesh):
     in_specs = (
         P("wide", "narrow", None),
@@ -333,6 +1455,8 @@
         P("wide", None),
         P("wide"),
     )
+    small = mesh.shape["wide"] == 16 and mesh.shape["narrow"] == 2
+    per_device = fast_device if small else on_device
     return jax.shard_map(
-        on_device, mesh=mesh, in_specs=in_specs, out_specs=out_specs, check_vma=False
-    )
+        per_device, mesh=mesh, in_specs=in_specs, out_specs=out_specs, check_vma=False
+    )

time: 866 us -> 289 us (0.33)
  waiting for transfers between devices: 452 us -> 0 us
  Pallas kernels: 0 us -> 262 us
  blocking collectives: 212 us -> 0 us
  matrix products: 78.1 us -> 1.72 us
  local copies, waits for them, and re-layouts: 60.2 us -> 7.23 us
  between operations: 17.3 us -> 1.44 us
  other arithmetic: 27.5 us -> 15.5 us
  starting transfers between devices: 8.71 us -> 0 us
    pallas_call x0 -> x1, Pallas kernels: none -> 262 us  [fast_device(): pl.pallas_call(functools.partial(block_kernel, ORDER, n_wide), out_shape=...]
    all_gather x7 -> x0, waiting for transfers between devices: 220 us -> none  [the longest x4 185 us: gather_wide(): return lax.all_gather(value, 'wide', axis=axis, tiled=True)]
    reduce_scatter x6 -> x0, waiting for transfers between devices: 191 us -> none  [the longest x3 158 us: scatter_wide(): lax.psum_scatter(part.astype(BF16), 'wide', scatter_dimension=0, tiled=True)]
    unnamed x2 -> x0, blocking collectives: 119 us -> none
    all_gather x6 -> x0, blocking collectives: 74.2 us -> none  [the longest x2 41.7 us: gather_wide(): return lax.all_gather(value, 'wide', axis=axis, tiled=True)]
    dot_general x16 -> x0, matrix products: 52.6 us -> none  [the longest x4 25.4 us: mm(): return jnp.einsum('sk,kn->sn', left, right, preferred_element_type=F32)]
    reshape x20 -> x7, local copies, waits for them, and re-layouts: 32.6 us -> 2.32 us  [the longest x1 0.76 us: fast_device(): fc1_pieces = lax.dynamic_slice_in_dim(b_fc1.reshape(4, shard), 2 * y, 2, 0)]
    unnamed x17 -> x0, waiting for transfers between devices: 30 us -> none
  transfers between devices with their start and end apart: 17 -> 0, of which waited for: 15 -> 0; matrix products, arithmetic and copies ran while one was open for 13% -> 0% of each run, Pallas kernels for 0% -> 0%
where the time goes in v3:
time: 289 us; the launch traced here: 288 us
  Pallas kernels  262 us (91%)
  other arithmetic  15.5 us (5%)
  local copies, waits for them, and re-layouts  7.23 us (3%)
    pallas_call x1, Pallas kernels, fast_device(): pl.pallas_call(functools.partial(block_kernel, ORDER, n_wide), out_shape=...  262 us

profile of v3, /device:TPU:0, one launch (start us, length us, event | category | flops | bytes accessed | tf_op | source)
XLA Modules:
  0.0 288.0 jit_solution(8488435762532969025)
XLA Ops:
  1.3 0.7 convert_element_type.52
  2.0 0.7 convert_element_type.55
  2.7 0.7 pad_convert_fusion.2
  3.4 0.7 pad_convert_fusion.1
  4.0 0.1 pad.48.clone
  4.1 0.8 reshape.73
  4.9 0.7 broadcast_in_dim.44
  5.6 0.2 multiply_cosine_fusion
  5.8 0.8 multiply_convert_fusion
  6.6 0.1 reshape.72
  6.7 0.2 dynamic_update_slice.3.bada_ref
  6.9 0.0 copy-start.6
  6.9 0.1 reshape.74
  7.0 0.8 maximum_maximum_fusion.parcel_ref
  7.8 2.0 broadcast_select_fusion.1.cot_ref
  9.8 0.0 copy-done.6
  9.8 262.1 %shard_map.246 = (bf16[2,128,1152]{2,1,0:T(8,128)(2,1)}, f32[2,128,1152]{2,1,0:T(8,128)}, f32[16,4,640]{2,1,0:T(4,128)}, bf16[32,6912]{1,0:T(8,128)(2,1)}, f32[2...) custom-call(bf16[2,128,1152]{2,1,0:T(8,128)(2,1)} %tok_ref.1, ...), custom_call_target="tpu_custom_call" | custom-call | tf_op jit(solution)/shard_map/pallas_call | solution.py:1375
  271.9 0.0 copy-start.7
  271.9 0.0 copy-start.5
  271.9 0.0 copy-start.4
  271.9 2.1 broadcast_select_fusion
  274.0 0.0 copy-start.2
  274.0 1.5 convert_reduce_fusion
  275.5 0.7 slice.35
  276.2 0.7 add_bitcast_fusion
  276.9 0.7 reshape.78
  277.5 0.5 slice_bitcast_fusion.1
  278.0 0.6 reshape.77
  278.7 0.8 slice.44
  279.4 0.7 slice_bitcast_fusion
  280.2 0.1 reshape.76
  280.3 0.0 copy-done.7
  280.3 0.7 add_multiply_fusion
  281.0 0.0 copy-done.5
  281.0 0.7 convert_element_type.59
  281.7 0.0 copy-done.4
  281.7 1.0 convert_element_type.58
  282.7 0.0 copy-done.2
  282.7 0.0 copy-start.1
  282.7 1.2 convert_element_type.60
  283.9 0.1 copy-done.1
  284.0 0.0 copy-start.3
  284.0 1.2 bitcast_convert_fusion
  285.2 0.0 copy-done.3
  285.2 0.0 copy-start
  285.2 1.7 fusion
  286.9 0.0 copy-done
  286.9 1.0 copy.39
  (14 shorter events, 0.1 us)
Async XLA Ops:
  6.9 2.9 %copy-start.6 = (f32[1,6912]{1,0:T(1,128)}, f32[1,6912]{1,0:T(1,128)S(1)}, u32[]{:S(2)}) copy-start(f32[1,6912]{1,0:T(1,128)S(1)} %dynamic_update_slice.3.bada_ref) | copy-start | bytes 82948
  271.9 8.4 %copy-start.7 = (bf16[2,1152]{1,0:T(2,128)(2,1)S(1)}, bf16[2,1152]{1,0:T(2,128)(2,1)}, u32[]{:S(2)}) copy-start(bf16[2,1152]{1,0:T(2,128)(2,1)} %param.16) | copy-start | bytes 13828
  271.9 9.1 %copy-start.5 = (bf16[72,1152]{1,0:T(8,128)(2,1)S(1)}, bf16[72,1152]{1,0:T(8,128)(2,1)}, u32[]{:S(2)}) copy-start(bf16[72,1152]{1,0:T(8,128)(2,1)} %get-tuple-element.30) | copy-start | bytes 497668
  271.9 9.8 %copy-start.4 = (bf16[72,3456]{1,0:T(8,128)(2,1)S(1)}, bf16[72,3456]{1,0:T(8,128)(2,1)}, u32[]{:S(2)}) copy-start(bf16[72,3456]{1,0:T(8,128)(2,1)} %get-tuple-element.28) | copy-start | bytes 1492996
  274.0 8.8 %copy-start.2 = (bf16[72,4608]{1,0:T(8,128)(2,1)S(1)}, bf16[72,4608]{1,0:T(8,128)(2,1)}, u32[]{:S(2)}) copy-start(bf16[72,4608]{1,0:T(8,128)(2,1)} %get-tuple-element.31) | copy-start | bytes 1990660
  282.7 1.3 copy-start.1
  284.0 1.2 copy-start.3
  285.2 1.7 copy-start

commit v4 on v3

--- a/solution.py
+++ b/solution.py
@@ -1277,7 +1277,7 @@
     "dm", "w1", "tr", "E0", "res", "ln2b", "F0", "gr", "E1", "E2", "gf", "attb", "F1", "F2",
     "E3", "dam", "wq", "v1", "F3", "E4", "F4", "xr", "F5", "Q0", "FJ", "wp", "P0", "P1",
     "P2", "E5", "v2", "EJ", "Q1", "Q2", "P3", "P4", "Q3", "P5", "PJ", "ln1b", "t1", "PK",
-    "Q4", "EG", "Q5", "QJ", "FG", "PG", "v3", "t2", "t3", "QG", "end",
+    "Q4", "FG", "Q5", "QJ", "EG", "PG", "v3", "t2", "t3", "QG", "end",
 )
 
 

time: 289 us -> 289 us (level)
  no operation moved by 1% of the time
where the time goes in v4:
time: 289 us; the launch traced here: 288 us
  Pallas kernels  262 us (91%)
  other arithmetic  15.5 us (5%)
  local copies, waits for them, and re-layouts  7.23 us (3%)
    pallas_call x1, Pallas kernels, fast_device(): pl.pallas_call(functools.partial(block_kernel, ORDER, n_wide), out_shape=...  262 us

profile of v4, /device:TPU:0, one launch (start us, length us, event | category | flops | bytes accessed | tf_op | source)
XLA Modules:
  0.0 288.0 jit_solution(6893569060837777678)
XLA Ops:
  1.3 0.7 convert_element_type.52
  2.0 0.7 convert_element_type.55
  2.7 0.7 pad_convert_fusion.2
  3.4 0.7 pad_convert_fusion.1
  4.0 0.1 pad.48.clone
  4.1 0.8 reshape.73
  4.9 0.7 broadcast_in_dim.44
  5.6 0.2 multiply_cosine_fusion
  5.8 0.8 multiply_convert_fusion
  6.6 0.1 reshape.72
  6.7 0.2 dynamic_update_slice.3.bada_ref
  6.9 0.0 copy-start.6
  6.9 0.1 reshape.74
  7.0 0.8 maximum_maximum_fusion.parcel_ref
  7.8 2.0 broadcast_select_fusion.1.cot_ref
  9.8 0.0 copy-done.6
  9.8 262.1 %shard_map.246 = (bf16[2,128,1152]{2,1,0:T(8,128)(2,1)}, f32[2,128,1152]{2,1,0:T(8,128)}, f32[16,4,640]{2,1,0:T(4,128)}, bf16[32,6912]{1,0:T(8,128)(2,1)}, f32[2...) custom-call(bf16[2,128,1152]{2,1,0:T(8,128)(2,1)} %tok_ref.1, ...), custom_call_target="tpu_custom_call" | custom-call | tf_op jit(solution)/shard_map/pallas_call | solution.py:1375
  271.9 0.0 copy-start.7
  271.9 0.0 copy-start.5
  271.9 0.0 copy-start.4
  271.9 2.1 broadcast_select_fusion
  274.0 0.0 copy-start.2
  274.0 1.5 convert_reduce_fusion
  275.5 0.7 slice.35
  276.2 0.7 add_bitcast_fusion
  276.9 0.7 reshape.78
  277.5 0.5 slice_bitcast_fusion.1
  278.0 0.6 reshape.77
  278.7 0.8 slice.44
  279.4 0.7 slice_bitcast_fusion
  280.2 0.1 reshape.76
  280.3 0.0 copy-done.7
  280.3 0.7 add_multiply_fusion
  281.0 0.0 copy-done.5
  281.0 0.7 convert_element_type.59
  281.7 0.0 copy-done.4
  281.7 1.0 convert_element_type.58
  282.7 0.0 copy-done.2
  282.7 0.0 copy-start.1
  282.7 1.2 convert_element_type.60
  283.9 0.1 copy-done.1
  284.0 0.0 copy-start.3
  284.0 1.2 bitcast_convert_fusion
  285.2 0.0 copy-done.3
  285.2 0.0 copy-start
  285.2 1.7 fusion
  286.9 0.0 copy-done
  286.9 1.0 copy.39
  (14 shorter events, 0.1 us)
Async XLA Ops:
  6.9 2.9 %copy-start.6 = (f32[1,6912]{1,0:T(1,128)}, f32[1,6912]{1,0:T(1,128)S(1)}, u32[]{:S(2)}) copy-start(f32[1,6912]{1,0:T(1,128)S(1)} %dynamic_update_slice.3.bada_ref) | copy-start | bytes 82948
  271.9 8.4 %copy-start.7 = (bf16[2,1152]{1,0:T(2,128)(2,1)S(1)}, bf16[2,1152]{1,0:T(2,128)(2,1)}, u32[]{:S(2)}) copy-start(bf16[2,1152]{1,0:T(2,128)(2,1)} %param.16) | copy-start | bytes 13828
  271.9 9.1 %copy-start.5 = (bf16[72,1152]{1,0:T(8,128)(2,1)S(1)}, bf16[72,1152]{1,0:T(8,128)(2,1)}, u32[]{:S(2)}) copy-start(bf16[72,1152]{1,0:T(8,128)(2,1)} %get-tuple-element.30) | copy-start | bytes 497668
  271.9 9.8 %copy-start.4 = (bf16[72,3456]{1,0:T(8,128)(2,1)S(1)}, bf16[72,3456]{1,0:T(8,128)(2,1)}, u32[]{:S(2)}) copy-start(bf16[72,3456]{1,0:T(8,128)(2,1)} %get-tuple-element.28) | copy-start | bytes 1492996
  274.0 8.8 %copy-start.2 = (bf16[72,4608]{1,0:T(8,128)(2,1)S(1)}, bf16[72,4608]{1,0:T(8,128)(2,1)}, u32[]{:S(2)}) copy-start(bf16[72,4608]{1,0:T(8,128)(2,1)} %get-tuple-element.31) | copy-start | bytes 1990660
  282.7 1.3 copy-start.1
  284.0 1.2 copy-start.3
  285.2 1.7 copy-start

commit v5 on v4

--- a/solution.py
+++ b/solution.py
@@ -495,7 +495,10 @@
 
     def begin(self):
         z, x, c, y = self.pos["z"], self.pos["x"], self.pos["c"], self.pos["y"]
-        for s in (3, 0, 2, 1):
+        far = jnp.where(z < 2, 3, 0)
+        middle = jnp.where(z == 0, 2, jnp.where(z == 3, 1, 3 - far))
+        near = jnp.where(z % 2 == 0, 1, 2)
+        for s in (far, middle, near, z):
             self.links.start(
                 self.source, self.block(s, 1 - x), self.sums_x.at[s], self.x_at + s,
                 self.x_at + s, self.pos["dev"](z, 1 - x, c, y),
@@ -505,27 +508,25 @@
         self.links.arrived(True, self.sums_x.at[s], self.x_at + s, self.pos["me"])
         return self.block(s, self.pos["x"])[...].astype(F32) + self.sums_x[s].astype(F32)
 
-    def hop(self, s, up):
+    def hop(self, here, s, up):
         z, x, c, y = self.pos["z"], self.pos["x"], self.pos["c"], self.pos["y"]
-        cond = both(self.sink, (z < s) if up else (z > s))
+        first = here == (0 if up else NZ - 1)
+        ref = self.block(s, x)
 
         def run():
-            ref = self.block(s, x)
-            ref[...] = self.add_x(s).astype(BF16)
-            inner = (z > 0) if up else (z < NZ - 1)
-
-            @pl.when(inner)
-            def _():
+            total = self.add_x(s)
+            if not first:
                 self.links.arrived(True, self.sums_z.at[s], self.z_at + s, self.pos["me"])
-                ref[...] = (ref[...].astype(F32) + self.sums_z[s].astype(F32)).astype(BF16)
-
+                total = total + self.sums_z[s].astype(F32)
+            ref[...] = total.astype(BF16)
+
+        cond = z == here
         do_when(cond, run)
-        near = (z == s - 1) if up else (z == s + 1)
-        slot = s if up else jnp.where(near, 4, s)
-        to = self.pos["dev"](z + 1 if up else z - 1, x, c, y)
+        to = here + 1 if up else here - 1
+        slot = 4 if s == to and not up else s
         at = (self.up_at if up else self.down_at) + s
         self.links.start(
-            cond, self.block(s, x), self.sums_z.at[slot], at, self.z_at + slot, to
+            cond, ref, self.sums_z.at[slot], at, self.z_at + slot, self.pos["dev"](to, x, c, y)
         )
 
     def finish(self, store):
@@ -553,10 +554,15 @@
         do_when(self.sink, run)
 
     def hops(self):
-        out = []
-        for k in range(3):
-            out.append(lambda k=k: self.hop(3 - k, True))
-            out.append(lambda k=k: self.hop(k, False))
+        out = {}
+        for here in range(NZ - 1):
+            for s in range(here + 1, NZ):
+
+                def both_ways(here=here, s=s):
+                    self.hop(here, s, True)
+                    self.hop(NZ - 1 - here, NZ - 1 - s, False)
+
+                out[str(s) + str(here)] = both_ways
         return out
 
 
@@ -753,7 +759,7 @@
     gs_attn = GroupSum(links, pos, sum_a, core_a, to_a, from_a)
     gs_mlp = GroupSum(links, pos, sum_b, core_b, to_b, from_b)
     gs_dm = GroupSum(links, pos, sum_a, core_a, to_a, from_a)
-    gs_da = GroupSum(links, pos, sum_b, core_b, to_b, from_b)
+    gs_da = GroupSum(links, pos, sum_a, core_a, to_a, from_a)
     sc_fc2 = Scatter(links, pos, rows_of(w_fc2), x_fc2, z_fc2, True, True)
     sc_fc1 = Scatter(links, pos, rows_of(g_fc2), x_fc1, z_fc1, True, True)
     sc_qkv = Scatter(links, pos, rows_of(g_qkv), x_qkv, z_qkv, True, True)
@@ -1105,12 +1111,12 @@
 
     @step
     def dam():
-        links.left(gs_mlp.core_copy)
+        links.left(gs_dm.core_copy)
 
         @pl.loop(0, 4)
         def _(i):
             res = dot_nt(qkv_all[i], g_qkv[...])
-            sum_b[i] = res.astype(BF16).reshape(2, half_len, width)
+            sum_a[i] = res.astype(BF16).reshape(2, half_len, width)
 
         gs_da.begin()
 
@@ -1125,7 +1131,7 @@
 
     @step
     def xr():
-        links.left(gs_mlp.pair_copy)
+        links.left(gs_dm.pair_copy)
         gs_da.relay()
 
     @step
@@ -1139,8 +1145,8 @@
             g_proj[h] = dot_tn(value, da_all[...].reshape(all_rows, width)).astype(BF16)
 
     for letter, scatter in (("E", sc_fc2), ("F", sc_fc1), ("Q", sc_qkv), ("P", sc_proj)):
-        for k, fn in enumerate(scatter.hops()):
-            steps[letter + str(k)] = fn
+        for name, fn in scatter.hops().items():
+            steps[letter + name] = fn
 
     def join(scatter, pack, target, index):
         at = sems.take(3)
@@ -1271,13 +1277,13 @@
 
 
 ORDER = (
-    "init0", "px", "q0", "h1", "hb", "p0", "q1", "h2", "h3", "ln1", "q2", "p1", "q3",
-    "init1", "p2", "ar", "f0", "d0", "af", "qkv", "e0", "p3", "att", "f1", "sr", "dr", "e1",
-    "f2", "e2", "ln2", "f3", "e3", "mr", "mf", "df", "fc1", "ef", "fc2", "w2", "ur", "dh",
-    "dm", "w1", "tr", "E0", "res", "ln2b", "F0", "gr", "E1", "E2", "gf", "attb", "F1", "F2",
-    "E3", "dam", "wq", "v1", "F3", "E4", "F4", "xr", "F5", "Q0", "FJ", "wp", "P0", "P1",
-    "P2", "E5", "v2", "EJ", "Q1", "Q2", "P3", "P4", "Q3", "P5", "PJ", "ln1b", "t1", "PK",
-    "Q4", "FG", "Q5", "QJ", "EG", "PG", "v3", "t2", "t3", "QG", "end",
+    "init0", "px", "q0", "h1", "q1", "p0", "init1", "h2", "h3", "ln1", "hb", "q2", "q3",
+    "p1", "p2", "e0", "ar", "d0", "f0", "af", "qkv", "p3", "att", "f1", "sr", "dr", "f2",
+    "e1", "ln2", "f3", "e2", "e3", "mr", "mf", "fc1", "df", "w2", "ef", "dh", "fc2", "dm",
+    "E30", "tr", "w1", "E20", "E21", "E10", "ln2b", "ur", "F30", "E31", "gr", "F31", "F20",
+    "gf", "attb", "F10", "wp", "E32", "P30", "dam", "P20", "F21", "wq", "xr", "EJ", "P31",
+    "res", "P21", "F32", "P32", "v1", "Q30", "Q20", "P10", "Q31", "Q10", "ln1b", "Q21", "FJ",
+    "Q32", "t1", "QJ", "FG", "v2", "PJ", "PK", "v3", "EG", "QG", "t2", "t3", "PG", "end",
 )
 
 

time: 289 us -> 254 us (0.88)
  Pallas kernels: 262 us -> 227 us
    pallas_call x1, Pallas kernels: 262 us -> 227 us  [fast_device(): pl.pallas_call(functools.partial(block_kernel, ORDER, n_wide), out_shape=...]
where the time goes in v5:
time: 254 us; the launch traced here: 253 us
  Pallas kernels  227 us (89%)
  other arithmetic  15.5 us (6%)
  local copies, waits for them, and re-layouts  7.23 us (3%)
    pallas_call x1, Pallas kernels, fast_device(): pl.pallas_call(functools.partial(block_kernel, ORDER, n_wide), out_shape=...  227 us

profile of v5, /device:TPU:0, one launch (start us, length us, event | category | flops | bytes accessed | tf_op | source)
XLA Modules:
  0.0 253.3 jit_solution(12118762717543946506)
XLA Ops:
  1.3 0.7 convert_element_type.52
  2.0 0.7 convert_element_type.55
  2.7 0.7 pad_convert_fusion.2
  3.4 0.7 pad_convert_fusion.1
  4.0 0.1 pad.48.clone
  4.1 0.8 reshape.73
  4.9 0.7 broadcast_in_dim.44
  5.6 0.2 multiply_cosine_fusion
  5.8 0.8 multiply_convert_fusion
  6.6 0.1 reshape.72
  6.7 0.2 dynamic_update_slice.3.bada_ref
  6.9 0.0 copy-start.6
  6.9 0.1 reshape.74
  7.0 0.8 maximum_maximum_fusion.parcel_ref
  7.8 2.0 broadcast_select_fusion.1.cot_ref
  9.8 0.0 copy-done.6
  9.8 227.4 %shard_map.246 = (bf16[2,128,1152]{2,1,0:T(8,128)(2,1)}, f32[2,128,1152]{2,1,0:T(8,128)}, f32[16,4,640]{2,1,0:T(4,128)}, bf16[32,6912]{1,0:T(8,128)(2,1)}, f32[2...) custom-call(bf16[2,128,1152]{2,1,0:T(8,128)(2,1)} %tok_ref.1, ...), custom_call_target="tpu_custom_call" | custom-call | tf_op jit(solution)/shard_map/pallas_call | solution.py:1381
  237.1 0.0 copy-start.7
  237.2 0.0 copy-start.5
  237.2 0.0 copy-start.4
  237.2 2.1 broadcast_select_fusion
  239.2 0.0 copy-start.2
  239.2 1.5 convert_reduce_fusion
  240.8 0.7 slice.35
  241.5 0.7 add_bitcast_fusion
  242.1 0.7 reshape.78
  242.8 0.5 slice_bitcast_fusion.1
  243.3 0.6 reshape.77
  244.0 0.8 slice.44
  244.7 0.7 slice_bitcast_fusion
  245.5 0.1 reshape.76
  245.6 0.0 copy-done.7
  245.6 0.7 add_multiply_fusion
  246.3 0.0 copy-done.5
  246.3 0.7 convert_element_type.59
  247.0 0.0 copy-done.4
  247.0 1.0 convert_element_type.58
  248.0 0.0 copy-done.2
  248.0 0.0 copy-start.1
  248.0 1.2 convert_element_type.60
  249.2 0.1 copy-done.1
  249.3 0.0 copy-start.3
  249.3 1.2 bitcast_convert_fusion
  250.5 0.0 copy-done.3
  250.5 0.0 copy-start
  250.5 1.7 fusion
  252.2 0.0 copy-done
  252.2 1.0 copy.39
  (14 shorter events, 0.1 us)
Async XLA Ops:
  6.9 2.9 %copy-start.6 = (f32[1,6912]{1,0:T(1,128)}, f32[1,6912]{1,0:T(1,128)S(1)}, u32[]{:S(2)}) copy-start(f32[1,6912]{1,0:T(1,128)S(1)} %dynamic_update_slice.3.bada_ref) | copy-start | bytes 82948
  237.1 8.4 %copy-start.7 = (bf16[2,1152]{1,0:T(2,128)(2,1)S(1)}, bf16[2,1152]{1,0:T(2,128)(2,1)}, u32[]{:S(2)}) copy-start(bf16[2,1152]{1,0:T(2,128)(2,1)} %param.16) | copy-start | bytes 13828
  237.2 9.1 %copy-start.5 = (bf16[72,1152]{1,0:T(8,128)(2,1)S(1)}, bf16[72,1152]{1,0:T(8,128)(2,1)}, u32[]{:S(2)}) copy-start(bf16[72,1152]{1,0:T(8,128)(2,1)} %get-tuple-element.30) | copy-start | bytes 497668
  237.2 9.8 %copy-start.4 = (bf16[72,3456]{1,0:T(8,128)(2,1)S(1)}, bf16[72,3456]{1,0:T(8,128)(2,1)}, u32[]{:S(2)}) copy-start(bf16[72,3456]{1,0:T(8,128)(2,1)} %get-tuple-element.28) | copy-start | bytes 1492996
  239.2 8.8 %copy-start.2 = (bf16[72,4608]{1,0:T(8,128)(2,1)S(1)}, bf16[72,4608]{1,0:T(8,128)(2,1)}, u32[]{:S(2)}) copy-start(bf16[72,4608]{1,0:T(8,128)(2,1)} %get-tuple-element.31) | copy-start | bytes 1990660
  248.0 1.3 copy-start.1
  249.3 1.2 copy-start.3
  250.5 1.7 copy-start

commit v6 on v5

--- a/solution.py
+++ b/solution.py
@@ -1274,6 +1274,15 @@
 
     for name in order:
         steps[name]()
+
+
+def finish_kernel(*refs):
+    count = (len(refs) - 3) // 2
+    for source, target in zip(refs[:count], refs[count + 2 : 2 * count + 2]):
+        target[...] = source[...].astype(target.dtype).reshape(target.shape)
+    left, right, product = refs[count], refs[count + 1], refs[-1]
+    shard = product.shape[0]
+    product[...] = dot_tn(left[...][:, :shard], right[...])
 
 
 ORDER = (
@@ -1404,7 +1413,26 @@
     )
     out = jnp.where(live, out, jnp.zeros_like(out))
     silu_cols = got[:, 0:2, :shard].reshape(n_wide * slots, shard).astype(BF16)
-    grad_ada = outer_sum(silu_cols, dm_all)
+    passed = (gtok, p_qkv, j_proj, p_fc1, j_fc2.reshape(w_fc2.shape))
+    parts = 3
+
+    def cut(value):
+        dims = value.shape[:-1]
+        return pl.BlockSpec(
+            (*dims, value.shape[-1] // parts), lambda i: (0,) * len(dims) + (i,)
+        )
+
+    given = [jax.ShapeDtypeStruct(value.shape, F32) for value in passed]
+    product = jax.ShapeDtypeStruct(w_ada.shape, F32)
+    gtok, grad_qkv, grad_proj, grad_fc1, grad_fc2, grad_ada = pl.pallas_call(
+        finish_kernel,
+        grid=(parts,),
+        out_shape=given + [product],
+        in_specs=[cut(value) for value in passed]
+        + [pl.BlockSpec(silu_cols.shape, lambda i: (0, 0)), cut(dm_all)],
+        out_specs=[cut(value) for value in given] + [cut(product)],
+        compiler_params=pltpu.CompilerParams(vmem_limit_bytes=VMEM_LIMIT),
+    )(*passed, silu_cols, dm_all)
     grad_b_ada = jnp.sum(
         lax.dynamic_slice_in_dim(dm_all, w * ada_cut, ada_cut, 1).astype(F32), axis=0
     )
@@ -1417,13 +1445,13 @@
         grad_cond,
         grad_ada,
         grad_b_ada,
-        p_qkv.astype(F32),
+        grad_qkv,
         v_sum[4:6].reshape(-1),
-        j_proj.astype(F32),
+        grad_proj,
         v_sum[2],
-        p_fc1.astype(F32),
+        grad_fc1,
         v_out[:, 0:2, :shard].reshape(-1),
-        j_fc2.astype(F32).reshape(w_fc2.shape),
+        grad_fc2,
         v_sum[3],
     )
 

time: 254 us -> 253 us (level)
  Pallas kernels: 227 us -> 233 us
  other arithmetic: 15.5 us -> 11.2 us
    pallas_call x0 -> x1, Pallas kernels: none -> 5.71 us  [fast_device(): pl.pallas_call(finish_kernel, grid=(parts,), out_shape=given + [product],...]
    convert_element_type x3 -> x0, other arithmetic: 2.93 us -> none  [the longest x1 1.17 us: fast_device(): p_fc1.astype(F32)]
where the time goes in v6:
time: 253 us
  Pallas kernels  233 us (92%)
  other arithmetic  11.2 us (4%)
  local copies, waits for them, and re-layouts  6.68 us (3%)
    pallas_call x1, Pallas kernels, fast_device(): pl.pallas_call(functools.partial(block_kernel, ORDER, n_wide), out_shape=...  227 us
    pallas_call x1, Pallas kernels, fast_device(): pl.pallas_call(finish_kernel, grid=(parts,), out_shape=given + [product],...  5.71 us

profile of v6, /device:TPU:0, one launch (start us, length us, event | category | flops | bytes accessed | tf_op | source)
XLA Modules:
  0.0 252.6 jit_solution(17538725901654672193)
XLA Ops:
  1.3 0.7 convert_element_type.41
  2.0 0.7 convert_element_type.44
  2.7 0.7 pad_convert_fusion.2
  3.4 0.7 pad_convert_fusion.1
  4.0 0.1 pad.48.clone
  4.1 0.8 reshape.70
  4.9 0.7 broadcast_in_dim.44
  5.6 0.2 multiply_cosine_fusion
  5.8 0.8 multiply_convert_fusion
  6.6 0.1 reshape.69
  6.7 0.2 dynamic_update_slice.3.bada_ref
  6.9 0.0 copy-start
  6.9 0.1 reshape.71
  7.0 0.8 maximum_maximum_fusion.parcel_ref
  7.8 2.0 broadcast_select_fusion.1.cot_ref
  9.8 0.0 copy-done
  9.8 227.3 %shard_map.246 = (bf16[2,128,1152]{2,1,0:T(8,128)(2,1)}, f32[2,128,1152]{2,1,0:T(8,128)}, f32[16,4,640]{2,1,0:T(4,128)}, bf16[32,6912]{1,0:T(8,128)(2,1)}, f32[2...) custom-call(bf16[2,128,1152]{2,1,0:T(8,128)(2,1)} %tok_ref.1, ...), custom_call_target="tpu_custom_call" | custom-call | tf_op jit(solution)/shard_map/pallas_call | solution.py:1390
  237.1 0.0 copy-start.1
  237.1 2.0 broadcast_select_fusion
  239.1 1.4 convert_reduce_fusion
  240.6 0.7 slice.35
  241.3 0.7 add_bitcast_fusion
  241.9 0.7 reshape.76
  242.6 0.5 slice_bitcast_fusion.1
  243.1 0.6 reshape.75
  243.8 1.4 slice.44
  245.1 0.7 slice_bitcast_fusion
  245.8 0.1 reshape.74
  245.9 0.0 copy-done.1
  245.9 0.7 add_multiply_fusion
  246.6 5.7 %shard_map.247 = (f32[2,128,1152]{2,1,0:T(8,128)}, f32[72,3456]{1,0:T(8,128)}, f32[72,1152]{1,0:T(8,128)}, f32[72,4608]{1,0:T(8,128)}, f32[288,1152]{1,0:T(8,128)}, /*index=5*/f32[72,6912]{1,0:T(8,128)}) custom-call(f32[2,128,1152]{2,1,0:T(8,128)} %get-tuple-element.30.refs_0_, bf16[72,3456]{1,0:T(8,128)(2,1)} %get-tuple-element.31.refs_1_, ...), custom_call_target="tpu_custom_call" | custom-call | tf_op jit(solution)/shard_map/pallas_call | solution.py:1427
  (14 shorter events, 0.1 us)
Async XLA Ops:
  6.9 2.9 %copy-start = (f32[1,6912]{1,0:T(1,128)}, f32[1,6912]{1,0:T(1,128)S(1)}, u32[]{:S(2)}) copy-start(f32[1,6912]{1,0:T(1,128)S(1)} %dynamic_update_slice.3.bada_ref) | copy-start | bytes 82948
  237.1 8.9 %copy-start.1 = (bf16[2,1152]{1,0:T(2,128)(2,1)S(1)}, bf16[2,1152]{1,0:T(2,128)(2,1)}, u32[]{:S(2)}) copy-start(bf16[2,1152]{1,0:T(2,128)(2,1)} %param.16) | copy-start | bytes 13828
